TPU v7x, 32 devices: a whole 2x2x4 slice. The times are simulated.
32 devices in a mesh: groups: 2 (over y), tm: 4 (over z), cuts: 2 (over x), col: 2 (over core).
Axes of the slice: x: 2, y: 2, z: 4, core: 2. Of those that a mesh axis runs over, the one named last changes fastest.
Arguments:
- turns: bfloat16 [4096, 4, 1280], P(('groups', 'tm'), 'cuts', 'col'), parts along dimension 0, may hold values from -25 to 25
- shifts: int32 [8], P(('groups', 'tm')), parts along dimension 0, may hold values from -16 to 16
- bands: int32 [8], P(('groups', 'cuts')), parts along dimension 0, may hold values from 2 to 24
- memory: float32 [8], P(('groups', 'cuts')), parts along dimension 0, may hold values from 0.8 to 0.995
Outputs:
- filtered: bfloat16 [8192, 4, 1280], P(('groups', 'tm', 'col'), 'cuts'), parts along dimension 0
There are 2 independent parts, one for each index of `groups`. A program takes and returns all parts, laid end to end along the dimension named above; each array names one. Nothing has to cross between parts.
All inputs are finite; a program needn't handle non-finite values.
Results may differ from a plain program's by a relative error of at most 0.015.
The roundings to bfloat16 on the way count: a program that leaves them out, or rounds other values in their place, can miss the bound.
Values may be sent and summed in bfloat16 or wider, within the bound.
No kernel may reach another device: no remote copies, remote signals or barrier semaphores. Data moves between devices by JAX's collectives and lax.ppermute only.
A program may use at most 64 MiB of HBM per device.

v0:
```python
import functools
import math

import jax
import jax.numpy as jnp
import numpy as np
from jax import lax
from jax.experimental import pallas as pl
from jax.experimental.pallas import tpu as pltpu
from jax.sharding import PartitionSpec as P

BAND_FREQS = 64
WAVES = 2 * BAND_FREQS
TAP_ROWS = 256
PIECES = ((0, 256), (256, 512), (512, 640))

VMEM = pl.BlockSpec(memory_space=pltpu.VMEM)
SMEM = pl.BlockSpec(memory_space=pltpu.SMEM)
F32 = jnp.float32
BF16 = jnp.bfloat16


def wave_tables(half, rows):
    k = np.arange(BAND_FREQS)[:, None] + 1
    m = (k * np.arange(half)[None, :]) % (2 * half)
    phase = m.astype(np.float64) * (2.0 * math.pi / (2 * half))
    waves = np.concatenate([np.cos(phase), np.sin(phase)], axis=0).astype(np.float32)
    eye = np.eye(rows, dtype=np.float32)
    spread = (waves[:, None, :, None] * eye[None, :, None, :]).reshape(WAVES * rows, half * rows)
    return spread.astype(jnp.bfloat16), np.ascontiguousarray(spread.T).astype(jnp.bfloat16)


def params(flops, size, grant=8 << 20):
    return dict(
        compiler_params=pltpu.CompilerParams(vmem_limit_bytes=grant),
        cost_estimate=pl.CostEstimate(flops=flops, bytes_accessed=size, transcendentals=0),
    )


def pattern(shape, dim, rows):
    return lax.broadcasted_iota(jnp.int32, shape, dim) % rows


def split_kernel(raw, *outs):
    *pieces, sums = outs
    half, rows, cols = raw.shape
    block = 128
    total = None
    for start in range(0, half, block):
        x = raw[start : start + block].reshape(block * rows, cols)
        shape = (8, block * rows)
        pick = pattern(shape, 1, rows) == lax.broadcasted_iota(jnp.int32, shape, 0)
        part = jnp.dot(pick.astype(F32).astype(BF16), x, preferred_element_type=F32)
        total = part if total is None else total + part
        for (lo, hi), out in zip(PIECES, pieces):
            out[start * rows : (start + block) * rows, :] = x[:, lo:hi]
    sums[...] = total[:rows, :]


def spec_kernel(rows, angles, table, bands, *refs):
    *pieces, spec, gain = refs
    waves = spec.shape[0]
    index = lax.broadcasted_iota(jnp.int32, (waves, 1), 0)
    k = index // rows % BAND_FREQS + 1
    flip = jnp.where(k % 2 == 0, 1.0, -1.0)
    for (lo, hi), piece in zip(PIECES, pieces):
        spec[:, lo:hi] = flip * jnp.dot(table[...], piece[...], preferred_element_type=F32)
    band = bands[:, :1]
    for s in range(1, rows):
        band = jnp.where(index % rows == s, bands[:, s : s + 1], band)
    square = (k * k).astype(F32)
    gain[...] = jnp.exp(-square / (2.0 * band * band)) * (2.0 / angles)


def smooth_kernel(estimate, before, after, left, right):
    cols = left.shape[1]
    x = estimate[...]
    place = lax.axis_index("cuts")
    first = jnp.where(place != 0, before[...], 0.0)
    last = jnp.where(place != lax.axis_size("cuts") - 1, after[...], 0.0)
    up = jnp.concatenate([first, x[:-1]], axis=0)
    down = jnp.concatenate([x[1:], last], axis=0)
    ring = (up + 2.0 * x + down) * 0.25
    left[...] = ring[:, :cols]
    right[...] = ring[:, cols:]


def damp_kernel(lo, rows, raw, piece, own, spec, gain, table, turned, left, right, *outs):
    keep, send, old = outs
    count, cols = piece.shape
    waves = turned.shape[1]
    core = lax.axis_index("col")

    @pl.when(core == 0)
    def _():
        old[...] = raw[:, :, lo : lo + cols].reshape(count, cols)

    @pl.when(core != 0)
    def _():
        old[...] = piece[...]

    total = jnp.dot(table[...], old[...], preferred_element_type=F32)
    total = (total + spec[:, lo : lo + cols]) * gain[...]
    index = lax.broadcasted_iota(jnp.int32, (waves, 1), 0)
    k = index // rows % BAND_FREQS + 1
    flip = jnp.where(k % 2 == 0, 1.0, -1.0)
    row = pattern((8, cols), 0, rows)
    ring = None
    for s in range(rows):
        line = jnp.where(
            core == 0, left[s : s + 1, lo : lo + cols], right[s : s + 1, lo : lo + cols]
        )
        line = jnp.broadcast_to(line, (8, cols))
        ring = line if s == 0 else jnp.where(row == s, line, ring)

    def damp(half, source, target):
        scaled = (total if half == 0 else total * flip).astype(BF16)
        for r in range(0, count, 256):
            low = jnp.dot(turned[r : r + 256, :], scaled, preferred_element_type=F32)
            rest = source[r : r + 256, :].astype(F32) - low
            rest = rest.reshape(32, 8, cols) - ring[None]
            target[r : r + 256, :] = rest.reshape(256, cols).astype(BF16)

    @pl.when(core == 0)
    def _():
        damp(1, own, send)
        damp(0, old, keep)

    @pl.when(core != 0)
    def _():
        damp(0, old, send)
        damp(1, own, keep)


def filter_kernel(starts, first, last, rows, *refs):
    n = len(starts)
    taps = refs[n]
    acc = None if first else refs[n + 1]
    out = refs[-1]
    width = out.shape[-1]
    step = 256
    count = refs[0].shape[0]

    def block(r):
        total = None if first else acc[r, :]
        for start, ref in zip(starts, refs):
            off = (-start) % width
            weights = taps[: ref.shape[1], off : off + width]
            part = jnp.dot(ref[r, :], weights, preferred_element_type=F32)
            total = part if total is None else total + part
        return total

    if last:
        r = pl.ds(pl.multiple_of(pl.program_id(0) * step, step), step)
        out[...] = block(r).astype(BF16).reshape(step // rows, rows, width)
    else:
        for b in range(0, count, step):
            out[b : b + step, :] = block(slice(b, b + step))


def tap_kernel(shift, out):
    width = out.shape[1] // 2
    lanes = 128
    for r in range(0, lanes, 16):
        row = lax.broadcasted_iota(jnp.int32, (16, width), 0) + r
        col = lax.broadcasted_iota(jnp.int32, (16, width), 1)
        lag = col - row - shift[0]
        lag = jnp.where(lag < 0, lag + width, lag)
        lag = jnp.where(lag < 0, lag + width, lag)
        near = jnp.minimum(lag, width - lag)
        size = jnp.maximum(near, 1).astype(F32)
        odd = -1.0 / (math.pi**2 * size**2)
        tap = jnp.where(near == 0, 0.25, jnp.where((near & 1) == 1, odd, 0.0)).astype(BF16)
        for b in range(out.shape[0] // lanes):
            for c in range(0, 2 * width, width):
                start = (c + b * lanes) % (2 * width)
                rows = slice(b * lanes + r, b * lanes + r + 16)
                room = min(width, 2 * width - start)
                out[rows, start : start + room] = tap[:, :room]
                if room < width:
                    out[rows, : width - room] = tap[:, room:]


def along_tm(x, core, distance):
    tm, cores = lax.axis_size("tm"), lax.axis_size("col")
    route = [(cores * i + core, cores * (i + distance) + core) for i in range(tm - distance)]
    return lax.ppermute(x, ("tm", "col"), route)


def tiny(body, shapes, *args):
    def kernel(*refs):
        for ref, value in zip(refs[len(args) :], body(*(r[...] for r in refs[: len(args)]))):
            ref[...] = value

    return pl.pallas_call(
        kernel,
        out_shape=tuple(jax.ShapeDtypeStruct(s, F32) for s in shapes),
        in_specs=[VMEM] * len(args),
        out_specs=(VMEM,) * len(shapes),
        **params(1 << 16, 1 << 16),
    )(*args)


def row_edges(x):
    place = lax.axis_index("cuts")
    if lax.axis_size("cuts") == 2:
        return (jnp.where(place == 0, x[-1:], x[:1]),) * 2
    return x[-1:], x[:1]


def row_neighbours(last, first):
    cuts, cores = lax.axis_size("cuts"), lax.axis_size("col")
    at = [cores * i + cores - 1 for i in range(cuts)]
    if cuts == 1:
        return first, last
    if cuts == 2:
        got = lax.ppermute(last, ("cuts", "col"), [(at[0], at[1]), (at[1], at[0])])
        return got, got
    up = list(zip(at[:-1], at[1:]))
    before = lax.ppermute(last, ("cuts", "col"), up)
    after = lax.ppermute(first, ("cuts", "col"), [(j, i) for i, j in up])
    return before, after


def cycle_of(sums, memory, angles):
    rows, cols = sums.shape
    tm, cores = lax.axis_size("tm"), lax.axis_size("col")
    wide = (rows, cores * cols)
    decay = memory.reshape(rows, 1)
    steps = lax.axis_index("tm") - jnp.arange(tm, dtype=jnp.int32)
    powers = jnp.power(memory[None, :], jnp.maximum(steps, 0).astype(F32)[:, None])
    weight = jnp.sum(jnp.where(steps[:, None] >= 0, powers, 0.0), axis=0)[:, None]
    distances = [1 << i for i in range(max(tm - 1, 1).bit_length())]
    scales = [decay ** (d - 1) for d in distances] + [decay**d for d in distances]
    scales = jnp.concatenate(scales + [decay, weight * angles], axis=1)
    n = len(distances)
    left = lax.ppermute(sums, "col", [(0, 1)])
    (whole,) = tiny(lambda a, b: (jnp.concatenate([a, b], axis=1),), [wide], left, sums)
    older, window = None, whole
    for i, d in enumerate(distances):
        got = along_tm(window, 1, d)
        if i == n - 1:
            break

        def extend(c, got, window, older=None, i=i):
            further = got if older is None else older + c[:, i : i + 1] * got
            return further, window + c[:, n + i : n + i + 1] * got

        extra = () if older is None else (older,)
        older, window = tiny(extend, [wide] * 2, scales, got, window, *extra)

    def estimate_of(c, got, whole, older=None):
        total = got if older is None else older + c[:, n - 1 : n] * got
        x = (whole + c[:, 2 * n : 2 * n + 1] * total + total) / c[:, 2 * n + 1 :]
        return x, *row_edges(x)

    extra = () if older is None else (older,)
    edge = (1, wide[1])
    estimate, last, first = tiny(estimate_of, [wide, edge, edge], scales, got, whole, *extra)
    before, after = row_neighbours(last, first)
    shape = jax.ShapeDtypeStruct((rows, cols), F32)
    left, right = pl.pallas_call(
        smooth_kernel,
        out_shape=(shape, shape),
        in_specs=[VMEM] * 3,
        out_specs=[VMEM] * 2,
        name="smooth",
        **params(1 << 16, 1 << 16),
    )(estimate, before, after)
    left = lax.ppermute(left, "col", [(1, 0)])
    return left, right


def local(turns, shifts, bands, memory):
    half, rows, cols = turns.shape
    angles, count = 2 * half, half * rows
    width = lax.axis_size("col") * cols
    waves = WAVES * rows
    table, turned = (jnp.asarray(t) for t in wave_tables(half, rows))
    core = lax.axis_index("col").astype(jnp.int32)

    raw = along_tm(turns, 0, 1)
    shapes = [jax.ShapeDtypeStruct((count, hi - lo), BF16) for lo, hi in PIECES]
    *pieces, sums = pl.pallas_call(
        split_kernel,
        out_shape=(*shapes, jax.ShapeDtypeStruct((rows, cols), F32)),
        in_specs=[VMEM],
        out_specs=[VMEM] * (len(PIECES) + 1),
        name="split",
        **params(16 * count * cols, 4 * count * cols),
    )(turns)
    left, right = cycle_of(sums, memory, angles)
    spec, gain = pl.pallas_call(
        functools.partial(spec_kernel, rows, angles),
        out_shape=(
            jax.ShapeDtypeStruct((waves, cols), F32),
            jax.ShapeDtypeStruct((waves, 1), F32),
        ),
        in_specs=[VMEM] * (2 + len(PIECES)),
        out_specs=[VMEM] * 2,
        name="spec",
        **params(2 * waves * count * cols, 4 * count * cols),
    )(table, bands.astype(F32).reshape(1, rows), *pieces)
    olds = []
    for x in pieces:
        olds.append(along_tm(x, 1, 1))
    offset = (shifts + core.reshape(1) * cols) % width
    taps = pl.pallas_call(
        tap_kernel,
        out_shape=jax.ShapeDtypeStruct((TAP_ROWS, 2 * width), BF16),
        in_specs=[SMEM],
        out_specs=VMEM,
        name="taps",
        **params(1 << 20, 1 << 20),
    )(offset)

    def damp(i):
        lo, hi = PIECES[i]
        shape = jax.ShapeDtypeStruct((count, hi - lo), BF16)
        keep, send = pl.pallas_call(
            functools.partial(damp_kernel, lo, rows),
            out_shape=(shape, shape),
            in_specs=[VMEM] * 9,
            out_specs=[VMEM] * 2,
            scratch_shapes=[pltpu.VMEM((count, hi - lo), BF16)],
            **params(6 * waves * count * (hi - lo), 8 * count * (hi - lo)),
        )(raw, olds[i], pieces[i], spec, gain, table, turned, left, right)
        recv = lax.ppermute(send, "col", [(0, 1), (1, 0)])
        return (lo, cols + lo), (keep, recv)

    def accumulate(part, acc, last):
        starts, data = part
        inputs = [*data, taps] + ([] if acc is None else [acc])
        kernel = functools.partial(filter_kernel, starts, acc is None, last, rows)
        depth = 2 * data[0].shape[1]
        cost = params(2 * count * depth * width, 8 * count * width)
        specs = [VMEM] * len(inputs)
        if last:
            return pl.pallas_call(
                kernel,
                grid=(count // 256,),
                out_shape=jax.ShapeDtypeStruct((half, rows, width), BF16),
                in_specs=specs,
                out_specs=pl.BlockSpec((256 // rows, rows, width), lambda g: (g, 0, 0)),
                name="finish",
                **cost,
            )(*inputs)
        return pl.pallas_call(
            kernel,
            out_shape=jax.ShapeDtypeStruct((count, width), F32),
            in_specs=specs,
            out_specs=VMEM,
            input_output_aliases={} if acc is None else {len(inputs) - 1: 0},
            **cost,
        )(*inputs)

    acc = None
    for i in range(len(PIECES)):
        acc = accumulate(damp(i), acc, i == len(PIECES) - 1)
    return acc


def solution(mesh):
    placed = (
        P(("groups", "tm"), "cuts", "col"),
        P(("groups", "tm")),
        P(("groups", "cuts")),
        P(("groups", "cuts")),
    )

    return jax.shard_map(
        local,
        mesh=mesh,
        in_specs=placed,
        out_specs=P(("groups", "tm", "col"), "cuts", None),
        check_vma=False,
    )
```

profile of v0, /device:TPU:0, one launch (start us, length us, event | category | flops | bytes accessed | tf_op | source)
XLA Modules:
  0.0 71.1 jit_solution(5174172804431530467)
XLA Ops:
  0.0 0.0 copy-start.1
  0.0 0.0 copy-start.2
  0.0 5.2 %collective-permute-start = (bf16[512,2,640]{2,1,0:T(2,128)(2,1)}, bf16[512,2,640]{2,1,0:T(2,128)(2,1)S(1)}, u32[]{:S(2)}, u32[]{:S(2)}) collective-permute-start(bf16[512,2,640]{2,1,0:T(2,128)(2,1)} %raw.1), channel_id=1, source_target_pairs={{0,4},{4,8},{8,12},{2,6},{6,10},{10,14},{16,20},{20,24},{24,28},{1... | collective-permute-start | bytes 3932168 | tf_op jit(solution)/shard_map/ppermute | solution.py:187
  5.2 0.0 copy-start.3
  5.2 1.3 %copy-done.3 = bf16[512,2,640]{2,1,0:T(2,128)(2,1)S(1)} copy-done((bf16[512,2,640]{2,1,0:T(2,128)(2,1)S(1)}, bf16[512,2,640]{2,1,0:T(2,128)(2,1)}, u32[]{:S(2)}) %copy-start.3) | copy-done | bytes 1310744
  6.5 0.6 split.1
  7.1 0.0 copy-start.4
  7.1 0.7 copy-done.4
  7.8 1.3 %collective-permute-start.2 = (f32[2,640]{1,0:T(2,128)S(1)}, f32[2,640]{1,0:T(2,128)S(1)}, u32[]{:S(2)}, u32[]{:S(2)}) collective-permute-start(f32[2,640]{1,0:T(2,128)S(1)} %get-tuple-element.28.refs_1_), channel_id=1, source_target_pairs={{0,1},{2,3},{4,5},{6,7},{8,9},{10,11},{12,13},{14,15},{16,17},{18,... | collective-permute-start | bytes 15368 | tf_op jit(solution)/shard_map/ppermute | solution.py:237
  9.1 1.5 %collective-permute-start.10 = (bf16[1024,256]{1,0:T(8,128)(2,1)S(1)}, bf16[1024,256]{1,0:T(8,128)(2,1)}, u32[]{:S(2)}, u32[]{:S(2)}) collective-permute-start(bf16[1024,256]{1,0:T(8,128)(2,1)S(1)} %get-tuple-element.24.refs_0_.own), channel_id=1, source_target_pairs={{1,5},{5,9},{9,13},{3,7},{7,11},{11,15},{17,21},{21,25},{25,29},{1... | collective-permute-start | bytes 1572872 | tf_op jit(solution)/shard_map/ppermute | solution.py:187
  10.6 1.4 %collective-permute-start.8 = (bf16[1024,256]{1,0:T(8,128)(2,1)S(1)}, bf16[1024,256]{1,0:T(8,128)(2,1)}, u32[]{:S(2)}, u32[]{:S(2)}) collective-permute-start(bf16[1024,256]{1,0:T(8,128)(2,1)S(1)} %get-tuple-element.25.refs_1_.own), channel_id=1, source_target_pairs={{1,5},{5,9},{9,13},{3,7},{7,11},{11,15},{17,21},{21,25},{25,29},{1... | collective-permute-start | bytes 1572872 | tf_op jit(solution)/shard_map/ppermute | solution.py:187
  12.0 0.7 multiply_bitcast_fusion.1
  12.7 0.8 %select_reduce_fusion = f32[2]{0:T(128)S(1)} fusion(pred[4]{0:T(512)(128)(4,1)S(1)} %fusion, f32[4]{0:T(128)S(1)} %maximum_convert_fusion, f32[2]{0:T(128)} %param.9), kind=kLoop, calls=%fused_computation | loop fusion | flops 14 | bytes 36 | tf_op jit(solution)/shard_map/reduce_sum | solution.py:232
  13.5 0.0 collective-permute-done.2.refs_0_
  13.6 0.7 collective-permute-start.3
  14.3 0.1 copy.15
  14.3 0.1 copy.17
  14.4 0.7 %copy.13 = f32[2,1]{1,0:T(2,128)S(1)} copy(f32[2,1]{0,1:T(1,128)} %bitcast.8) | data formatting | bytes 16 | tf_op jit(solution)/shard_map/reshape | solution.py:229
  15.2 0.1 concatenate.3.refs_0_
  15.3 0.0 collective-permute-done.3.refs_1_
  15.3 0.1 shard_map.65
  15.4 0.7 collective-permute-start.4
  16.0 0.0 collective-permute-done.4.refs_1_
  16.0 0.7 shard_map.66
  16.7 0.6 collective-permute-start.5
  17.4 0.7 convert_bitcast_fusion.bands
  18.0 0.0 collective-permute-done.5.before.after
  18.1 1.3 %collective-permute-start.6 = (f32[2,640]{1,0:T(2,128)S(1)}, f32[2,640]{1,0:T(2,128)S(1)}, u32[]{:S(2)}, u32[]{:S(2)}) collective-permute-start(f32[2,640]{1,0:T(2,128)S(1)} %get-tuple-element.33), channel_id=1, source_target_pairs={{1,0},{3,2},{5,4},{7,6},{9,8},{11,10},{13,12},{15,14},{17,16},{19,... | collective-permute-start | bytes 15368 | tf_op jit(solution)/shard_map/ppermute | solution.py:270
  19.4 0.0 copy-start
  19.4 1.0 %copy-done = bf16[256,1024]{1,0:T(8,128)(2,1)S(1)} copy-done((bf16[256,1024]{1,0:T(8,128)(2,1)S(1)}, bf16[256,1024]{1,0:T(8,128)(2,1)}, u32[]{:S(2)}) %copy-start) | copy-done | bytes 524312
  20.4 0.0 copy-start.5
  20.4 0.9 %copy-done.5 = bf16[1024,128]{1,0:T(8,128)(2,1)S(1)} copy-done((bf16[1024,128]{1,0:T(8,128)(2,1)S(1)}, bf16[1024,128]{1,0:T(8,128)(2,1)}, u32[]{:S(2)}) %copy-start.5) | copy-done | bytes 262168
  21.4 0.6 spec.1
  21.9 22.6 %collective-permute-done.6.left = f32[2,640]{1,0:T(2,128)S(1)} collective-permute-done((f32[2,640]{1,0:T(2,128)S(1)}, f32[2,640]{1,0:T(2,128)S(1)}, u32[]{:S(2)}, u32[]{:S(2)}) %collective-permute-start.6) | collective-permute-done | bytes 5152 | tf_op jit(solution)/shard_map/ppermute | solution.py:270
  44.5 0.0 collective-permute-done.10.piece
  44.5 0.0 collective-permute-done.raw
  44.5 0.0 copy-done.1
  44.6 0.0 copy-done.2
  44.6 2.7 %shard_map.69 = (bf16[1024,256]{1,0:T(8,128)(2,1)S(1)}, bf16[1024,256]{1,0:T(8,128)(2,1)}) custom-call(bf16[512,2,640]{2,1,0:T(2,128)(2,1)S(1)} %collective-permute-done.raw, bf16[1024,256]{1,0:T(8,128)(2,1)} %collective-permute-done.10.piece, bf16[1024,256]{1,0:T(8,128)(2,1)S(1)} %get-tuple-element.24.refs_0_.own, f32[256,640]{1,0:T(8,128)S(1)} %get-tuple-element.26.spec, ...), custom_call_target="tpu_custom_call" | custom-call | flops 402653184 | bytes 2097152 | tf_op jit(solution)/shard_map/pallas_call | solution.py:320
  47.3 0.0 copy-start.6
  47.3 1.9 %collective-permute-start.11 = (bf16[1024,256]{1,0:T(8,128)(2,1)}, bf16[1024,256]{1,0:T(8,128)(2,1)}, u32[]{:S(2)}, u32[]{:S(2)}) collective-permute-start(bf16[1024,256]{1,0:T(8,128)(2,1)} %get-tuple-element.40), channel_id=1, source_target_pairs={{0,1},{1,0},{2,3},{3,2},{4,5},{5,4},{6,7},{7,6},{8,9},{9,8},{10,11... | collective-permute-start | bytes 1572872 | tf_op jit(solution)/shard_map/ppermute | solution.py:328
  49.2 0.0 collective-permute-done.8.piece
  49.2 2.7 %shard_map.68 = (bf16[1024,256]{1,0:T(8,128)(2,1)S(1)}, bf16[1024,256]{1,0:T(8,128)(2,1)}) custom-call(bf16[512,2,640]{2,1,0:T(2,128)(2,1)S(1)} %collective-permute-done.raw, bf16[1024,256]{1,0:T(8,128)(2,1)} %collective-permute-done.8.piece, bf16[1024,256]{1,0:T(8,128)(2,1)S(1)} %get-tuple-element.25.refs_1_.own, f32[256,640]{1,0:T(8,128)S(1)} %get-tuple-element.26.spec, ...), custom_call_target="tpu_custom_call" | custom-call | flops 402653184 | bytes 2097152 | tf_op jit(solution)/shard_map/pallas_call | solution.py:320
  52.0 0.1 collective-permute-start.9
  52.1 0.7 collective-permute-start.1
  52.8 0.0 collective-permute-done.1.piece
  52.8 1.6 %shard_map.67 = (bf16[1024,128]{1,0:T(8,128)(2,1)S(1)}, bf16[1024,128]{1,0:T(8,128)(2,1)}) custom-call(bf16[512,2,640]{2,1,0:T(2,128)(2,1)S(1)} %collective-permute-done.raw, bf16[1024,128]{1,0:T(8,128)(2,1)S(1)} %collective-permute-done.1.piece, bf16[1024,128]{1,0:T(8,128)(2,1)S(1)} %copy-done.5, f32[256,640]{1,0:T(8,128)S(1)} %get-tuple-element.26.spec, ...), custom_call_target="tpu_custom_call" | custom-call | flops 201326592 | bytes 1048576 | tf_op jit(solution)/shard_map/pallas_call | solution.py:320
  54.4 0.0 copy-done.6
  54.4 0.0 copy-start.8
  54.4 0.7 copy-done.8
  55.1 6.1 %collective-permute-start.7 = (bf16[1024,128]{1,0:T(8,128)(2,1)}, bf16[1024,128]{1,0:T(8,128)(2,1)S(1)}, u32[]{:S(2)}, u32[]{:S(2)}) collective-permute-start(bf16[1024,128]{1,0:T(8,128)(2,1)} %get-tuple-element.36), channel_id=1, source_target_pairs={{0,1},{1,0},{2,3},{3,2},{4,5},{5,4},{6,7},{7,6},{8,9},{9,8},{10,11... | collective-permute-start | bytes 786440 | tf_op jit(solution)/shard_map/ppermute | solution.py:328
  61.8 0.5 taps.1.refs_2_
  62.3 0.0 collective-permute-done.11.refs_1_
  62.3 0.0 copy-start.7
  62.4 1.0 %copy-done.7 = bf16[1024,256]{1,0:T(8,128)(2,1)S(1)} copy-done((bf16[1024,256]{1,0:T(8,128)(2,1)S(1)}, bf16[1024,256]{1,0:T(8,128)(2,1)}, u32[]{:S(2)}) %copy-start.7) | copy-done | bytes 524312
  63.4 2.6 %shard_map.70.refs_3_ = f32[1024,1280]{1,0:T(8,128)S(1)} custom-call(bf16[1024,256]{1,0:T(8,128)(2,1)S(1)} %copy-done.7, bf16[1024,256]{1,0:T(8,128)(2,1)} %collective-permute-done.11.refs_1_, bf16[256,2560]{1,0:T(8,128)(2,1)S(1)} %taps.1.refs_2_), custom_call_target="tpu_custom_call" | custom-call | flops 1342177280 | bytes 10485760 | tf_op jit(solution)/shard_map/pallas_call | solution.py:348
  66.0 0.0 collective-permute-done.9.refs_1_
  66.0 0.0 copy-start.9
  66.0 1.8 %shard_map.71.refs_3_ = f32[1024,1280]{1,0:T(8,128)S(1)} custom-call(bf16[1024,256]{1,0:T(8,128)(2,1)S(1)} %get-tuple-element.37.refs_0_, bf16[1024,256]{1,0:T(8,128)(2,1)S(1)} %collective-permute-done.9.refs_1_, bf16[256,2560]{1,0:T(8,128)(2,1)S(1)} %taps.1.refs_2_, f32[1024,1280]{1,0:T(8,128)S(1)} %shard_map.70.refs_3_), custom_call_target="tpu_custom_call", output_to_operand_aliasing={{}: (3, {})} | custom-call | flops 1342177280 | bytes 10485760 | tf_op jit(solution)/shard_map/pallas_call | solution.py:348
  67.8 0.0 collective-permute-done.7.refs_1_
  67.8 0.0 copy-done.9
  67.8 3.3 %finish.1 = bf16[512,2,1280]{2,1,0:T(2,128)(2,1)} custom-call(bf16[1024,128]{1,0:T(8,128)(2,1)S(1)} %copy-done.9, bf16[1024,128]{1,0:T(8,128)(2,1)S(1)} %collective-permute-done.7.refs_1_, bf16[256,2560]{1,0:T(8,128)(2,1)S(1)} %taps.1.refs_2_, f32[1024,1280]{1,0:T(8,128)S(1)} %shard_map.71.refs_3_), custom_call_target="tpu_custom_call" | custom-call | flops 671088640 | bytes 10485760 | tf_op jit(solution)/shard_map/finish/pallas_call | solution.py:339
  (6 shorter events, 0.0 us)
Async XLA Ops:
  0.0 44.5 %copy-start.1 = (bf16[256,1024]{1,0:T(8,128)(2,1)S(1)}, bf16[256,1024]{1,0:T(8,128)(2,1)}, u32[]{:S(2)}) copy-start(bf16[256,1024]{1,0:T(8,128)(2,1)} %constant.39.clone.table) | copy-start | bytes 1572868
  0.0 44.6 %copy-start.2 = (bf16[1024,256]{1,0:T(8,128)(2,1)S(1)}, bf16[1024,256]{1,0:T(8,128)(2,1)}, u32[]{:S(2)}) copy-start(bf16[1024,256]{1,0:T(8,128)(2,1)} %constant.40.clone.turned) | copy-start | bytes 1572868
  0.0 44.5 %collective-permute-start = (bf16[512,2,640]{2,1,0:T(2,128)(2,1)}, bf16[512,2,640]{2,1,0:T(2,128)(2,1)S(1)}, u32[]{:S(2)}, u32[]{:S(2)}) collective-permute-start(bf16[512,2,640]{2,1,0:T(2,128)(2,1)} %raw.1), channel_id=1, source_target_pairs={{0,4},{4,8},{8,12},{2,6},{6,10},{10,14},{16,20},{20,24},{24,28},{1... | collective-permute-start | bytes 3932168 | tf_op jit(solution)/shard_map/ppermute | solution.py:187
  5.2 1.3 %copy-start.3 = (bf16[512,2,640]{2,1,0:T(2,128)(2,1)S(1)}, bf16[512,2,640]{2,1,0:T(2,128)(2,1)}, u32[]{:S(2)}) copy-start(bf16[512,2,640]{2,1,0:T(2,128)(2,1)} %raw.1) | copy-start | bytes 3932164
  7.1 0.7 copy-start.4
  7.8 5.7 %collective-permute-start.2 = (f32[2,640]{1,0:T(2,128)S(1)}, f32[2,640]{1,0:T(2,128)S(1)}, u32[]{:S(2)}, u32[]{:S(2)}) collective-permute-start(f32[2,640]{1,0:T(2,128)S(1)} %get-tuple-element.28.refs_1_), channel_id=1, source_target_pairs={{0,1},{2,3},{4,5},{6,7},{8,9},{10,11},{12,13},{14,15},{16,17},{18,... | collective-permute-start | bytes 15368 | tf_op jit(solution)/shard_map/ppermute | solution.py:237
  9.1 35.4 %collective-permute-start.10 = (bf16[1024,256]{1,0:T(8,128)(2,1)S(1)}, bf16[1024,256]{1,0:T(8,128)(2,1)}, u32[]{:S(2)}, u32[]{:S(2)}) collective-permute-start(bf16[1024,256]{1,0:T(8,128)(2,1)S(1)} %get-tuple-element.24.refs_0_.own), channel_id=1, source_target_pairs={{1,5},{5,9},{9,13},{3,7},{7,11},{11,15},{17,21},{21,25},{25,29},{1... | collective-permute-start | bytes 1572872 | tf_op jit(solution)/shard_map/ppermute | solution.py:187
  10.6 38.7 %collective-permute-start.8 = (bf16[1024,256]{1,0:T(8,128)(2,1)S(1)}, bf16[1024,256]{1,0:T(8,128)(2,1)}, u32[]{:S(2)}, u32[]{:S(2)}) collective-permute-start(bf16[1024,256]{1,0:T(8,128)(2,1)S(1)} %get-tuple-element.25.refs_1_.own), channel_id=1, source_target_pairs={{1,5},{5,9},{9,13},{3,7},{7,11},{11,15},{17,21},{21,25},{25,29},{1... | collective-permute-start | bytes 1572872 | tf_op jit(solution)/shard_map/ppermute | solution.py:187
  13.6 1.7 %collective-permute-start.3 = (f32[2,1280]{1,0:T(2,128)S(1)}, f32[2,1280]{1,0:T(2,128)S(1)}, u32[]{:S(2)}, u32[]{:S(2)}) collective-permute-start(f32[2,1280]{1,0:T(2,128)S(1)} %shard_map.64.refs_2_), channel_id=1, source_target_pairs={{1,5},{5,9},{9,13},{3,7},{7,11},{11,15},{17,21},{21,25},{25,29},{1... | collective-permute-start | bytes 30728 | tf_op jit(solution)/shard_map/ppermute | solution.py:187
  15.4 0.7 collective-permute-start.4
  16.7 1.3 %collective-permute-start.5 = (f32[1,1280]{1,0:T(1,128)S(1)}, f32[1,1280]{1,0:T(1,128)S(1)}, u32[]{:S(2)}, u32[]{:S(2)}) collective-permute-start(f32[1,1280]{1,0:T(1,128)S(1)} %get-tuple-element.32), channel_id=1, source_target_pairs={{1,3},{3,1},{5,7},{7,5},{9,11},{11,9},{13,15},{15,13},{17,19},{19,... | collective-permute-start | bytes 15368 | tf_op jit(solution)/shard_map/ppermute | solution.py:217
  18.1 26.5 %collective-permute-start.6 = (f32[2,640]{1,0:T(2,128)S(1)}, f32[2,640]{1,0:T(2,128)S(1)}, u32[]{:S(2)}, u32[]{:S(2)}) collective-permute-start(f32[2,640]{1,0:T(2,128)S(1)} %get-tuple-element.33), channel_id=1, source_target_pairs={{1,0},{3,2},{5,4},{7,6},{9,8},{11,10},{13,12},{15,14},{17,16},{19,... | collective-permute-start | bytes 15368 | tf_op jit(solution)/shard_map/ppermute | solution.py:270
  19.4 1.0 %copy-start = (bf16[256,1024]{1,0:T(8,128)(2,1)S(1)}, bf16[256,1024]{1,0:T(8,128)(2,1)}, u32[]{:S(2)}) copy-start(bf16[256,1024]{1,0:T(8,128)(2,1)} %constant.39.clone.table) | copy-start | bytes 1572868
  20.4 0.9 %copy-start.5 = (bf16[1024,128]{1,0:T(8,128)(2,1)S(1)}, bf16[1024,128]{1,0:T(8,128)(2,1)}, u32[]{:S(2)}) copy-start(bf16[1024,128]{1,0:T(8,128)(2,1)} %copy-done.4) | copy-start | bytes 786436
  47.3 7.1 %copy-start.6 = (bf16[1024,256]{1,0:T(8,128)(2,1)}, bf16[1024,256]{1,0:T(8,128)(2,1)S(1)}, u32[]{:S(2)}) copy-start(bf16[1024,256]{1,0:T(8,128)(2,1)S(1)} %get-tuple-element.39.refs_0_) | copy-start | bytes 1572868
  47.3 15.0 %collective-permute-start.11 = (bf16[1024,256]{1,0:T(8,128)(2,1)}, bf16[1024,256]{1,0:T(8,128)(2,1)}, u32[]{:S(2)}, u32[]{:S(2)}) collective-permute-start(bf16[1024,256]{1,0:T(8,128)(2,1)} %get-tuple-element.40), channel_id=1, source_target_pairs={{0,1},{1,0},{2,3},{3,2},{4,5},{5,4},{6,7},{7,6},{8,9},{9,8},{10,11... | collective-permute-start | bytes 1572872 | tf_op jit(solution)/shard_map/ppermute | solution.py:328
  52.0 14.0 %collective-permute-start.9 = (bf16[1024,256]{1,0:T(8,128)(2,1)}, bf16[1024,256]{1,0:T(8,128)(2,1)S(1)}, u32[]{:S(2)}, u32[]{:S(2)}) collective-permute-start(bf16[1024,256]{1,0:T(8,128)(2,1)} %get-tuple-element.38), channel_id=1, source_target_pairs={{0,1},{1,0},{2,3},{3,2},{4,5},{5,4},{6,7},{7,6},{8,9},{9,8},{10,11... | collective-permute-start | bytes 1572872 | tf_op jit(solution)/shard_map/ppermute | solution.py:328
  52.1 0.7 collective-permute-start.1
  54.4 0.7 copy-start.8
  55.1 12.7 %collective-permute-start.7 = (bf16[1024,128]{1,0:T(8,128)(2,1)}, bf16[1024,128]{1,0:T(8,128)(2,1)S(1)}, u32[]{:S(2)}, u32[]{:S(2)}) collective-permute-start(bf16[1024,128]{1,0:T(8,128)(2,1)} %get-tuple-element.36), channel_id=1, source_target_pairs={{0,1},{1,0},{2,3},{3,2},{4,5},{5,4},{6,7},{7,6},{8,9},{9,8},{10,11... | collective-permute-start | bytes 786440 | tf_op jit(solution)/shard_map/ppermute | solution.py:328
  62.3 1.0 %copy-start.7 = (bf16[1024,256]{1,0:T(8,128)(2,1)S(1)}, bf16[1024,256]{1,0:T(8,128)(2,1)}, u32[]{:S(2)}) copy-start(bf16[1024,256]{1,0:T(8,128)(2,1)} %copy-done.6) | copy-start | bytes 1572868
  66.0 1.8 %copy-start.9 = (bf16[1024,128]{1,0:T(8,128)(2,1)S(1)}, bf16[1024,128]{1,0:T(8,128)(2,1)}, u32[]{:S(2)}) copy-start(bf16[1024,128]{1,0:T(8,128)(2,1)} %copy-done.8) | copy-start | bytes 786436
where the time goes:
time: 71.7 us; the launch traced here: 71.1 us
  waiting for transfers between devices  22.6 us (32%)
  starting transfers between devices  21.4 us (30%)
  Pallas kernels  17.3 us (24%)
  local copies, waits for them, and re-layouts  6.78 us (9%)
  other arithmetic  2.18 us (3%)
  between operations  0.89 us (1%)
    ppermute x1, waiting for transfers between devices, cycle_of(): left = lax.ppermute(left, 'col', [(1, 0)])  22.6 us
    ppermute x6, starting transfers between devices, along_tm(): return lax.ppermute(x, ('tm', 'col'), route)  10.1 us
    ppermute x3, starting transfers between devices, damp(): recv = lax.ppermute(send, 'col', [(0, 1), (1, 0)])  8.11 us
    pallas_call x3, Pallas kernels, damp(): pl.pallas_call(functools.partial(damp_kernel, lo, rows), out_shape=(shape...  7.08 us
    unnamed x20, local copies, waits for them, and re-layouts  5.75 us
    pallas_call x2, Pallas kernels, accumulate(): pl.pallas_call(kernel, out_shape=jax.ShapeDtypeStruct((count, width), F32...  4.35 us
    pallas_call x1, Pallas kernels, accumulate(): pl.pallas_call(kernel, grid=(count // 256,), out_shape=jax.ShapeDtypeStru...  3.35 us
  transfers between devices with their start and end apart: 12, of which 1 were waited for; matrix products, arithmetic and copies ran while one was open for 5% of the time, Pallas kernels for 20%

commit v1 on v0

--- a/solution.py
+++ b/solution.py
@@ -12,10 +12,13 @@
 BAND_FREQS = 64
 WAVES = 2 * BAND_FREQS
 TAP_ROWS = 256
-PIECES = ((0, 256), (256, 512), (512, 640))
+PIECES = ((0, 128), (128, 256), (256, 512), (512, 640))
+GROUPS = ((0, 1), (2,), (3,))
+WRAPS = 2
 
 VMEM = pl.BlockSpec(memory_space=pltpu.VMEM)
 SMEM = pl.BlockSpec(memory_space=pltpu.SMEM)
+HBM = pl.BlockSpec(memory_space=pltpu.HBM)
 F32 = jnp.float32
 BF16 = jnp.bfloat16
 
@@ -41,39 +44,50 @@
     return lax.broadcasted_iota(jnp.int32, shape, dim) % rows
 
 
-def split_kernel(raw, *outs):
-    *pieces, sums = outs
+def split_kernel(raw, *refs):
+    *pieces, sums = refs
     half, rows, cols = raw.shape
-    block = 128
-    total = None
-    for start in range(0, half, block):
-        x = raw[start : start + block].reshape(block * rows, cols)
-        shape = (8, block * rows)
-        pick = pattern(shape, 1, rows) == lax.broadcasted_iota(jnp.int32, shape, 0)
-        part = jnp.dot(pick.astype(F32).astype(BF16), x, preferred_element_type=F32)
-        total = part if total is None else total + part
-        for (lo, hi), out in zip(PIECES, pieces):
-            out[start * rows : (start + block) * rows, :] = x[:, lo:hi]
+    x = raw[...].reshape(half * rows, cols)
+    for (lo, hi), out in zip(PIECES, pieces):
+        out[...] = x[:, lo:hi]
+    shape = (8, half * rows)
+    pick = pattern(shape, 1, rows) == lax.broadcasted_iota(jnp.int32, shape, 0)
+    total = jnp.dot(pick.astype(F32).astype(BF16), x, preferred_element_type=F32)
     sums[...] = total[:rows, :]
 
 
-def spec_kernel(rows, angles, table, bands, *refs):
-    *pieces, spec, gain = refs
+def spec_kernel(rows, distances, angles, bands, memory, table, *refs):
+    *pieces, spec, gain, scales = refs
     waves = spec.shape[0]
     index = lax.broadcasted_iota(jnp.int32, (waves, 1), 0)
     k = index // rows % BAND_FREQS + 1
     flip = jnp.where(k % 2 == 0, 1.0, -1.0)
     for (lo, hi), piece in zip(PIECES, pieces):
         spec[:, lo:hi] = flip * jnp.dot(table[...], piece[...], preferred_element_type=F32)
-    band = bands[:, :1]
+    band = jnp.full((waves, 1), bands[0], jnp.int32)
+    row = lax.broadcasted_iota(jnp.int32, (rows, 1), 0)
+    decay = jnp.full((rows, 1), memory[0], F32)
     for s in range(1, rows):
-        band = jnp.where(index % rows == s, bands[:, s : s + 1], band)
+        band = jnp.where(index % rows == s, bands[s], band)
+        decay = jnp.where(row == s, memory[s], decay)
     square = (k * k).astype(F32)
-    gain[...] = jnp.exp(-square / (2.0 * band * band)) * (2.0 / angles)
-
-
-def smooth_kernel(estimate, before, after, left, right):
-    cols = left.shape[1]
+    gain[...] = jnp.exp(-square / (2.0 * (band * band).astype(F32))) * (2.0 / angles)
+    power, done = decay, 1
+    for i, d in enumerate(distances):
+        while done < d:
+            power, done = power * power, 2 * done
+        scales[:, i : i + 1] = jnp.ones_like(decay) if d == 1 else power / decay
+        scales[:, len(distances) + i : len(distances) + i + 1] = power
+    weight = jnp.ones_like(decay)
+    steps = lax.axis_index("tm")
+    for j in range(lax.axis_size("tm") - 1):
+        weight = jnp.where(j < steps, weight * decay + 1.0, weight)
+    scales[:, 2 * len(distances) : 2 * len(distances) + 1] = decay
+    scales[:, 2 * len(distances) + 1 : 2 * len(distances) + 2] = 1.0 / (weight * angles)
+
+
+def smooth_kernel(estimate, before, after, out):
+    rows, cols = estimate.shape
     x = estimate[...]
     place = lax.axis_index("cuts")
     first = jnp.where(place != 0, before[...], 0.0)
@@ -81,37 +95,24 @@
     up = jnp.concatenate([first, x[:-1]], axis=0)
     down = jnp.concatenate([x[1:], last], axis=0)
     ring = (up + 2.0 * x + down) * 0.25
-    left[...] = ring[:, :cols]
-    right[...] = ring[:, cols:]
-
-
-def damp_kernel(lo, rows, raw, piece, own, spec, gain, table, turned, left, right, *outs):
-    keep, send, old = outs
+    row = pattern((8, cols), 0, rows)
+    total = jnp.broadcast_to(ring[:1], (8, cols))
+    for s in range(1, rows):
+        total = jnp.where(row == s, jnp.broadcast_to(ring[s : s + 1], (8, cols)), total)
+    out[...] = total
+
+
+def damp_kernel(lo, rows, piece, own, spec, gain, table, turned, cycle, keep, send, old):
     count, cols = piece.shape
     waves = turned.shape[1]
     core = lax.axis_index("col")
-
-    @pl.when(core == 0)
-    def _():
-        old[...] = raw[:, :, lo : lo + cols].reshape(count, cols)
-
-    @pl.when(core != 0)
-    def _():
-        old[...] = piece[...]
-
+    old[...] = jnp.where(lax.axis_index("tm") > 0, piece[...], jnp.zeros_like(piece))
     total = jnp.dot(table[...], old[...], preferred_element_type=F32)
     total = (total + spec[:, lo : lo + cols]) * gain[...]
     index = lax.broadcasted_iota(jnp.int32, (waves, 1), 0)
     k = index // rows % BAND_FREQS + 1
     flip = jnp.where(k % 2 == 0, 1.0, -1.0)
-    row = pattern((8, cols), 0, rows)
-    ring = None
-    for s in range(rows):
-        line = jnp.where(
-            core == 0, left[s : s + 1, lo : lo + cols], right[s : s + 1, lo : lo + cols]
-        )
-        line = jnp.broadcast_to(line, (8, cols))
-        ring = line if s == 0 else jnp.where(row == s, line, ring)
+    ring = cycle[:, lo : lo + cols]
 
     def damp(half, source, target):
         scaled = (total if half == 0 else total * flip).astype(BF16)
@@ -181,10 +182,10 @@
                     out[rows, : width - room] = tap[:, room:]
 
 
-def along_tm(x, core, distance):
-    tm, cores = lax.axis_size("tm"), lax.axis_size("col")
-    route = [(cores * i + core, cores * (i + distance) + core) for i in range(tm - distance)]
-    return lax.ppermute(x, ("tm", "col"), route)
+def along_tm(x, distance, wrap=True):
+    tm = lax.axis_size("tm")
+    route = [(i, (i + distance) % tm) for i in range(tm if wrap else tm - distance)]
+    return lax.ppermute(x, "tm", route)
 
 
 def tiny(body, shapes, *args):
@@ -209,40 +210,34 @@
 
 
 def row_neighbours(last, first):
-    cuts, cores = lax.axis_size("cuts"), lax.axis_size("col")
-    at = [cores * i + cores - 1 for i in range(cuts)]
+    cuts = lax.axis_size("cuts")
     if cuts == 1:
         return first, last
+    up = [(i, (i + 1) % cuts) for i in range(cuts)]
+    before = lax.ppermute(last, "cuts", up)
     if cuts == 2:
-        got = lax.ppermute(last, ("cuts", "col"), [(at[0], at[1]), (at[1], at[0])])
-        return got, got
-    up = list(zip(at[:-1], at[1:]))
-    before = lax.ppermute(last, ("cuts", "col"), up)
-    after = lax.ppermute(first, ("cuts", "col"), [(j, i) for i, j in up])
-    return before, after
-
-
-def cycle_of(sums, memory, angles):
+        return before, before
+    return before, lax.ppermute(first, "cuts", [(j, i) for i, j in up])
+
+
+def lag_distances(tm):
+    return [1 << i for i in range(max(tm - 1, 1).bit_length())]
+
+
+def cycle_of(sums, first_lag, scales):
     rows, cols = sums.shape
-    tm, cores = lax.axis_size("tm"), lax.axis_size("col")
-    wide = (rows, cores * cols)
-    decay = memory.reshape(rows, 1)
-    steps = lax.axis_index("tm") - jnp.arange(tm, dtype=jnp.int32)
-    powers = jnp.power(memory[None, :], jnp.maximum(steps, 0).astype(F32)[:, None])
-    weight = jnp.sum(jnp.where(steps[:, None] >= 0, powers, 0.0), axis=0)[:, None]
-    distances = [1 << i for i in range(max(tm - 1, 1).bit_length())]
-    scales = [decay ** (d - 1) for d in distances] + [decay**d for d in distances]
-    scales = jnp.concatenate(scales + [decay, weight * angles], axis=1)
+    wide = (rows, cols)
+    distances = lag_distances(lax.axis_size("tm"))
     n = len(distances)
-    left = lax.ppermute(sums, "col", [(0, 1)])
-    (whole,) = tiny(lambda a, b: (jnp.concatenate([a, b], axis=1),), [wide], left, sums)
-    older, window = None, whole
+    older, window, got = None, sums, first_lag
     for i, d in enumerate(distances):
-        got = along_tm(window, 1, d)
+        if i > 0:
+            got = along_tm(window, d)
         if i == n - 1:
             break
 
-        def extend(c, got, window, older=None, i=i):
+        def extend(c, got, window, older=None, i=i, d=d):
+            got = jnp.where(lax.axis_index("tm") >= d, got, 0.0)
             further = got if older is None else older + c[:, i : i + 1] * got
             return further, window + c[:, n + i : n + i + 1] * got
 
@@ -250,25 +245,24 @@
         older, window = tiny(extend, [wide] * 2, scales, got, window, *extra)
 
     def estimate_of(c, got, whole, older=None):
+        got = jnp.where(lax.axis_index("tm") >= distances[-1], got, 0.0)
         total = got if older is None else older + c[:, n - 1 : n] * got
-        x = (whole + c[:, 2 * n : 2 * n + 1] * total + total) / c[:, 2 * n + 1 :]
+        total = whole + c[:, 2 * n : 2 * n + 1] * total + total
+        x = total * c[:, 2 * n + 1 : 2 * n + 2]
         return x, *row_edges(x)
 
     extra = () if older is None else (older,)
-    edge = (1, wide[1])
-    estimate, last, first = tiny(estimate_of, [wide, edge, edge], scales, got, whole, *extra)
+    edge = (1, cols)
+    estimate, last, first = tiny(estimate_of, [wide, edge, edge], scales, got, sums, *extra)
     before, after = row_neighbours(last, first)
-    shape = jax.ShapeDtypeStruct((rows, cols), F32)
-    left, right = pl.pallas_call(
+    return pl.pallas_call(
         smooth_kernel,
-        out_shape=(shape, shape),
+        out_shape=jax.ShapeDtypeStruct((8, cols), F32),
         in_specs=[VMEM] * 3,
-        out_specs=[VMEM] * 2,
+        out_specs=VMEM,
         name="smooth",
         **params(1 << 16, 1 << 16),
     )(estimate, before, after)
-    left = lax.ppermute(left, "col", [(1, 0)])
-    return left, right
 
 
 def local(turns, shifts, bands, memory):
@@ -278,32 +272,35 @@
     waves = WAVES * rows
     table, turned = (jnp.asarray(t) for t in wave_tables(half, rows))
     core = lax.axis_index("col").astype(jnp.int32)
-
-    raw = along_tm(turns, 0, 1)
+    distances = lag_distances(lax.axis_size("tm"))
+    n = len(PIECES)
+
     shapes = [jax.ShapeDtypeStruct((count, hi - lo), BF16) for lo, hi in PIECES]
     *pieces, sums = pl.pallas_call(
         split_kernel,
         out_shape=(*shapes, jax.ShapeDtypeStruct((rows, cols), F32)),
         in_specs=[VMEM],
-        out_specs=[VMEM] * (len(PIECES) + 1),
+        out_specs=[VMEM] * (n + 1),
         name="split",
         **params(16 * count * cols, 4 * count * cols),
     )(turns)
-    left, right = cycle_of(sums, memory, angles)
-    spec, gain = pl.pallas_call(
-        functools.partial(spec_kernel, rows, angles),
+    spec, gain, scales = pl.pallas_call(
+        functools.partial(spec_kernel, rows, distances, angles),
         out_shape=(
             jax.ShapeDtypeStruct((waves, cols), F32),
             jax.ShapeDtypeStruct((waves, 1), F32),
+            jax.ShapeDtypeStruct((rows, 128), F32),
         ),
-        in_specs=[VMEM] * (2 + len(PIECES)),
-        out_specs=[VMEM] * 2,
+        in_specs=[SMEM] * 2 + [VMEM] * (1 + n),
+        out_specs=[VMEM] * 3,
         name="spec",
         **params(2 * waves * count * cols, 4 * count * cols),
-    )(table, bands.astype(F32).reshape(1, rows), *pieces)
+    )(bands, memory, table, *pieces)
+    first_lag = along_tm(sums, 1)
+    cycle = cycle_of(sums, first_lag, scales)
     olds = []
-    for x in pieces:
-        olds.append(along_tm(x, 1, 1))
+    for i, x in enumerate(pieces):
+        olds.append(along_tm(x, 1, wrap=i < WRAPS))
     offset = (shifts + core.reshape(1) * cols) % width
     taps = pl.pallas_call(
         tap_kernel,
@@ -320,19 +317,20 @@
         keep, send = pl.pallas_call(
             functools.partial(damp_kernel, lo, rows),
             out_shape=(shape, shape),
-            in_specs=[VMEM] * 9,
+            in_specs=[VMEM] * 7,
             out_specs=[VMEM] * 2,
             scratch_shapes=[pltpu.VMEM((count, hi - lo), BF16)],
             **params(6 * waves * count * (hi - lo), 8 * count * (hi - lo)),
-        )(raw, olds[i], pieces[i], spec, gain, table, turned, left, right)
+        )(olds[i], pieces[i], spec, gain, table, turned, cycle)
         recv = lax.ppermute(send, "col", [(0, 1), (1, 0)])
         return (lo, cols + lo), (keep, recv)
 
-    def accumulate(part, acc, last):
-        starts, data = part
+    def accumulate(parts, acc, last):
+        starts = sum((p[0] for p in parts), ())
+        data = sum((p[1] for p in parts), ())
         inputs = [*data, taps] + ([] if acc is None else [acc])
         kernel = functools.partial(filter_kernel, starts, acc is None, last, rows)
-        depth = 2 * data[0].shape[1]
+        depth = sum(x.shape[1] for x in data)
         cost = params(2 * count * depth * width, 8 * count * width)
         specs = [VMEM] * len(inputs)
         if last:
@@ -354,9 +352,10 @@
             **cost,
         )(*inputs)
 
+    parts = [damp(i) for i in range(n)]
     acc = None
-    for i in range(len(PIECES)):
-        acc = accumulate(damp(i), acc, i == len(PIECES) - 1)
+    for i, group in enumerate(GROUPS):
+        acc = accumulate([parts[j] for j in group], acc, i == len(GROUPS) - 1)
     return acc
 
 

time: 71.7 us -> 61 us (0.85)
  starting transfers between devices: 21.4 us -> 17.7 us
  local copies, waits for them, and re-layouts: 6.78 us -> 3.76 us
  other arithmetic: 2.18 us -> 0 us
  Pallas kernels: 17.3 us -> 15.8 us
    ppermute x3 -> x4, starting transfers between devices: 8.11 us -> 0.65 us  [damp(): recv = lax.ppermute(send, 'col', [(0, 1), (1, 0)])]
    ppermute x9 -> x7, starting transfers between devices: 13.3 us -> 17 us  [the longest x6 15.6 us: along_tm(): return lax.ppermute(x, 'tm', route)]
    pallas_call x3 -> x4, Pallas kernels: 7.08 us -> 4.59 us  [damp(): pl.pallas_call(functools.partial(damp_kernel, lo, rows), out_shape=(shape...]
    unnamed x20 -> x12, local copies, waits for them, and re-layouts: 5.75 us -> 3.76 us
    reduce_sum x1 -> x0, other arithmetic: 0.85 us -> none  [cycle_of(): jnp.sum(jnp.where(steps[:, None] >= 0, powers, 0.0), axis=0)[:, None]]
    reshape x1 -> x0, local copies, waits for them, and re-layouts: 0.74 us -> none  [cycle_of(): decay = memory.reshape(rows, 1)]
    ppermute x9 -> x7, waiting for transfers between devices: 22.6 us -> 22.6 us  [the longest x6 20.5 us: along_tm(): return lax.ppermute(x, 'tm', route)]
  transfers between devices with their start and end apart: 12 -> 11, of which waited for: 1 -> 4; matrix products, arithmetic and copies ran while one was open for 5% -> 0% of each run, Pallas kernels for 20% -> 19%
where the time goes in v1:
time: 61 us; the launch traced here: 60.6 us
  waiting for transfers between devices  22.6 us (37%)
  starting transfers between devices  17.7 us (29%)
  Pallas kernels  15.8 us (26%)
  local copies, waits for them, and re-layouts  3.76 us (6%)
  between operations  0.82 us (1%)
    ppermute x6, waiting for transfers between devices, along_tm(): return lax.ppermute(x, 'tm', route)  20.5 us
    ppermute x6, starting transfers between devices, along_tm(): return lax.ppermute(x, 'tm', route)  15.6 us
    pallas_call x2, Pallas kernels, accumulate(): pl.pallas_call(kernel, out_shape=jax.ShapeDtypeStruct((count, width), F32...  4.64 us
    pallas_call x4, Pallas kernels, damp(): pl.pallas_call(functools.partial(damp_kernel, lo, rows), out_shape=(shape...  4.59 us
    unnamed x12, local copies, waits for them, and re-layouts  3.76 us
    pallas_call x1, Pallas kernels, accumulate(): pl.pallas_call(kernel, grid=(count // 256,), out_shape=jax.ShapeDtypeStru...  3.35 us
    ppermute x1, waiting for transfers between devices, row_neighbours(): before = lax.ppermute(last, 'cuts', up)  2.1 us
    ppermute x1, starting transfers between devices, row_neighbours(): before = lax.ppermute(last, 'cuts', up)  1.49 us
  transfers between devices with their start and end apart: 11, of which 4 were waited for; matrix products, arithmetic and copies ran while one was open for 0% of the time, Pallas kernels for 19%

profile of v1, /device:TPU:0, one launch (start us, length us, event | category | flops | bytes accessed | tf_op | source)
XLA Modules:
  0.0 60.6 jit_solution(13963235192103271443)
XLA Ops:
  0.0 0.0 copy-start.1
  0.0 0.0 copy-start.2
  0.0 0.0 copy-start.3
  0.0 1.4 %copy-done.3 = bf16[512,2,640]{2,1,0:T(2,128)(2,1)S(1)} copy-done((bf16[512,2,640]{2,1,0:T(2,128)(2,1)S(1)}, bf16[512,2,640]{2,1,0:T(2,128)(2,1)}, u32[]{:S(2)}) %copy-start.3) | copy-done | bytes 1310744
  1.4 0.6 %split.1 = (bf16[1024,128]{1,0:T(8,128)(2,1)S(1)}, bf16[1024,128]{1,0:T(8,128)(2,1)S(1)}, bf16[1024,256]{1,0:T(8,128)(2,1)S(1)}, bf16[1024,128]{1,0:T(8,128)(2,1)S(1)}, f32[2,640]{1,0:T(2,128)S(1)}) custom-call(bf16[512,2,640]{2,1,0:T(2,128)(2,1)S(1)} %copy-done.3), custom_call_target="tpu_custom_call" | custom-call | flops 10485760 | bytes 2621440 | tf_op jit(solution)/shard_map/split/pallas_call | solution.py:279
  2.1 5.0 %collective-permute-start.5 = (bf16[1024,256]{1,0:T(8,128)(2,1)S(1)}, bf16[1024,256]{1,0:T(8,128)(2,1)S(1)}, u32[]{:S(2)}, u32[]{:S(2)}) collective-permute-start(bf16[1024,256]{1,0:T(8,128)(2,1)S(1)} %get-tuple-element.28.refs_2_.own), channel_id=1, source_target_pairs={{0,4},{4,8},{8,12},{1,5},{5,9},{9,13},{2,6},{6,10},{10,14},{3,7},{... | collective-permute-start | bytes 1572872 | tf_op jit(solution)/shard_map/ppermute | solution.py:188
  7.0 1.6 %collective-permute-start.7 = (bf16[1024,128]{1,0:T(8,128)(2,1)S(1)}, bf16[1024,128]{1,0:T(8,128)(2,1)S(1)}, u32[]{:S(2)}, u32[]{:S(2)}) collective-permute-start(bf16[1024,128]{1,0:T(8,128)(2,1)S(1)} %get-tuple-element.26.refs_0_.own), channel_id=1, source_target_pairs={{0,4},{4,8},{8,12},{12,0},{1,5},{5,9},{9,13},{13,1},{2,6},{6,10},{... | collective-permute-start | bytes 786440 | tf_op jit(solution)/shard_map/ppermute | solution.py:188
  8.6 1.6 %collective-permute-start.9 = (bf16[1024,128]{1,0:T(8,128)(2,1)S(1)}, bf16[1024,128]{1,0:T(8,128)(2,1)S(1)}, u32[]{:S(2)}, u32[]{:S(2)}) collective-permute-start(bf16[1024,128]{1,0:T(8,128)(2,1)S(1)} %get-tuple-element.27.refs_1_.own), channel_id=1, source_target_pairs={{0,4},{4,8},{8,12},{12,0},{1,5},{5,9},{9,13},{13,1},{2,6},{6,10},{... | collective-permute-start | bytes 786440 | tf_op jit(solution)/shard_map/ppermute | solution.py:188
  10.2 0.1 collective-permute-start.1
  10.3 0.0 copy-start
  10.3 1.0 %copy-done = bf16[256,1024]{1,0:T(8,128)(2,1)S(1)} copy-done((bf16[256,1024]{1,0:T(8,128)(2,1)S(1)}, bf16[256,1024]{1,0:T(8,128)(2,1)}, u32[]{:S(2)}) %copy-start) | copy-done | bytes 524312
  11.3 0.0 copy-start.4
  11.3 0.7 %copy-done.4 = s32[2]{0:T(128)S(1)} copy-done((s32[2]{0:T(128)S(1)}, s32[2]{0:T(128)}, u32[]{:S(2)}) %copy-start.4) | copy-done | bytes 32
  12.0 0.0 copy-start.5
  12.0 0.7 %copy-done.5 = f32[2]{0:T(128)S(1)} copy-done((f32[2]{0:T(128)S(1)}, f32[2]{0:T(128)}, u32[]{:S(2)}) %copy-start.5) | copy-done | bytes 32
  12.6 1.3 %spec.1 = (f32[256,640]{1,0:T(8,128)S(1)}, f32[256,1]{1,0:T(8,128)S(1)}, f32[2,128]{1,0:T(2,128)S(1)}) custom-call(s32[2]{0:T(128)S(1)} %copy-done.4, f32[2]{0:T(128)S(1)} %copy-done.5, bf16[256,1024]{1,0:T(8,128)(2,1)S(1)} %copy-done, bf16[1024,128]{1,0:T(8,128)(2,1)S(1)} %get-tuple-element.26.refs_0_.own, ...), custom_call_target="tpu_custom_call" | custom-call | flops 335544320 | bytes 2621440 | tf_op jit(solution)/shard_map/spec/pallas_call | solution.py:287
  13.9 15.6 %collective-permute-done.1.refs_1_ = f32[2,640]{1,0:T(2,128)S(1)} collective-permute-done((f32[2,640]{1,0:T(2,128)S(1)}, f32[2,640]{1,0:T(2,128)S(1)}, u32[]{:S(2)}, u32[]{:S(2)}) %collective-permute-start.1) | collective-permute-done | bytes 5152 | tf_op jit(solution)/shard_map/ppermute | solution.py:188
  29.5 0.1 shard_map.64
  29.6 3.5 %collective-permute-start.2 = (f32[2,640]{1,0:T(2,128)S(1)}, f32[2,640]{1,0:T(2,128)S(1)}, u32[]{:S(2)}, u32[]{:S(2)}) collective-permute-start(f32[2,640]{1,0:T(2,128)S(1)} %get-tuple-element.33), channel_id=1, source_target_pairs={{0,8},{4,12},{8,0},{12,4},{1,9},{5,13},{9,1},{13,5},{2,10},{6,14},... | collective-permute-start | bytes 15368 | tf_op jit(solution)/shard_map/ppermute | solution.py:188
  33.1 1.6 %collective-permute-done.2.refs_1_ = f32[2,640]{1,0:T(2,128)S(1)} collective-permute-done((f32[2,640]{1,0:T(2,128)S(1)}, f32[2,640]{1,0:T(2,128)S(1)}, u32[]{:S(2)}, u32[]{:S(2)}) %collective-permute-start.2) | collective-permute-done | bytes 5152 | tf_op jit(solution)/shard_map/ppermute | solution.py:188
  34.7 0.7 %shard_map.65 = (f32[2,640]{1,0:T(2,128)S(1)}, f32[1,640]{1,0:T(1,128)S(1)}, f32[1,640]{1,0:T(1,128)}) custom-call(f32[2,128]{1,0:T(2,128)S(1)} %get-tuple-element.31.refs_0_, f32[2,640]{1,0:T(2,128)S(1)} %collective-permute-done.2.refs_1_, f32[2,640]{1,0:T(2,128)S(1)} %get-tuple-element.32.refs_2_, f32[2,640]{1,0:T(2,128)S(1)} %get-tuple-element.34.refs_3_), custom_call_target="tpu_custom_call" | custom-call | flops 65536 | bytes 65536 | tf_op jit(solution)/shard_map/pallas_call | solution.py:196
  35.4 1.5 %collective-permute-start.3 = (f32[1,640]{1,0:T(1,128)S(1)}, f32[1,640]{1,0:T(1,128)S(1)}, u32[]{:S(2)}, u32[]{:S(2)}) collective-permute-start(f32[1,640]{1,0:T(1,128)S(1)} %get-tuple-element.36), channel_id=1, source_target_pairs={{0,2},{2,0},{1,3},{3,1},{4,6},{6,4},{5,7},{7,5},{8,10},{10,8},{9,1... | collective-permute-start | bytes 7688 | tf_op jit(solution)/shard_map/ppermute | solution.py:217
  36.9 2.1 %collective-permute-done.3.before.after = f32[1,640]{1,0:T(1,128)S(1)} collective-permute-done((f32[1,640]{1,0:T(1,128)S(1)}, f32[1,640]{1,0:T(1,128)S(1)}, u32[]{:S(2)}, u32[]{:S(2)}) %collective-permute-start.3) | collective-permute-done | bytes 2592 | tf_op jit(solution)/shard_map/ppermute | solution.py:217
  39.0 0.0 collective-permute-done.5.piece
  39.0 0.0 copy-done.1
  39.0 0.0 copy-done.2
  39.0 0.8 %shard_map.67 = (bf16[1024,256]{1,0:T(8,128)(2,1)S(1)}, bf16[1024,256]{1,0:T(8,128)(2,1)S(1)}) custom-call(bf16[1024,256]{1,0:T(8,128)(2,1)S(1)} %collective-permute-done.5.piece, bf16[1024,256]{1,0:T(8,128)(2,1)S(1)} %get-tuple-element.28.refs_2_.own, f32[256,640]{1,0:T(8,128)S(1)} %get-tuple-element.29.spec, f32[256,1]{1,0:T(8,128)S(1)} %get-tuple-element.30.gain, ...), custom_call_target="tpu_custom_call" | custom-call | flops 402653184 | bytes 2097152 | tf_op jit(solution)/shard_map/pallas_call | solution.py:317
  39.8 0.1 collective-permute-start.6
  39.9 3.8 %collective-permute-start = (bf16[1024,128]{1,0:T(8,128)(2,1)S(1)}, bf16[1024,128]{1,0:T(8,128)(2,1)S(1)}, u32[]{:S(2)}, u32[]{:S(2)}) collective-permute-start(bf16[1024,128]{1,0:T(8,128)(2,1)S(1)} %get-tuple-element.25.refs_3_.own), channel_id=1, source_target_pairs={{0,4},{4,8},{8,12},{1,5},{5,9},{9,13},{2,6},{6,10},{10,14},{3,7},{... | collective-permute-start | bytes 786440 | tf_op jit(solution)/shard_map/ppermute | solution.py:188
  43.7 0.0 collective-permute-done.7.piece
  43.7 0.8 %shard_map.68 = (bf16[1024,128]{1,0:T(8,128)(2,1)S(1)}, bf16[1024,128]{1,0:T(8,128)(2,1)S(1)}) custom-call(bf16[1024,128]{1,0:T(8,128)(2,1)S(1)} %collective-permute-done.7.piece, bf16[1024,128]{1,0:T(8,128)(2,1)S(1)} %get-tuple-element.26.refs_0_.own, f32[256,640]{1,0:T(8,128)S(1)} %get-tuple-element.29.spec, f32[256,1]{1,0:T(8,128)S(1)} %get-tuple-element.30.gain, ...), custom_call_target="tpu_custom_call" | custom-call | flops 201326592 | bytes 1048576 | tf_op jit(solution)/shard_map/pallas_call | solution.py:317
  44.5 0.3 collective-permute-start.8
  44.8 0.0 collective-permute-done.9.piece
  44.8 1.5 %shard_map.69 = (bf16[1024,128]{1,0:T(8,128)(2,1)S(1)}, bf16[1024,128]{1,0:T(8,128)(2,1)}) custom-call(bf16[1024,128]{1,0:T(8,128)(2,1)S(1)} %collective-permute-done.9.piece, bf16[1024,128]{1,0:T(8,128)(2,1)S(1)} %get-tuple-element.27.refs_1_.own, f32[256,640]{1,0:T(8,128)S(1)} %get-tuple-element.29.spec, f32[256,1]{1,0:T(8,128)S(1)} %get-tuple-element.30.gain, ...), custom_call_target="tpu_custom_call" | custom-call | flops 201326592 | bytes 1048576 | tf_op jit(solution)/shard_map/pallas_call | solution.py:317
  46.3 0.3 collective-permute-start.10
  46.6 3.3 %collective-permute-done.piece = bf16[1024,128]{1,0:T(8,128)(2,1)S(1)} collective-permute-done((bf16[1024,128]{1,0:T(8,128)(2,1)S(1)}, bf16[1024,128]{1,0:T(8,128)(2,1)S(1)}, u32[]{:S(2)}, u32[]{:S(2)}) %collective-permute-start) | collective-permute-done | bytes 262176 | tf_op jit(solution)/shard_map/ppermute | solution.py:188
  49.9 1.5 %shard_map.66 = (bf16[1024,128]{1,0:T(8,128)(2,1)S(1)}, bf16[1024,128]{1,0:T(8,128)(2,1)}) custom-call(bf16[1024,128]{1,0:T(8,128)(2,1)S(1)} %collective-permute-done.piece, bf16[1024,128]{1,0:T(8,128)(2,1)S(1)} %get-tuple-element.25.refs_3_.own, f32[256,640]{1,0:T(8,128)S(1)} %get-tuple-element.29.spec, f32[256,1]{1,0:T(8,128)S(1)} %get-tuple-element.30.gain, ...), custom_call_target="tpu_custom_call" | custom-call | flops 201326592 | bytes 1048576 | tf_op jit(solution)/shard_map/pallas_call | solution.py:317
  51.4 0.0 collective-permute-start.4
  52.1 0.5 taps.1.refs_4_.refs_2_
  52.6 0.0 collective-permute-done.8.refs_1_
  52.6 0.0 collective-permute-done.10.refs_3_
  52.6 2.9 %shard_map.70.refs_3_ = f32[1024,1280]{1,0:T(8,128)S(1)} custom-call(bf16[1024,128]{1,0:T(8,128)(2,1)S(1)} %get-tuple-element.41.refs_0_, bf16[1024,128]{1,0:T(8,128)(2,1)S(1)} %collective-permute-done.8.refs_1_, bf16[1024,128]{1,0:T(8,128)(2,1)S(1)} %get-tuple-element.43.refs_2_, bf16[1024,128]{1,0:T(8,128)(2,1)S(1)} %collective-permute-done.10.refs_3_, ...), custom_call_target="tpu_custom_call" | custom-call | flops 1342177280 | bytes 10485760 | tf_op jit(solution)/shard_map/pallas_call | solution.py:346
  55.5 0.0 collective-permute-done.6.refs_1_
  55.5 1.8 %shard_map.71.refs_3_ = f32[1024,1280]{1,0:T(8,128)S(1)} custom-call(bf16[1024,256]{1,0:T(8,128)(2,1)S(1)} %get-tuple-element.39.refs_0_, bf16[1024,256]{1,0:T(8,128)(2,1)S(1)} %collective-permute-done.6.refs_1_, bf16[256,2560]{1,0:T(8,128)(2,1)S(1)} %taps.1.refs_4_.refs_2_, f32[1024,1280]{1,0:T(8,128)S(1)} %shard_map.70.refs_3_), custom_call_target="tpu_custom_call", output_to_operand_aliasing={{}: (3, {})} | custom-call | flops 1342177280 | bytes 10485760 | tf_op jit(solution)/shard_map/pallas_call | solution.py:346
  57.3 0.0 collective-permute-done.4.refs_1_
  57.3 3.3 %finish.1 = bf16[512,2,1280]{2,1,0:T(2,128)(2,1)} custom-call(bf16[1024,128]{1,0:T(8,128)(2,1)S(1)} %get-tuple-element.37.refs_0_, bf16[1024,128]{1,0:T(8,128)(2,1)S(1)} %collective-permute-done.4.refs_1_, bf16[256,2560]{1,0:T(8,128)(2,1)S(1)} %taps.1.refs_4_.refs_2_, f32[1024,1280]{1,0:T(8,128)S(1)} %shard_map.71.refs_3_), custom_call_target="tpu_custom_call" | custom-call | flops 671088640 | bytes 10485760 | tf_op jit(solution)/shard_map/finish/pallas_call | solution.py:337
  (1 shorter events, 0.0 us)
Async XLA Ops:
  0.0 39.0 %copy-start.1 = (bf16[256,1024]{1,0:T(8,128)(2,1)S(1)}, bf16[256,1024]{1,0:T(8,128)(2,1)}, u32[]{:S(2)}) copy-start(bf16[256,1024]{1,0:T(8,128)(2,1)} %constant.25.clone.table) | copy-start | bytes 1572868
  0.0 39.0 %copy-start.2 = (bf16[1024,256]{1,0:T(8,128)(2,1)S(1)}, bf16[1024,256]{1,0:T(8,128)(2,1)}, u32[]{:S(2)}) copy-start(bf16[1024,256]{1,0:T(8,128)(2,1)} %constant.26.clone.turned) | copy-start | bytes 1572868
  0.0 1.4 %copy-start.3 = (bf16[512,2,640]{2,1,0:T(2,128)(2,1)S(1)}, bf16[512,2,640]{2,1,0:T(2,128)(2,1)}, u32[]{:S(2)}) copy-start(bf16[512,2,640]{2,1,0:T(2,128)(2,1)} %raw.1) | copy-start | bytes 3932164
  2.1 36.9 %collective-permute-start.5 = (bf16[1024,256]{1,0:T(8,128)(2,1)S(1)}, bf16[1024,256]{1,0:T(8,128)(2,1)S(1)}, u32[]{:S(2)}, u32[]{:S(2)}) collective-permute-start(bf16[1024,256]{1,0:T(8,128)(2,1)S(1)} %get-tuple-element.28.refs_2_.own), channel_id=1, source_target_pairs={{0,4},{4,8},{8,12},{1,5},{5,9},{9,13},{2,6},{6,10},{10,14},{3,7},{... | collective-permute-start | bytes 1572872 | tf_op jit(solution)/shard_map/ppermute | solution.py:188
  7.0 36.7 %collective-permute-start.7 = (bf16[1024,128]{1,0:T(8,128)(2,1)S(1)}, bf16[1024,128]{1,0:T(8,128)(2,1)S(1)}, u32[]{:S(2)}, u32[]{:S(2)}) collective-permute-start(bf16[1024,128]{1,0:T(8,128)(2,1)S(1)} %get-tuple-element.26.refs_0_.own), channel_id=1, source_target_pairs={{0,4},{4,8},{8,12},{12,0},{1,5},{5,9},{9,13},{13,1},{2,6},{6,10},{... | collective-permute-start | bytes 786440 | tf_op jit(solution)/shard_map/ppermute | solution.py:188
  8.6 36.2 %collective-permute-start.9 = (bf16[1024,128]{1,0:T(8,128)(2,1)S(1)}, bf16[1024,128]{1,0:T(8,128)(2,1)S(1)}, u32[]{:S(2)}, u32[]{:S(2)}) collective-permute-start(bf16[1024,128]{1,0:T(8,128)(2,1)S(1)} %get-tuple-element.27.refs_1_.own), channel_id=1, source_target_pairs={{0,4},{4,8},{8,12},{12,0},{1,5},{5,9},{9,13},{13,1},{2,6},{6,10},{... | collective-permute-start | bytes 786440 | tf_op jit(solution)/shard_map/ppermute | solution.py:188
  10.2 19.3 %collective-permute-start.1 = (f32[2,640]{1,0:T(2,128)S(1)}, f32[2,640]{1,0:T(2,128)S(1)}, u32[]{:S(2)}, u32[]{:S(2)}) collective-permute-start(f32[2,640]{1,0:T(2,128)S(1)} %get-tuple-element.32.refs_2_), channel_id=1, source_target_pairs={{0,4},{4,8},{8,12},{12,0},{1,5},{5,9},{9,13},{13,1},{2,6},{6,10},{... | collective-permute-start | bytes 15368 | tf_op jit(solution)/shard_map/ppermute | solution.py:188
  10.3 1.0 %copy-start = (bf16[256,1024]{1,0:T(8,128)(2,1)S(1)}, bf16[256,1024]{1,0:T(8,128)(2,1)}, u32[]{:S(2)}) copy-start(bf16[256,1024]{1,0:T(8,128)(2,1)} %constant.25.clone.table) | copy-start | bytes 1572868
  11.3 0.7 %copy-start.4 = (s32[2]{0:T(128)S(1)}, s32[2]{0:T(128)}, u32[]{:S(2)}) copy-start(s32[2]{0:T(128)} %bands.1) | copy-start | bytes 28
  12.0 0.7 %copy-start.5 = (f32[2]{0:T(128)S(1)}, f32[2]{0:T(128)}, u32[]{:S(2)}) copy-start(f32[2]{0:T(128)} %memory.1) | copy-start | bytes 28
  29.6 5.1 %collective-permute-start.2 = (f32[2,640]{1,0:T(2,128)S(1)}, f32[2,640]{1,0:T(2,128)S(1)}, u32[]{:S(2)}, u32[]{:S(2)}) collective-permute-start(f32[2,640]{1,0:T(2,128)S(1)} %get-tuple-element.33), channel_id=1, source_target_pairs={{0,8},{4,12},{8,0},{12,4},{1,9},{5,13},{9,1},{13,5},{2,10},{6,14},... | collective-permute-start | bytes 15368 | tf_op jit(solution)/shard_map/ppermute | solution.py:188
  35.4 3.6 %collective-permute-start.3 = (f32[1,640]{1,0:T(1,128)S(1)}, f32[1,640]{1,0:T(1,128)S(1)}, u32[]{:S(2)}, u32[]{:S(2)}) collective-permute-start(f32[1,640]{1,0:T(1,128)S(1)} %get-tuple-element.36), channel_id=1, source_target_pairs={{0,2},{2,0},{1,3},{3,1},{4,6},{6,4},{5,7},{7,5},{8,10},{10,8},{9,1... | collective-permute-start | bytes 7688 | tf_op jit(solution)/shard_map/ppermute | solution.py:217
  39.8 15.7 %collective-permute-start.6 = (bf16[1024,256]{1,0:T(8,128)(2,1)S(1)}, bf16[1024,256]{1,0:T(8,128)(2,1)S(1)}, u32[]{:S(2)}, u32[]{:S(2)}) collective-permute-start(bf16[1024,256]{1,0:T(8,128)(2,1)S(1)} %get-tuple-element.40), channel_id=1, source_target_pairs={{0,1},{1,0},{2,3},{3,2},{4,5},{5,4},{6,7},{7,6},{8,9},{9,8},{10,11... | collective-permute-start | bytes 1572872 | tf_op jit(solution)/shard_map/ppermute | solution.py:325
  39.9 10.0 %collective-permute-start = (bf16[1024,128]{1,0:T(8,128)(2,1)S(1)}, bf16[1024,128]{1,0:T(8,128)(2,1)S(1)}, u32[]{:S(2)}, u32[]{:S(2)}) collective-permute-start(bf16[1024,128]{1,0:T(8,128)(2,1)S(1)} %get-tuple-element.25.refs_3_.own), channel_id=1, source_target_pairs={{0,4},{4,8},{8,12},{1,5},{5,9},{9,13},{2,6},{6,10},{10,14},{3,7},{... | collective-permute-start | bytes 786440 | tf_op jit(solution)/shard_map/ppermute | solution.py:188
  44.5 8.1 %collective-permute-start.8 = (bf16[1024,128]{1,0:T(8,128)(2,1)S(1)}, bf16[1024,128]{1,0:T(8,128)(2,1)S(1)}, u32[]{:S(2)}, u32[]{:S(2)}) collective-permute-start(bf16[1024,128]{1,0:T(8,128)(2,1)S(1)} %get-tuple-element.42), channel_id=1, source_target_pairs={{0,1},{1,0},{2,3},{3,2},{4,5},{5,4},{6,7},{7,6},{8,9},{9,8},{10,11... | collective-permute-start | bytes 786440 | tf_op jit(solution)/shard_map/ppermute | solution.py:325
  46.3 6.3 %collective-permute-start.10 = (bf16[1024,128]{1,0:T(8,128)(2,1)}, bf16[1024,128]{1,0:T(8,128)(2,1)S(1)}, u32[]{:S(2)}, u32[]{:S(2)}) collective-permute-start(bf16[1024,128]{1,0:T(8,128)(2,1)} %get-tuple-element.44), channel_id=1, source_target_pairs={{0,1},{1,0},{2,3},{3,2},{4,5},{5,4},{6,7},{7,6},{8,9},{9,8},{10,11... | collective-permute-start | bytes 786440 | tf_op jit(solution)/shard_map/ppermute | solution.py:325
  51.4 5.9 %collective-permute-start.4 = (bf16[1024,128]{1,0:T(8,128)(2,1)}, bf16[1024,128]{1,0:T(8,128)(2,1)S(1)}, u32[]{:S(2)}, u32[]{:S(2)}) collective-permute-start(bf16[1024,128]{1,0:T(8,128)(2,1)} %get-tuple-element.38), channel_id=1, source_target_pairs={{0,1},{1,0},{2,3},{3,2},{4,5},{5,4},{6,7},{7,6},{8,9},{9,8},{10,11... | collective-permute-start | bytes 786440 | tf_op jit(solution)/shard_map/ppermute | solution.py:325

commit v2 on v1

--- a/solution.py
+++ b/solution.py
@@ -13,12 +13,12 @@
 WAVES = 2 * BAND_FREQS
 TAP_ROWS = 256
 PIECES = ((0, 128), (128, 256), (256, 512), (512, 640))
-GROUPS = ((0, 1), (2,), (3,))
-WRAPS = 2
+STAGES = ((0, 1), (2,), (3,))
+WRAPS = (0, 1)
 
 VMEM = pl.BlockSpec(memory_space=pltpu.VMEM)
 SMEM = pl.BlockSpec(memory_space=pltpu.SMEM)
-HBM = pl.BlockSpec(memory_space=pltpu.HBM)
+ANY = pl.BlockSpec(memory_space=pl.ANY)
 F32 = jnp.float32
 BF16 = jnp.bfloat16
 
@@ -44,15 +44,43 @@
     return lax.broadcasted_iota(jnp.int32, shape, dim) % rows
 
 
+def fetch(raw, buffer, sems, columns):
+    count = sems.shape[0]
+    block = raw.shape[0] // count
+    parts = [pl.ds(i * block, block) for i in range(count)]
+    copies = [
+        pltpu.make_async_copy(raw.at[p, :, columns], buffer.at[p], sems.at[i])
+        for i, p in enumerate(parts)
+    ]
+    for copy in copies:
+        copy.start()
+    return copies
+
+
+def head_kernel(raw, out, buffer, sems):
+    half, rows, cols = buffer.shape
+    block = half // sems.shape[0]
+    for i, copy in enumerate(fetch(raw, buffer, sems, pl.ds(*PIECES[0]))):
+        copy.wait()
+        x = buffer[i * block : (i + 1) * block].reshape(block * rows, cols)
+        out[i * block * rows : (i + 1) * block * rows, :] = x
+
+
 def split_kernel(raw, *refs):
-    *pieces, sums = refs
-    half, rows, cols = raw.shape
-    x = raw[...].reshape(half * rows, cols)
-    for (lo, hi), out in zip(PIECES, pieces):
-        out[...] = x[:, lo:hi]
-    shape = (8, half * rows)
+    *pieces, sums, buffer, sems = refs
+    half, rows, cols = buffer.shape
+    block = half // sems.shape[0]
+    shape = (8, block * rows)
     pick = pattern(shape, 1, rows) == lax.broadcasted_iota(jnp.int32, shape, 0)
-    total = jnp.dot(pick.astype(F32).astype(BF16), x, preferred_element_type=F32)
+    pick = pick.astype(F32).astype(BF16)
+    total = None
+    for i, copy in enumerate(fetch(raw, buffer, sems, pl.ds(0, cols))):
+        copy.wait()
+        x = buffer[i * block : (i + 1) * block].reshape(block * rows, cols)
+        for (lo, hi), out in zip(PIECES[1:], pieces):
+            out[i * block * rows : (i + 1) * block * rows, :] = x[:, lo:hi]
+        part = jnp.dot(pick, x, preferred_element_type=F32)
+        total = part if total is None else total + part
     sums[...] = total[:rows, :]
 
 
@@ -102,11 +130,22 @@
     out[...] = total
 
 
-def damp_kernel(lo, rows, piece, own, spec, gain, table, turned, cycle, keep, send, old):
-    count, cols = piece.shape
+def damp_kernel(lo, rows, parts, *refs):
+    pieces, owns = refs[:parts], refs[parts : 2 * parts]
+    spec, gain, table, turned, cycle, keep, send, old, own = refs[2 * parts :]
+    count, cols = old.shape
     waves = turned.shape[1]
     core = lax.axis_index("col")
-    old[...] = jnp.where(lax.axis_index("tm") > 0, piece[...], jnp.zeros_like(piece))
+    at = 0
+    for piece, mine in zip(pieces, owns):
+        place = slice(at, at + piece.shape[1])
+        at = place.stop
+        older = piece[...]
+        old[:, place] = jnp.where(lax.axis_index("tm") > 0, older, jnp.zeros_like(older))
+        if parts > 1:
+            own[:, place] = mine[...]
+    if parts == 1:
+        own = owns[0]
     total = jnp.dot(table[...], old[...], preferred_element_type=F32)
     total = (total + spec[:, lo : lo + cols]) * gain[...]
     index = lax.broadcasted_iota(jnp.int32, (waves, 1), 0)
@@ -276,14 +315,29 @@
     n = len(PIECES)
 
     shapes = [jax.ShapeDtypeStruct((count, hi - lo), BF16) for lo, hi in PIECES]
+    turns = pltpu.with_memory_space_constraint(turns, pltpu.HBM)
+    head = pl.pallas_call(
+        head_kernel,
+        out_shape=shapes[0],
+        in_specs=[ANY],
+        out_specs=VMEM,
+        scratch_shapes=[
+            pltpu.VMEM((half, rows, PIECES[0][1]), BF16),
+            pltpu.SemaphoreType.DMA((4,)),
+        ],
+        name="head",
+        **params(count * cols, count * cols),
+    )(turns)
     *pieces, sums = pl.pallas_call(
         split_kernel,
-        out_shape=(*shapes, jax.ShapeDtypeStruct((rows, cols), F32)),
-        in_specs=[VMEM],
-        out_specs=[VMEM] * (n + 1),
+        out_shape=(*shapes[1:], jax.ShapeDtypeStruct((rows, cols), F32)),
+        in_specs=[ANY],
+        out_specs=[VMEM] * n,
+        scratch_shapes=[pltpu.VMEM(turns.shape, BF16), pltpu.SemaphoreType.DMA((4,))],
         name="split",
         **params(16 * count * cols, 4 * count * cols),
     )(turns)
+    pieces = [head, *pieces]
     spec, gain, scales = pl.pallas_call(
         functools.partial(spec_kernel, rows, distances, angles),
         out_shape=(
@@ -300,7 +354,7 @@
     cycle = cycle_of(sums, first_lag, scales)
     olds = []
     for i, x in enumerate(pieces):
-        olds.append(along_tm(x, 1, wrap=i < WRAPS))
+        olds.append(along_tm(x, 1, wrap=i in WRAPS))
     offset = (shifts + core.reshape(1) * cols) % width
     taps = pl.pallas_call(
         tap_kernel,
@@ -312,22 +366,25 @@
     )(offset)
 
     def damp(i):
-        lo, hi = PIECES[i]
+        stage = STAGES[i]
+        lo, hi = PIECES[stage[0]][0], PIECES[stage[-1]][1]
         shape = jax.ShapeDtypeStruct((count, hi - lo), BF16)
+        inputs = [olds[j] for j in stage] + [pieces[j] for j in stage]
+        inputs += [spec, gain, table, turned, cycle]
+        spare = (count, hi - lo) if len(stage) > 1 else (16, 128)
         keep, send = pl.pallas_call(
-            functools.partial(damp_kernel, lo, rows),
+            functools.partial(damp_kernel, lo, rows, len(stage)),
             out_shape=(shape, shape),
-            in_specs=[VMEM] * 7,
+            in_specs=[VMEM] * len(inputs),
             out_specs=[VMEM] * 2,
-            scratch_shapes=[pltpu.VMEM((count, hi - lo), BF16)],
+            scratch_shapes=[pltpu.VMEM((count, hi - lo), BF16), pltpu.VMEM(spare, BF16)],
             **params(6 * waves * count * (hi - lo), 8 * count * (hi - lo)),
-        )(olds[i], pieces[i], spec, gain, table, turned, cycle)
+        )(*inputs)
         recv = lax.ppermute(send, "col", [(0, 1), (1, 0)])
         return (lo, cols + lo), (keep, recv)
 
-    def accumulate(parts, acc, last):
-        starts = sum((p[0] for p in parts), ())
-        data = sum((p[1] for p in parts), ())
+    def accumulate(part, acc, last):
+        starts, data = part
         inputs = [*data, taps] + ([] if acc is None else [acc])
         kernel = functools.partial(filter_kernel, starts, acc is None, last, rows)
         depth = sum(x.shape[1] for x in data)
@@ -352,10 +409,9 @@
             **cost,
         )(*inputs)
 
-    parts = [damp(i) for i in range(n)]
     acc = None
-    for i, group in enumerate(GROUPS):
-        acc = accumulate([parts[j] for j in group], acc, i == len(GROUPS) - 1)
+    for i in range(len(STAGES)):
+        acc = accumulate(damp(i), acc, i == len(STAGES) - 1)
     return acc
 
 

time: 61 us -> 60.8 us (level)
  waiting for transfers between devices: 22.6 us -> 26.4 us
  local copies, waits for them, and re-layouts: 3.76 us -> 0.01 us
    ppermute x6, waiting for transfers between devices: 20.5 us -> 24.2 us  [along_tm(): return lax.ppermute(x, 'tm', route)]
    unnamed x12 -> x8, local copies, waits for them, and re-layouts: 3.76 us -> 0.01 us
    pallas_call x2, Pallas kernels: 4.64 us -> 3.31 us  [accumulate(): pl.pallas_call(kernel, out_shape=jax.ShapeDtypeStruct((count, width), F32...]
    pallas_call x5, Pallas kernels: 5.23 us -> 6.37 us  [the longest x3 3.33 us: damp(): pl.pallas_call(functools.partial(damp_kernel, lo, rows, len(stage)), out_...]
  transfers between devices with their start and end apart: 11 -> 10, of which waited for: 4 -> 4; matrix products, arithmetic and copies ran while one was open for 0% -> 0% of each run, Pallas kernels for 19% -> 17%
where the time goes in v2:
time: 60.8 us; the launch traced here: 60.4 us
  waiting for transfers between devices  26.4 us (43%)
  starting transfers between devices  17.7 us (29%)
  Pallas kernels  15.5 us (25%)
  between operations  0.82 us (1%)
    ppermute x6, waiting for transfers between devices, along_tm(): return lax.ppermute(x, 'tm', route)  24.2 us
    ppermute x6, starting transfers between devices, along_tm(): return lax.ppermute(x, 'tm', route)  15.6 us
    pallas_call x1, Pallas kernels, accumulate(): pl.pallas_call(kernel, grid=(count // 256,), out_shape=jax.ShapeDtypeStru...  3.34 us
    pallas_call x3, Pallas kernels, damp(): pl.pallas_call(functools.partial(damp_kernel, lo, rows, len(stage)), out_...  3.33 us
    pallas_call x2, Pallas kernels, accumulate(): pl.pallas_call(kernel, out_shape=jax.ShapeDtypeStruct((count, width), F32...  3.31 us
    ppermute x1, waiting for transfers between devices, row_neighbours(): before = lax.ppermute(last, 'cuts', up)  2.1 us
    pallas_call x1, Pallas kernels, local(): pl.pallas_call(split_kernel, out_shape=(*shapes[1:], jax.ShapeDtypeStruct...  2.02 us
    ppermute x1, starting transfers between devices, row_neighbours(): before = lax.ppermute(last, 'cuts', up)  1.49 us
  transfers between devices with their start and end apart: 10, of which 4 were waited for; matrix products, arithmetic and copies ran while one was open for 0% of the time, Pallas kernels for 17%

profile of v2, /device:TPU:0, one launch (start us, length us, event | category | flops | bytes accessed | tf_op | source)
XLA Modules:
  0.0 60.4 jit_solution(1829389333261390812)
XLA Ops:
  0.0 0.0 copy-start
  0.0 0.0 copy-start.1
  0.0 0.0 copy-start.3
  0.0 0.0 copy-start.2
  0.0 2.0 %split.1 = (bf16[1024,128]{1,0:T(8,128)(2,1)S(1)}, bf16[1024,256]{1,0:T(8,128)(2,1)S(1)}, bf16[1024,128]{1,0:T(8,128)(2,1)S(1)}, f32[2,640]{1,0:T(2,128)S(1)}) custom-call(bf16[512,2,640]{2,1,0:T(2,128)(2,1)} %raw.3), custom_call_target="tpu_custom_call" | custom-call | flops 10485760 | bytes 2621440 | tf_op jit(solution)/shard_map/split/pallas_call | solution.py:331
  2.0 5.0 %collective-permute-start.5 = (bf16[1024,256]{1,0:T(8,128)(2,1)S(1)}, bf16[1024,256]{1,0:T(8,128)(2,1)S(1)}, u32[]{:S(2)}, u32[]{:S(2)}) collective-permute-start(bf16[1024,256]{1,0:T(8,128)(2,1)S(1)} %get-tuple-element.24.refs_2_.refs_1_), channel_id=1, source_target_pairs={{0,4},{4,8},{8,12},{1,5},{5,9},{9,13},{2,6},{6,10},{10,14},{3,7},{... | collective-permute-start | bytes 1572872 | tf_op jit(solution)/shard_map/ppermute | solution.py:227
  7.0 1.0 %head.1.refs_0_.refs_2_ = bf16[1024,128]{1,0:T(8,128)(2,1)S(1)} custom-call(bf16[512,2,640]{2,1,0:T(2,128)(2,1)} %raw.3), custom_call_target="tpu_custom_call" | custom-call | flops 655360 | bytes 655360 | tf_op jit(solution)/shard_map/head/pallas_call | solution.py:319
  8.1 1.6 %collective-permute-start.7 = (bf16[1024,128]{1,0:T(8,128)(2,1)S(1)}, bf16[1024,128]{1,0:T(8,128)(2,1)S(1)}, u32[]{:S(2)}, u32[]{:S(2)}) collective-permute-start(bf16[1024,128]{1,0:T(8,128)(2,1)S(1)} %head.1.refs_0_.refs_2_), channel_id=1, source_target_pairs={{0,4},{4,8},{8,12},{12,0},{1,5},{5,9},{9,13},{13,1},{2,6},{6,10},{... | collective-permute-start | bytes 786440 | tf_op jit(solution)/shard_map/ppermute | solution.py:227
  9.7 1.6 %collective-permute-start.8 = (bf16[1024,128]{1,0:T(8,128)(2,1)S(1)}, bf16[1024,128]{1,0:T(8,128)(2,1)S(1)}, u32[]{:S(2)}, u32[]{:S(2)}) collective-permute-start(bf16[1024,128]{1,0:T(8,128)(2,1)S(1)} %get-tuple-element.23.refs_1_.refs_3_), channel_id=1, source_target_pairs={{0,4},{4,8},{8,12},{12,0},{1,5},{5,9},{9,13},{13,1},{2,6},{6,10},{... | collective-permute-start | bytes 786440 | tf_op jit(solution)/shard_map/ppermute | solution.py:227
  11.3 0.1 collective-permute-start.1
  11.3 0.0 copy-done
  11.3 0.0 copy-done.3
  11.3 0.0 copy-done.2
  11.3 1.3 %spec.1 = (f32[256,640]{1,0:T(8,128)S(1)}, f32[256,1]{1,0:T(8,128)S(1)}, f32[2,128]{1,0:T(2,128)S(1)}) custom-call(s32[2]{0:T(128)S(1)} %copy-done.2, f32[2]{0:T(128)S(1)} %copy-done.3, bf16[256,1024]{1,0:T(8,128)(2,1)S(1)} %copy-done, bf16[1024,128]{1,0:T(8,128)(2,1)S(1)} %head.1.refs_0_.refs_2_, bf16[1024,128]{1,0:T(8,128)(2,1)S(1)} %get-tuple-element.23.refs_1_.refs_3_, ...), custom_call_target="tpu_custom_call" | custom-call | flops 335544320 | bytes 2621440 | tf_op jit(solution)/shard_map/spec/pallas_call | solution.py:341
  12.6 16.9 %collective-permute-done.1.refs_1_ = f32[2,640]{1,0:T(2,128)S(1)} collective-permute-done((f32[2,640]{1,0:T(2,128)S(1)}, f32[2,640]{1,0:T(2,128)S(1)}, u32[]{:S(2)}, u32[]{:S(2)}) %collective-permute-start.1) | collective-permute-done | bytes 5152 | tf_op jit(solution)/shard_map/ppermute | solution.py:227
  29.5 0.1 shard_map.64
  29.6 3.5 %collective-permute-start.2 = (f32[2,640]{1,0:T(2,128)S(1)}, f32[2,640]{1,0:T(2,128)S(1)}, u32[]{:S(2)}, u32[]{:S(2)}) collective-permute-start(f32[2,640]{1,0:T(2,128)S(1)} %get-tuple-element.29), channel_id=1, source_target_pairs={{0,8},{4,12},{8,0},{12,4},{1,9},{5,13},{9,1},{13,5},{2,10},{6,14},... | collective-permute-start | bytes 15368 | tf_op jit(solution)/shard_map/ppermute | solution.py:227
  33.1 1.6 %collective-permute-done.2.refs_1_ = f32[2,640]{1,0:T(2,128)S(1)} collective-permute-done((f32[2,640]{1,0:T(2,128)S(1)}, f32[2,640]{1,0:T(2,128)S(1)}, u32[]{:S(2)}, u32[]{:S(2)}) %collective-permute-start.2) | collective-permute-done | bytes 5152 | tf_op jit(solution)/shard_map/ppermute | solution.py:227
  34.7 0.7 %shard_map.65 = (f32[2,640]{1,0:T(2,128)S(1)}, f32[1,640]{1,0:T(1,128)S(1)}, f32[1,640]{1,0:T(1,128)}) custom-call(f32[2,128]{1,0:T(2,128)S(1)} %get-tuple-element.27.refs_0_, f32[2,640]{1,0:T(2,128)S(1)} %collective-permute-done.2.refs_1_, f32[2,640]{1,0:T(2,128)S(1)} %get-tuple-element.28.refs_2_, f32[2,640]{1,0:T(2,128)S(1)} %get-tuple-element.30.refs_3_), custom_call_target="tpu_custom_call" | custom-call | flops 65536 | bytes 65536 | tf_op jit(solution)/shard_map/pallas_call | solution.py:235
  35.4 1.5 %collective-permute-start.3 = (f32[1,640]{1,0:T(1,128)S(1)}, f32[1,640]{1,0:T(1,128)S(1)}, u32[]{:S(2)}, u32[]{:S(2)}) collective-permute-start(f32[1,640]{1,0:T(1,128)S(1)} %get-tuple-element.32), channel_id=1, source_target_pairs={{0,2},{2,0},{1,3},{3,1},{4,6},{6,4},{5,7},{7,5},{8,10},{10,8},{9,1... | collective-permute-start | bytes 7688 | tf_op jit(solution)/shard_map/ppermute | solution.py:256
  36.9 2.1 %collective-permute-done.3.before.after = f32[1,640]{1,0:T(1,128)S(1)} collective-permute-done((f32[1,640]{1,0:T(1,128)S(1)}, f32[1,640]{1,0:T(1,128)S(1)}, u32[]{:S(2)}, u32[]{:S(2)}) %collective-permute-start.3) | collective-permute-done | bytes 2592 | tf_op jit(solution)/shard_map/ppermute | solution.py:256
  39.0 0.0 collective-permute-done.7.refs_0_
  39.0 0.0 collective-permute-done.8.refs_1_
  39.0 0.0 copy-done.1
  39.0 1.0 %shard_map.68 = (bf16[1024,256]{1,0:T(8,128)(2,1)S(1)}, bf16[1024,256]{1,0:T(8,128)(2,1)S(1)}) custom-call(bf16[1024,128]{1,0:T(8,128)(2,1)S(1)} %collective-permute-done.7.refs_0_, bf16[1024,128]{1,0:T(8,128)(2,1)S(1)} %collective-permute-done.8.refs_1_, bf16[1024,128]{1,0:T(8,128)(2,1)S(1)} %head.1.refs_0_.refs_2_, ...), custom_call_target="tpu_custom_call" | custom-call | flops 402653184 | bytes 2097152 | tf_op jit(solution)/shard_map/pallas_call | solution.py:375
  40.0 0.1 collective-permute-start.9
  40.0 0.0 collective-permute-done.5.refs_0_
  40.1 1.6 %shard_map.67 = (bf16[1024,256]{1,0:T(8,128)(2,1)S(1)}, bf16[1024,256]{1,0:T(8,128)(2,1)}) custom-call(bf16[1024,256]{1,0:T(8,128)(2,1)S(1)} %collective-permute-done.5.refs_0_, bf16[1024,256]{1,0:T(8,128)(2,1)S(1)} %get-tuple-element.24.refs_2_.refs_1_, f32[256,640]{1,0:T(8,128)S(1)} %get-tuple-element.25.refs_2_.refs_4_, ...), custom_call_target="tpu_custom_call" | custom-call | flops 402653184 | bytes 2097152 | tf_op jit(solution)/shard_map/pallas_call | solution.py:375
  41.7 0.5 collective-permute-start.6
  42.1 3.8 %collective-permute-start = (bf16[1024,128]{1,0:T(8,128)(2,1)S(1)}, bf16[1024,128]{1,0:T(8,128)(2,1)S(1)}, u32[]{:S(2)}, u32[]{:S(2)}) collective-permute-start(bf16[1024,128]{1,0:T(8,128)(2,1)S(1)} %get-tuple-element.22.refs_3_.refs_1_), channel_id=1, source_target_pairs={{0,4},{4,8},{8,12},{1,5},{5,9},{9,13},{2,6},{6,10},{10,14},{3,7},{... | collective-permute-start | bytes 786440 | tf_op jit(solution)/shard_map/ppermute | solution.py:227
  46.0 5.7 %collective-permute-done.refs_0_ = bf16[1024,128]{1,0:T(8,128)(2,1)S(1)} collective-permute-done((bf16[1024,128]{1,0:T(8,128)(2,1)S(1)}, bf16[1024,128]{1,0:T(8,128)(2,1)S(1)}, u32[]{:S(2)}, u32[]{:S(2)}) %collective-permute-start) | collective-permute-done | bytes 262176 | tf_op jit(solution)/shard_map/ppermute | solution.py:227
  51.7 0.8 %shard_map.66 = (bf16[1024,128]{1,0:T(8,128)(2,1)S(1)}, bf16[1024,128]{1,0:T(8,128)(2,1)S(1)}) custom-call(bf16[1024,128]{1,0:T(8,128)(2,1)S(1)} %collective-permute-done.refs_0_, bf16[1024,128]{1,0:T(8,128)(2,1)S(1)} %get-tuple-element.22.refs_3_.refs_1_, f32[256,640]{1,0:T(8,128)S(1)} %get-tuple-element.25.refs_2_.refs_4_, ...), custom_call_target="tpu_custom_call" | custom-call | flops 201326592 | bytes 1048576 | tf_op jit(solution)/shard_map/pallas_call | solution.py:375
  52.5 0.1 collective-permute-start.4
  53.2 0.5 taps.1.refs_2_
  53.7 0.0 collective-permute-done.9.refs_1_
  53.7 1.5 %shard_map.69.refs_3_ = f32[1024,1280]{1,0:T(8,128)S(1)} custom-call(bf16[1024,256]{1,0:T(8,128)(2,1)S(1)} %get-tuple-element.37.refs_0_, bf16[1024,256]{1,0:T(8,128)(2,1)S(1)} %collective-permute-done.9.refs_1_, bf16[256,2560]{1,0:T(8,128)(2,1)S(1)} %taps.1.refs_2_), custom_call_target="tpu_custom_call" | custom-call | flops 1342177280 | bytes 10485760 | tf_op jit(solution)/shard_map/pallas_call | solution.py:403
  55.3 0.0 collective-permute-done.6.refs_1_
  55.3 1.8 %shard_map.70.refs_3_ = f32[1024,1280]{1,0:T(8,128)S(1)} custom-call(bf16[1024,256]{1,0:T(8,128)(2,1)S(1)} %get-tuple-element.35.refs_0_, bf16[1024,256]{1,0:T(8,128)(2,1)S(1)} %collective-permute-done.6.refs_1_, bf16[256,2560]{1,0:T(8,128)(2,1)S(1)} %taps.1.refs_2_, f32[1024,1280]{1,0:T(8,128)S(1)} %shard_map.69.refs_3_), custom_call_target="tpu_custom_call", output_to_operand_aliasing={{}: (3, {})} | custom-call | flops 1342177280 | bytes 10485760 | tf_op jit(solution)/shard_map/pallas_call | solution.py:403
  57.1 0.0 collective-permute-done.4.refs_1_
  57.1 3.3 %finish.1 = bf16[512,2,1280]{2,1,0:T(2,128)(2,1)} custom-call(bf16[1024,128]{1,0:T(8,128)(2,1)S(1)} %get-tuple-element.33.refs_0_, bf16[1024,128]{1,0:T(8,128)(2,1)S(1)} %collective-permute-done.4.refs_1_, bf16[256,2560]{1,0:T(8,128)(2,1)S(1)} %taps.1.refs_2_, f32[1024,1280]{1,0:T(8,128)S(1)} %shard_map.70.refs_3_), custom_call_target="tpu_custom_call" | custom-call | flops 671088640 | bytes 10485760 | tf_op jit(solution)/shard_map/finish/pallas_call | solution.py:394
  (1 shorter events, 0.0 us)
Async XLA Ops:
  0.0 11.3 %copy-start = (bf16[256,1024]{1,0:T(8,128)(2,1)S(1)}, bf16[256,1024]{1,0:T(8,128)(2,1)}, u32[]{:S(2)}) copy-start(bf16[256,1024]{1,0:T(8,128)(2,1)} %constant.25.clone.table.refs_4_.refs_6_) | copy-start | bytes 1572868
  0.0 39.0 %copy-start.1 = (bf16[1024,256]{1,0:T(8,128)(2,1)S(1)}, bf16[1024,256]{1,0:T(8,128)(2,1)}, u32[]{:S(2)}) copy-start(bf16[1024,256]{1,0:T(8,128)(2,1)} %constant.26.clone.refs_5_.refs_7_) | copy-start | bytes 1572868
  0.0 11.3 %copy-start.3 = (f32[2]{0:T(128)S(1)}, f32[2]{0:T(128)}, u32[]{:S(2)}) copy-start(f32[2]{0:T(128)} %memory.1) | copy-start | bytes 28
  0.0 11.3 %copy-start.2 = (s32[2]{0:T(128)S(1)}, s32[2]{0:T(128)}, u32[]{:S(2)}) copy-start(s32[2]{0:T(128)} %bands.1) | copy-start | bytes 28
  2.0 38.0 %collective-permute-start.5 = (bf16[1024,256]{1,0:T(8,128)(2,1)S(1)}, bf16[1024,256]{1,0:T(8,128)(2,1)S(1)}, u32[]{:S(2)}, u32[]{:S(2)}) collective-permute-start(bf16[1024,256]{1,0:T(8,128)(2,1)S(1)} %get-tuple-element.24.refs_2_.refs_1_), channel_id=1, source_target_pairs={{0,4},{4,8},{8,12},{1,5},{5,9},{9,13},{2,6},{6,10},{10,14},{3,7},{... | collective-permute-start | bytes 1572872 | tf_op jit(solution)/shard_map/ppermute | solution.py:227
  8.1 30.9 %collective-permute-start.7 = (bf16[1024,128]{1,0:T(8,128)(2,1)S(1)}, bf16[1024,128]{1,0:T(8,128)(2,1)S(1)}, u32[]{:S(2)}, u32[]{:S(2)}) collective-permute-start(bf16[1024,128]{1,0:T(8,128)(2,1)S(1)} %head.1.refs_0_.refs_2_), channel_id=1, source_target_pairs={{0,4},{4,8},{8,12},{12,0},{1,5},{5,9},{9,13},{13,1},{2,6},{6,10},{... | collective-permute-start | bytes 786440 | tf_op jit(solution)/shard_map/ppermute | solution.py:227
  9.7 29.3 %collective-permute-start.8 = (bf16[1024,128]{1,0:T(8,128)(2,1)S(1)}, bf16[1024,128]{1,0:T(8,128)(2,1)S(1)}, u32[]{:S(2)}, u32[]{:S(2)}) collective-permute-start(bf16[1024,128]{1,0:T(8,128)(2,1)S(1)} %get-tuple-element.23.refs_1_.refs_3_), channel_id=1, source_target_pairs={{0,4},{4,8},{8,12},{12,0},{1,5},{5,9},{9,13},{13,1},{2,6},{6,10},{... | collective-permute-start | bytes 786440 | tf_op jit(solution)/shard_map/ppermute | solution.py:227
  11.3 18.3 %collective-permute-start.1 = (f32[2,640]{1,0:T(2,128)S(1)}, f32[2,640]{1,0:T(2,128)S(1)}, u32[]{:S(2)}, u32[]{:S(2)}) collective-permute-start(f32[2,640]{1,0:T(2,128)S(1)} %get-tuple-element.28.refs_2_), channel_id=1, source_target_pairs={{0,4},{4,8},{8,12},{12,0},{1,5},{5,9},{9,13},{13,1},{2,6},{6,10},{... | collective-permute-start | bytes 15368 | tf_op jit(solution)/shard_map/ppermute | solution.py:227
  29.6 5.1 %collective-permute-start.2 = (f32[2,640]{1,0:T(2,128)S(1)}, f32[2,640]{1,0:T(2,128)S(1)}, u32[]{:S(2)}, u32[]{:S(2)}) collective-permute-start(f32[2,640]{1,0:T(2,128)S(1)} %get-tuple-element.29), channel_id=1, source_target_pairs={{0,8},{4,12},{8,0},{12,4},{1,9},{5,13},{9,1},{13,5},{2,10},{6,14},... | collective-permute-start | bytes 15368 | tf_op jit(solution)/shard_map/ppermute | solution.py:227
  35.4 3.6 %collective-permute-start.3 = (f32[1,640]{1,0:T(1,128)S(1)}, f32[1,640]{1,0:T(1,128)S(1)}, u32[]{:S(2)}, u32[]{:S(2)}) collective-permute-start(f32[1,640]{1,0:T(1,128)S(1)} %get-tuple-element.32), channel_id=1, source_target_pairs={{0,2},{2,0},{1,3},{3,1},{4,6},{6,4},{5,7},{7,5},{8,10},{10,8},{9,1... | collective-permute-start | bytes 7688 | tf_op jit(solution)/shard_map/ppermute | solution.py:256
  40.0 13.8 %collective-permute-start.9 = (bf16[1024,256]{1,0:T(8,128)(2,1)S(1)}, bf16[1024,256]{1,0:T(8,128)(2,1)S(1)}, u32[]{:S(2)}, u32[]{:S(2)}) collective-permute-start(bf16[1024,256]{1,0:T(8,128)(2,1)S(1)} %get-tuple-element.38), channel_id=1, source_target_pairs={{0,1},{1,0},{2,3},{3,2},{4,5},{5,4},{6,7},{7,6},{8,9},{9,8},{10,11... | collective-permute-start | bytes 1572872 | tf_op jit(solution)/shard_map/ppermute | solution.py:383
  41.7 13.6 %collective-permute-start.6 = (bf16[1024,256]{1,0:T(8,128)(2,1)}, bf16[1024,256]{1,0:T(8,128)(2,1)S(1)}, u32[]{:S(2)}, u32[]{:S(2)}) collective-permute-start(bf16[1024,256]{1,0:T(8,128)(2,1)} %get-tuple-element.36), channel_id=1, source_target_pairs={{0,1},{1,0},{2,3},{3,2},{4,5},{5,4},{6,7},{7,6},{8,9},{9,8},{10,11... | collective-permute-start | bytes 1572872 | tf_op jit(solution)/shard_map/ppermute | solution.py:383
  42.1 9.5 %collective-permute-start = (bf16[1024,128]{1,0:T(8,128)(2,1)S(1)}, bf16[1024,128]{1,0:T(8,128)(2,1)S(1)}, u32[]{:S(2)}, u32[]{:S(2)}) collective-permute-start(bf16[1024,128]{1,0:T(8,128)(2,1)S(1)} %get-tuple-element.22.refs_3_.refs_1_), channel_id=1, source_target_pairs={{0,4},{4,8},{8,12},{1,5},{5,9},{9,13},{2,6},{6,10},{10,14},{3,7},{... | collective-permute-start | bytes 786440 | tf_op jit(solution)/shard_map/ppermute | solution.py:227
  52.5 4.6 %collective-permute-start.4 = (bf16[1024,128]{1,0:T(8,128)(2,1)S(1)}, bf16[1024,128]{1,0:T(8,128)(2,1)S(1)}, u32[]{:S(2)}, u32[]{:S(2)}) collective-permute-start(bf16[1024,128]{1,0:T(8,128)(2,1)S(1)} %get-tuple-element.34), channel_id=1, source_target_pairs={{0,1},{1,0},{2,3},{3,2},{4,5},{5,4},{6,7},{7,6},{8,9},{9,8},{10,11... | collective-permute-start | bytes 786440 | tf_op jit(solution)/shard_map/ppermute | solution.py:383

commit v3 on v2

--- a/solution.py
+++ b/solution.py
@@ -12,6 +12,7 @@
 BAND_FREQS = 64
 WAVES = 2 * BAND_FREQS
 TAP_ROWS = 256
+FINISH = 2
 PIECES = ((0, 128), (128, 256), (256, 512), (512, 640))
 STAGES = ((0, 1), (2,), (3,))
 WRAPS = (0, 1)
@@ -178,15 +179,23 @@
     acc = None if first else refs[n + 1]
     out = refs[-1]
     width = out.shape[-1]
-    step = 256
     count = refs[0].shape[0]
+    step = count // FINISH if last else 256
+
+    depth = refs[0].shape[1]
+    offs = [(-start) % width for start in starts]
+    if n * depth <= TAP_ROWS:
+        weights = [jnp.concatenate([taps[:depth, o : o + width] for o in offs], axis=0)]
+    else:
+        weights = [taps[:depth, o : o + width] for o in offs]
 
     def block(r):
         total = None if first else acc[r, :]
-        for start, ref in zip(starts, refs):
-            off = (-start) % width
-            weights = taps[: ref.shape[1], off : off + width]
-            part = jnp.dot(ref[r, :], weights, preferred_element_type=F32)
+        data = [ref[r, :] for ref in refs[:n]]
+        if len(weights) == 1:
+            data = [jnp.concatenate(data, axis=1)]
+        for x, w in zip(data, weights):
+            part = jnp.dot(x, w, preferred_element_type=F32)
             total = part if total is None else total + part
         return total
 
@@ -244,14 +253,14 @@
 def row_edges(x):
     place = lax.axis_index("cuts")
     if lax.axis_size("cuts") == 2:
-        return (jnp.where(place == 0, x[-1:], x[:1]),) * 2
+        return (jnp.where(place == 0, x[-1:], x[:1]),)
     return x[-1:], x[:1]
 
 
-def row_neighbours(last, first):
+def row_neighbours(last, first=None):
     cuts = lax.axis_size("cuts")
     if cuts == 1:
-        return first, last
+        return last, last
     up = [(i, (i + 1) % cuts) for i in range(cuts)]
     before = lax.ppermute(last, "cuts", up)
     if cuts == 2:
@@ -292,8 +301,9 @@
 
     extra = () if older is None else (older,)
     edge = (1, cols)
-    estimate, last, first = tiny(estimate_of, [wide, edge, edge], scales, got, sums, *extra)
-    before, after = row_neighbours(last, first)
+    edges = [edge] * (1 if lax.axis_size("cuts") == 2 else 2)
+    estimate, *ends = tiny(estimate_of, [wide, *edges], scales, got, sums, *extra)
+    before, after = row_neighbours(*ends)
     return pl.pallas_call(
         smooth_kernel,
         out_shape=jax.ShapeDtypeStruct((8, cols), F32),
@@ -393,10 +403,10 @@
         if last:
             return pl.pallas_call(
                 kernel,
-                grid=(count // 256,),
+                grid=(FINISH,),
                 out_shape=jax.ShapeDtypeStruct((half, rows, width), BF16),
                 in_specs=specs,
-                out_specs=pl.BlockSpec((256 // rows, rows, width), lambda g: (g, 0, 0)),
+                out_specs=pl.BlockSpec((half // FINISH, rows, width), lambda g: (g, 0, 0)),
                 name="finish",
                 **cost,
             )(*inputs)

time: 60.8 us -> 59.2 us (0.974)
  Pallas kernels: 15.5 us -> 13.9 us
    pallas_call x1, Pallas kernels: 3.34 us -> 2.34 us  [accumulate(): pl.pallas_call(kernel, grid=(FINISH,), out_shape=jax.ShapeDtypeStruct((ha...]
  transfers between devices with their start and end apart: 10 -> 10, of which waited for: 4 -> 4; matrix products, arithmetic and copies ran while one was open for 0% -> 0% of each run, Pallas kernels for 17% -> 16%
where the time goes in v3:
time: 59.2 us; the launch traced here: 58.8 us
  waiting for transfers between devices  26.3 us (44%)
  starting transfers between devices  17.8 us (30%)
  Pallas kernels  13.9 us (23%)
  between operations  0.82 us (1%)
    ppermute x6, waiting for transfers between devices, along_tm(): return lax.ppermute(x, 'tm', route)  24.2 us
    ppermute x6, starting transfers between devices, along_tm(): return lax.ppermute(x, 'tm', route)  15.6 us
    pallas_call x3, Pallas kernels, damp(): pl.pallas_call(functools.partial(damp_kernel, lo, rows, len(stage)), out_...  3.33 us
    pallas_call x2, Pallas kernels, accumulate(): pl.pallas_call(kernel, out_shape=jax.ShapeDtypeStruct((count, width), F32...  3.24 us
    pallas_call x1, Pallas kernels, accumulate(): pl.pallas_call(kernel, grid=(FINISH,), out_shape=jax.ShapeDtypeStruct((ha...  2.34 us
    ppermute x1, waiting for transfers between devices, row_neighbours(): before = lax.ppermute(last, 'cuts', up)  2.1 us
    pallas_call x1, Pallas kernels, local(): pl.pallas_call(split_kernel, out_shape=(*shapes[1:], jax.ShapeDtypeStruct...  2.02 us
    ppermute x1, starting transfers between devices, row_neighbours(): before = lax.ppermute(last, 'cuts', up)  1.56 us
  transfers between devices with their start and end apart: 10, of which 4 were waited for; matrix products, arithmetic and copies ran while one was open for 0% of the time, Pallas kernels for 16%

profile of v3, /device:TPU:0, one launch (start us, length us, event | category | flops | bytes accessed | tf_op | source)
XLA Modules:
  0.0 58.8 jit_solution(10550382904455964726)
XLA Ops:
  0.0 0.0 copy-start
  0.0 0.0 copy-start.1
  0.0 0.0 copy-start.3
  0.0 0.0 copy-start.2
  0.0 2.0 %split.1 = (bf16[1024,128]{1,0:T(8,128)(2,1)S(1)}, bf16[1024,256]{1,0:T(8,128)(2,1)S(1)}, bf16[1024,128]{1,0:T(8,128)(2,1)S(1)}, f32[2,640]{1,0:T(2,128)S(1)}) custom-call(bf16[512,2,640]{2,1,0:T(2,128)(2,1)} %raw.3), custom_call_target="tpu_custom_call" | custom-call | flops 10485760 | bytes 2621440 | tf_op jit(solution)/shard_map/split/pallas_call | solution.py:341
  2.0 5.0 %collective-permute-start.5 = (bf16[1024,256]{1,0:T(8,128)(2,1)S(1)}, bf16[1024,256]{1,0:T(8,128)(2,1)S(1)}, u32[]{:S(2)}, u32[]{:S(2)}) collective-permute-start(bf16[1024,256]{1,0:T(8,128)(2,1)S(1)} %get-tuple-element.24.refs_2_.refs_1_), channel_id=1, source_target_pairs={{0,4},{4,8},{8,12},{1,5},{5,9},{9,13},{2,6},{6,10},{10,14},{3,7},{... | collective-permute-start | bytes 1572872 | tf_op jit(solution)/shard_map/ppermute | solution.py:236
  7.0 1.0 %head.1.refs_0_.refs_2_ = bf16[1024,128]{1,0:T(8,128)(2,1)S(1)} custom-call(bf16[512,2,640]{2,1,0:T(2,128)(2,1)} %raw.3), custom_call_target="tpu_custom_call" | custom-call | flops 655360 | bytes 655360 | tf_op jit(solution)/shard_map/head/pallas_call | solution.py:329
  8.1 1.6 %collective-permute-start.7 = (bf16[1024,128]{1,0:T(8,128)(2,1)S(1)}, bf16[1024,128]{1,0:T(8,128)(2,1)S(1)}, u32[]{:S(2)}, u32[]{:S(2)}) collective-permute-start(bf16[1024,128]{1,0:T(8,128)(2,1)S(1)} %head.1.refs_0_.refs_2_), channel_id=1, source_target_pairs={{0,4},{4,8},{8,12},{12,0},{1,5},{5,9},{9,13},{13,1},{2,6},{6,10},{... | collective-permute-start | bytes 786440 | tf_op jit(solution)/shard_map/ppermute | solution.py:236
  9.7 1.6 %collective-permute-start.8 = (bf16[1024,128]{1,0:T(8,128)(2,1)S(1)}, bf16[1024,128]{1,0:T(8,128)(2,1)S(1)}, u32[]{:S(2)}, u32[]{:S(2)}) collective-permute-start(bf16[1024,128]{1,0:T(8,128)(2,1)S(1)} %get-tuple-element.23.refs_1_.refs_3_), channel_id=1, source_target_pairs={{0,4},{4,8},{8,12},{12,0},{1,5},{5,9},{9,13},{13,1},{2,6},{6,10},{... | collective-permute-start | bytes 786440 | tf_op jit(solution)/shard_map/ppermute | solution.py:236
  11.3 0.1 collective-permute-start.1
  11.3 0.0 copy-done
  11.3 0.0 copy-done.3
  11.3 0.0 copy-done.2
  11.3 1.3 %spec.1 = (f32[256,640]{1,0:T(8,128)S(1)}, f32[256,1]{1,0:T(8,128)S(1)}, f32[2,128]{1,0:T(2,128)S(1)}) custom-call(s32[2]{0:T(128)S(1)} %copy-done.2, f32[2]{0:T(128)S(1)} %copy-done.3, bf16[256,1024]{1,0:T(8,128)(2,1)S(1)} %copy-done, bf16[1024,128]{1,0:T(8,128)(2,1)S(1)} %head.1.refs_0_.refs_2_, bf16[1024,128]{1,0:T(8,128)(2,1)S(1)} %get-tuple-element.23.refs_1_.refs_3_, ...), custom_call_target="tpu_custom_call" | custom-call | flops 335544320 | bytes 2621440 | tf_op jit(solution)/shard_map/spec/pallas_call | solution.py:351
  12.6 16.9 %collective-permute-done.1.refs_1_ = f32[2,640]{1,0:T(2,128)S(1)} collective-permute-done((f32[2,640]{1,0:T(2,128)S(1)}, f32[2,640]{1,0:T(2,128)S(1)}, u32[]{:S(2)}, u32[]{:S(2)}) %collective-permute-start.1) | collective-permute-done | bytes 5152 | tf_op jit(solution)/shard_map/ppermute | solution.py:236
  29.5 0.1 shard_map.64
  29.6 3.5 %collective-permute-start.2 = (f32[2,640]{1,0:T(2,128)S(1)}, f32[2,640]{1,0:T(2,128)S(1)}, u32[]{:S(2)}, u32[]{:S(2)}) collective-permute-start(f32[2,640]{1,0:T(2,128)S(1)} %get-tuple-element.29), channel_id=1, source_target_pairs={{0,8},{4,12},{8,0},{12,4},{1,9},{5,13},{9,1},{13,5},{2,10},{6,14},... | collective-permute-start | bytes 15368 | tf_op jit(solution)/shard_map/ppermute | solution.py:236
  33.1 1.6 %collective-permute-done.2.refs_1_ = f32[2,640]{1,0:T(2,128)S(1)} collective-permute-done((f32[2,640]{1,0:T(2,128)S(1)}, f32[2,640]{1,0:T(2,128)S(1)}, u32[]{:S(2)}, u32[]{:S(2)}) %collective-permute-start.2) | collective-permute-done | bytes 5152 | tf_op jit(solution)/shard_map/ppermute | solution.py:236
  34.7 0.1 shard_map.65
  34.8 1.6 %collective-permute-start.3 = (f32[1,640]{1,0:T(1,128)S(1)}, f32[1,640]{1,0:T(1,128)S(1)}, u32[]{:S(2)}, u32[]{:S(2)}) collective-permute-start(f32[1,640]{1,0:T(1,128)S(1)} %get-tuple-element.32), channel_id=1, source_target_pairs={{0,2},{2,0},{1,3},{3,1},{4,6},{6,4},{5,7},{7,5},{8,10},{10,8},{9,1... | collective-permute-start | bytes 7688 | tf_op jit(solution)/shard_map/ppermute | solution.py:265
  36.3 2.1 %collective-permute-done.3.before.after = f32[1,640]{1,0:T(1,128)S(1)} collective-permute-done((f32[1,640]{1,0:T(1,128)S(1)}, f32[1,640]{1,0:T(1,128)S(1)}, u32[]{:S(2)}, u32[]{:S(2)}) %collective-permute-start.3) | collective-permute-done | bytes 2592 | tf_op jit(solution)/shard_map/ppermute | solution.py:265
  38.5 0.0 collective-permute-done.7.refs_0_
  38.5 0.0 collective-permute-done.8.refs_1_
  38.5 0.0 copy-done.1
  38.5 1.0 %shard_map.68 = (bf16[1024,256]{1,0:T(8,128)(2,1)S(1)}, bf16[1024,256]{1,0:T(8,128)(2,1)S(1)}) custom-call(bf16[1024,128]{1,0:T(8,128)(2,1)S(1)} %collective-permute-done.7.refs_0_, bf16[1024,128]{1,0:T(8,128)(2,1)S(1)} %collective-permute-done.8.refs_1_, bf16[1024,128]{1,0:T(8,128)(2,1)S(1)} %head.1.refs_0_.refs_2_, ...), custom_call_target="tpu_custom_call" | custom-call | flops 402653184 | bytes 2097152 | tf_op jit(solution)/shard_map/pallas_call | solution.py:385
  39.5 0.1 collective-permute-start.9
  39.5 0.0 collective-permute-done.5.refs_0_
  39.5 1.6 %shard_map.67 = (bf16[1024,256]{1,0:T(8,128)(2,1)S(1)}, bf16[1024,256]{1,0:T(8,128)(2,1)}) custom-call(bf16[1024,256]{1,0:T(8,128)(2,1)S(1)} %collective-permute-done.5.refs_0_, bf16[1024,256]{1,0:T(8,128)(2,1)S(1)} %get-tuple-element.24.refs_2_.refs_1_, f32[256,640]{1,0:T(8,128)S(1)} %get-tuple-element.25.refs_2_.refs_4_, ...), custom_call_target="tpu_custom_call" | custom-call | flops 402653184 | bytes 2097152 | tf_op jit(solution)/shard_map/pallas_call | solution.py:385
  41.1 0.5 collective-permute-start.6
  41.6 3.8 %collective-permute-start = (bf16[1024,128]{1,0:T(8,128)(2,1)S(1)}, bf16[1024,128]{1,0:T(8,128)(2,1)S(1)}, u32[]{:S(2)}, u32[]{:S(2)}) collective-permute-start(bf16[1024,128]{1,0:T(8,128)(2,1)S(1)} %get-tuple-element.22.refs_3_.refs_1_), channel_id=1, source_target_pairs={{0,4},{4,8},{8,12},{1,5},{5,9},{9,13},{2,6},{6,10},{10,14},{3,7},{... | collective-permute-start | bytes 786440 | tf_op jit(solution)/shard_map/ppermute | solution.py:236
  45.5 5.7 %collective-permute-done.refs_0_ = bf16[1024,128]{1,0:T(8,128)(2,1)S(1)} collective-permute-done((bf16[1024,128]{1,0:T(8,128)(2,1)S(1)}, bf16[1024,128]{1,0:T(8,128)(2,1)S(1)}, u32[]{:S(2)}, u32[]{:S(2)}) %collective-permute-start) | collective-permute-done | bytes 262176 | tf_op jit(solution)/shard_map/ppermute | solution.py:236
  51.2 0.8 %shard_map.66 = (bf16[1024,128]{1,0:T(8,128)(2,1)S(1)}, bf16[1024,128]{1,0:T(8,128)(2,1)S(1)}) custom-call(bf16[1024,128]{1,0:T(8,128)(2,1)S(1)} %collective-permute-done.refs_0_, bf16[1024,128]{1,0:T(8,128)(2,1)S(1)} %get-tuple-element.22.refs_3_.refs_1_, f32[256,640]{1,0:T(8,128)S(1)} %get-tuple-element.25.refs_2_.refs_4_, ...), custom_call_target="tpu_custom_call" | custom-call | flops 201326592 | bytes 1048576 | tf_op jit(solution)/shard_map/pallas_call | solution.py:385
  52.0 0.1 collective-permute-start.4
  52.7 0.5 taps.1.refs_2_
  53.2 0.0 collective-permute-done.9.refs_1_
  53.2 1.5 %shard_map.69.refs_3_ = f32[1024,1280]{1,0:T(8,128)S(1)} custom-call(bf16[1024,256]{1,0:T(8,128)(2,1)S(1)} %get-tuple-element.37.refs_0_, bf16[1024,256]{1,0:T(8,128)(2,1)S(1)} %collective-permute-done.9.refs_1_, bf16[256,2560]{1,0:T(8,128)(2,1)S(1)} %taps.1.refs_2_), custom_call_target="tpu_custom_call" | custom-call | flops 1342177280 | bytes 10485760 | tf_op jit(solution)/shard_map/pallas_call | solution.py:413
  54.8 0.0 collective-permute-done.6.refs_1_
  54.8 1.7 %shard_map.70.refs_3_ = f32[1024,1280]{1,0:T(8,128)S(1)} custom-call(bf16[1024,256]{1,0:T(8,128)(2,1)S(1)} %get-tuple-element.35.refs_0_, bf16[1024,256]{1,0:T(8,128)(2,1)S(1)} %collective-permute-done.6.refs_1_, bf16[256,2560]{1,0:T(8,128)(2,1)S(1)} %taps.1.refs_2_, f32[1024,1280]{1,0:T(8,128)S(1)} %shard_map.69.refs_3_), custom_call_target="tpu_custom_call", output_to_operand_aliasing={{}: (3, {})} | custom-call | flops 1342177280 | bytes 10485760 | tf_op jit(solution)/shard_map/pallas_call | solution.py:413
  56.5 0.0 collective-permute-done.4.refs_1_
  56.5 2.3 %finish.1 = bf16[512,2,1280]{2,1,0:T(2,128)(2,1)} custom-call(bf16[1024,128]{1,0:T(8,128)(2,1)S(1)} %get-tuple-element.33.refs_0_, bf16[1024,128]{1,0:T(8,128)(2,1)S(1)} %collective-permute-done.4.refs_1_, bf16[256,2560]{1,0:T(8,128)(2,1)S(1)} %taps.1.refs_2_, f32[1024,1280]{1,0:T(8,128)S(1)} %shard_map.70.refs_3_), custom_call_target="tpu_custom_call" | custom-call | flops 671088640 | bytes 10485760 | tf_op jit(solution)/shard_map/finish/pallas_call | solution.py:404
  (1 shorter events, 0.0 us)
Async XLA Ops:
  0.0 11.3 %copy-start = (bf16[256,1024]{1,0:T(8,128)(2,1)S(1)}, bf16[256,1024]{1,0:T(8,128)(2,1)}, u32[]{:S(2)}) copy-start(bf16[256,1024]{1,0:T(8,128)(2,1)} %constant.25.clone.table.refs_4_.refs_6_) | copy-start | bytes 1572868
  0.0 38.5 %copy-start.1 = (bf16[1024,256]{1,0:T(8,128)(2,1)S(1)}, bf16[1024,256]{1,0:T(8,128)(2,1)}, u32[]{:S(2)}) copy-start(bf16[1024,256]{1,0:T(8,128)(2,1)} %constant.26.clone.refs_5_.refs_7_) | copy-start | bytes 1572868
  0.0 11.3 %copy-start.3 = (f32[2]{0:T(128)S(1)}, f32[2]{0:T(128)}, u32[]{:S(2)}) copy-start(f32[2]{0:T(128)} %memory.1) | copy-start | bytes 28
  0.0 11.3 %copy-start.2 = (s32[2]{0:T(128)S(1)}, s32[2]{0:T(128)}, u32[]{:S(2)}) copy-start(s32[2]{0:T(128)} %bands.1) | copy-start | bytes 28
  2.0 37.5 %collective-permute-start.5 = (bf16[1024,256]{1,0:T(8,128)(2,1)S(1)}, bf16[1024,256]{1,0:T(8,128)(2,1)S(1)}, u32[]{:S(2)}, u32[]{:S(2)}) collective-permute-start(bf16[1024,256]{1,0:T(8,128)(2,1)S(1)} %get-tuple-element.24.refs_2_.refs_1_), channel_id=1, source_target_pairs={{0,4},{4,8},{8,12},{1,5},{5,9},{9,13},{2,6},{6,10},{10,14},{3,7},{... | collective-permute-start | bytes 1572872 | tf_op jit(solution)/shard_map/ppermute | solution.py:236
  8.1 30.4 %collective-permute-start.7 = (bf16[1024,128]{1,0:T(8,128)(2,1)S(1)}, bf16[1024,128]{1,0:T(8,128)(2,1)S(1)}, u32[]{:S(2)}, u32[]{:S(2)}) collective-permute-start(bf16[1024,128]{1,0:T(8,128)(2,1)S(1)} %head.1.refs_0_.refs_2_), channel_id=1, source_target_pairs={{0,4},{4,8},{8,12},{12,0},{1,5},{5,9},{9,13},{13,1},{2,6},{6,10},{... | collective-permute-start | bytes 786440 | tf_op jit(solution)/shard_map/ppermute | solution.py:236
  9.7 28.8 %collective-permute-start.8 = (bf16[1024,128]{1,0:T(8,128)(2,1)S(1)}, bf16[1024,128]{1,0:T(8,128)(2,1)S(1)}, u32[]{:S(2)}, u32[]{:S(2)}) collective-permute-start(bf16[1024,128]{1,0:T(8,128)(2,1)S(1)} %get-tuple-element.23.refs_1_.refs_3_), channel_id=1, source_target_pairs={{0,4},{4,8},{8,12},{12,0},{1,5},{5,9},{9,13},{13,1},{2,6},{6,10},{... | collective-permute-start | bytes 786440 | tf_op jit(solution)/shard_map/ppermute | solution.py:236
  11.3 18.3 %collective-permute-start.1 = (f32[2,640]{1,0:T(2,128)S(1)}, f32[2,640]{1,0:T(2,128)S(1)}, u32[]{:S(2)}, u32[]{:S(2)}) collective-permute-start(f32[2,640]{1,0:T(2,128)S(1)} %get-tuple-element.28.refs_2_), channel_id=1, source_target_pairs={{0,4},{4,8},{8,12},{12,0},{1,5},{5,9},{9,13},{13,1},{2,6},{6,10},{... | collective-permute-start | bytes 15368 | tf_op jit(solution)/shard_map/ppermute | solution.py:236
  29.6 5.1 %collective-permute-start.2 = (f32[2,640]{1,0:T(2,128)S(1)}, f32[2,640]{1,0:T(2,128)S(1)}, u32[]{:S(2)}, u32[]{:S(2)}) collective-permute-start(f32[2,640]{1,0:T(2,128)S(1)} %get-tuple-element.29), channel_id=1, source_target_pairs={{0,8},{4,12},{8,0},{12,4},{1,9},{5,13},{9,1},{13,5},{2,10},{6,14},... | collective-permute-start | bytes 15368 | tf_op jit(solution)/shard_map/ppermute | solution.py:236
  34.8 3.7 %collective-permute-start.3 = (f32[1,640]{1,0:T(1,128)S(1)}, f32[1,640]{1,0:T(1,128)S(1)}, u32[]{:S(2)}, u32[]{:S(2)}) collective-permute-start(f32[1,640]{1,0:T(1,128)S(1)} %get-tuple-element.32), channel_id=1, source_target_pairs={{0,2},{2,0},{1,3},{3,1},{4,6},{6,4},{5,7},{7,5},{8,10},{10,8},{9,1... | collective-permute-start | bytes 7688 | tf_op jit(solution)/shard_map/ppermute | solution.py:265
  39.5 13.8 %collective-permute-start.9 = (bf16[1024,256]{1,0:T(8,128)(2,1)S(1)}, bf16[1024,256]{1,0:T(8,128)(2,1)S(1)}, u32[]{:S(2)}, u32[]{:S(2)}) collective-permute-start(bf16[1024,256]{1,0:T(8,128)(2,1)S(1)} %get-tuple-element.38), channel_id=1, source_target_pairs={{0,1},{1,0},{2,3},{3,2},{4,5},{5,4},{6,7},{7,6},{8,9},{9,8},{10,11... | collective-permute-start | bytes 1572872 | tf_op jit(solution)/shard_map/ppermute | solution.py:393
  41.1 13.6 %collective-permute-start.6 = (bf16[1024,256]{1,0:T(8,128)(2,1)}, bf16[1024,256]{1,0:T(8,128)(2,1)S(1)}, u32[]{:S(2)}, u32[]{:S(2)}) collective-permute-start(bf16[1024,256]{1,0:T(8,128)(2,1)} %get-tuple-element.36), channel_id=1, source_target_pairs={{0,1},{1,0},{2,3},{3,2},{4,5},{5,4},{6,7},{7,6},{8,9},{9,8},{10,11... | collective-permute-start | bytes 1572872 | tf_op jit(solution)/shard_map/ppermute | solution.py:393
  41.6 9.5 %collective-permute-start = (bf16[1024,128]{1,0:T(8,128)(2,1)S(1)}, bf16[1024,128]{1,0:T(8,128)(2,1)S(1)}, u32[]{:S(2)}, u32[]{:S(2)}) collective-permute-start(bf16[1024,128]{1,0:T(8,128)(2,1)S(1)} %get-tuple-element.22.refs_3_.refs_1_), channel_id=1, source_target_pairs={{0,4},{4,8},{8,12},{1,5},{5,9},{9,13},{2,6},{6,10},{10,14},{3,7},{... | collective-permute-start | bytes 786440 | tf_op jit(solution)/shard_map/ppermute | solution.py:236
  52.0 4.5 %collective-permute-start.4 = (bf16[1024,128]{1,0:T(8,128)(2,1)S(1)}, bf16[1024,128]{1,0:T(8,128)(2,1)S(1)}, u32[]{:S(2)}, u32[]{:S(2)}) collective-permute-start(bf16[1024,128]{1,0:T(8,128)(2,1)S(1)} %get-tuple-element.34), channel_id=1, source_target_pairs={{0,1},{1,0},{2,3},{3,2},{4,5},{5,4},{6,7},{7,6},{8,9},{9,8},{10,11... | collective-permute-start | bytes 786440 | tf_op jit(solution)/shard_map/ppermute | solution.py:393

commit v4 on v3

--- a/solution.py
+++ b/solution.py
@@ -86,7 +86,14 @@
 
 
 def spec_kernel(rows, distances, angles, bands, memory, table, *refs):
-    *pieces, spec, gain, scales = refs
+    *pieces, spec, gain, scales, local_table, local_bands, local_memory, sems = refs
+    pairs = [(bands, local_bands), (memory, local_memory), (table, local_table)]
+    copies = [pltpu.make_async_copy(a, b, sems.at[i]) for i, (a, b) in enumerate(pairs)]
+    for copy in copies:
+        copy.start()
+    for copy in copies:
+        copy.wait()
+    bands, memory, table = local_bands, local_memory, local_table
     waves = spec.shape[0]
     index = lax.broadcasted_iota(jnp.int32, (waves, 1), 0)
     k = index // rows % BAND_FREQS + 1
@@ -131,7 +138,7 @@
     out[...] = total
 
 
-def damp_kernel(lo, rows, parts, *refs):
+def damp_kernel(lo, rows, parts, late, *refs):
     pieces, owns = refs[:parts], refs[parts : 2 * parts]
     spec, gain, table, turned, cycle, keep, send, old, own = refs[2 * parts :]
     count, cols = old.shape
@@ -162,15 +169,41 @@
             rest = rest.reshape(32, 8, cols) - ring[None]
             target[r : r + 256, :] = rest.reshape(256, cols).astype(BF16)
 
+    def both(sent, kept, source, held):
+        damp(sent, source, send)
+        if late:
+            keep[...] = (total if kept == 0 else total * flip).astype(BF16)
+        else:
+            damp(kept, held, keep)
+
     @pl.when(core == 0)
     def _():
-        damp(1, own, send)
-        damp(0, old, keep)
+        both(1, 0, own, old)
 
     @pl.when(core != 0)
     def _():
-        damp(0, old, send)
-        damp(1, own, keep)
+        both(0, 1, old, own)
+
+
+def hold_kernel(lo, piece, own, scaled, turned, cycle, keep):
+    count, cols = own.shape
+    ring = cycle[:, lo : lo + cols]
+
+    def damp(source):
+        for r in range(0, count, 256):
+            low = jnp.dot(turned[r : r + 256, :], scaled[...], preferred_element_type=F32)
+            rest = source(slice(r, r + 256)).astype(F32) - low
+            rest = rest.reshape(32, 8, cols) - ring[None]
+            keep[r : r + 256, :] = rest.reshape(256, cols).astype(BF16)
+
+    @pl.when(lax.axis_index("col") == 0)
+    def _():
+        here = lax.axis_index("tm") > 0
+        damp(lambda r: jnp.where(here, piece[r, :], jnp.zeros((256, cols), BF16)))
+
+    @pl.when(lax.axis_index("col") != 0)
+    def _():
+        damp(lambda r: own[r, :])
 
 
 def filter_kernel(starts, first, last, rows, *refs):
@@ -355,11 +388,17 @@
             jax.ShapeDtypeStruct((waves, 1), F32),
             jax.ShapeDtypeStruct((rows, 128), F32),
         ),
-        in_specs=[SMEM] * 2 + [VMEM] * (1 + n),
+        in_specs=[ANY] * 3 + [VMEM] * n,
         out_specs=[VMEM] * 3,
+        scratch_shapes=[
+            pltpu.VMEM(table.shape, BF16),
+            pltpu.SMEM((rows,), jnp.int32),
+            pltpu.SMEM((rows,), F32),
+            pltpu.SemaphoreType.DMA((3,)),
+        ],
         name="spec",
         **params(2 * waves * count * cols, 4 * count * cols),
-    )(bands, memory, table, *pieces)
+    )(*(pltpu.with_memory_space_constraint(x, pltpu.HBM) for x in (bands, memory, table)), *pieces)
     first_lag = along_tm(sums, 1)
     cycle = cycle_of(sums, first_lag, scales)
     olds = []
@@ -382,15 +421,27 @@
         inputs = [olds[j] for j in stage] + [pieces[j] for j in stage]
         inputs += [spec, gain, table, turned, cycle]
         spare = (count, hi - lo) if len(stage) > 1 else (16, 128)
+        late = i == len(STAGES) - 1
+        held = jax.ShapeDtypeStruct((waves, hi - lo), BF16) if late else shape
         keep, send = pl.pallas_call(
-            functools.partial(damp_kernel, lo, rows, len(stage)),
-            out_shape=(shape, shape),
+            functools.partial(damp_kernel, lo, rows, len(stage), late),
+            out_shape=(held, shape),
             in_specs=[VMEM] * len(inputs),
             out_specs=[VMEM] * 2,
             scratch_shapes=[pltpu.VMEM((count, hi - lo), BF16), pltpu.VMEM(spare, BF16)],
             **params(6 * waves * count * (hi - lo), 8 * count * (hi - lo)),
         )(*inputs)
         recv = lax.ppermute(send, "col", [(0, 1), (1, 0)])
+        if late:
+            (j,) = stage
+            keep = pl.pallas_call(
+                functools.partial(hold_kernel, lo),
+                out_shape=shape,
+                in_specs=[VMEM] * 5,
+                out_specs=VMEM,
+                name="hold",
+                **params(2 * waves * count * (hi - lo), 4 * count * (hi - lo)),
+            )(olds[j], pieces[j], keep, turned, cycle)
         return (lo, cols + lo), (keep, recv)
 
     def accumulate(part, acc, last):
@@ -421,7 +472,12 @@
 
     acc = None
     for i in range(len(STAGES)):
-        acc = accumulate(damp(i), acc, i == len(STAGES) - 1)
+        starts, data = damp(i)
+        if i == len(STAGES) - 2:
+            acc = accumulate((starts[:1], data[:1]), acc, False)
+            acc = accumulate((starts[1:], data[1:]), acc, False)
+        else:
+            acc = accumulate((starts, data), acc, i == len(STAGES) - 1)
     return acc
 
 

time: 59.2 us -> 63.2 us (1.068)
  Pallas kernels: 13.9 us -> 16.4 us
  local copies, waits for them, and re-layouts: 0.01 us -> 2.09 us
    unnamed x8, local copies, waits for them, and re-layouts: 0.01 us -> 2.09 us
    pallas_call x3 -> x4, Pallas kernels: 3.33 us -> 4.96 us  [the longest x3 4.67 us: damp(): pl.pallas_call(functools.partial(damp_kernel, lo, rows, len(stage), late)...]
    pallas_call x2 -> x3, Pallas kernels: 3.24 us -> 3.52 us  [accumulate(): pl.pallas_call(kernel, out_shape=jax.ShapeDtypeStruct((count, width), F32...]
  transfers between devices with their start and end apart: 10 -> 10, of which waited for: 4 -> 4; matrix products, arithmetic and copies ran while one was open for 0% -> 0% of each run, Pallas kernels for 16% -> 19%
where the time goes in v4:
time: 63.2 us; the launch traced here: 62.7 us
  waiting for transfers between devices  25.8 us (41%)
  starting transfers between devices  17.6 us (28%)
  Pallas kernels  16.4 us (26%)
  local copies, waits for them, and re-layouts  2.09 us (3%)
  between operations  0.81 us (1%)
    ppermute x6, waiting for transfers between devices, along_tm(): return lax.ppermute(x, 'tm', route)  23.7 us
    ppermute x6, starting transfers between devices, along_tm(): return lax.ppermute(x, 'tm', route)  15.6 us
    pallas_call x3, Pallas kernels, damp(): pl.pallas_call(functools.partial(damp_kernel, lo, rows, len(stage), late)...  4.67 us
    pallas_call x3, Pallas kernels, accumulate(): pl.pallas_call(kernel, out_shape=jax.ShapeDtypeStruct((count, width), F32...  3.52 us
    pallas_call x1, Pallas kernels, accumulate(): pl.pallas_call(kernel, grid=(FINISH,), out_shape=jax.ShapeDtypeStruct((ha...  2.37 us
    ppermute x1, waiting for transfers between devices, row_neighbours(): before = lax.ppermute(last, 'cuts', up)  2.1 us
    unnamed x8, local copies, waits for them, and re-layouts  2.09 us
    pallas_call x1, Pallas kernels, local(): pl.pallas_call(split_kernel, out_shape=(*shapes[1:], jax.ShapeDtypeStruct...  1.99 us
  transfers between devices with their start and end apart: 10, of which 4 were waited for; matrix products, arithmetic and copies ran while one was open for 0% of the time, Pallas kernels for 19%

profile of v4, /device:TPU:0, one launch (start us, length us, event | category | flops | bytes accessed | tf_op | source)
XLA Modules:
  0.0 62.7 jit_solution(4352280034077901451)
XLA Ops:
  0.0 0.0 copy-start.1
  0.0 2.0 %split.1 = (bf16[1024,128]{1,0:T(8,128)(2,1)S(1)}, bf16[1024,256]{1,0:T(8,128)(2,1)S(1)}, bf16[1024,128]{1,0:T(8,128)(2,1)S(1)}, f32[2,640]{1,0:T(2,128)S(1)}) custom-call(bf16[512,2,640]{2,1,0:T(2,128)(2,1)} %raw.3), custom_call_target="tpu_custom_call" | custom-call | flops 10485760 | bytes 2621440 | tf_op jit(solution)/shard_map/split/pallas_call | solution.py:374
  2.0 5.0 %collective-permute-start.5 = (bf16[1024,256]{1,0:T(8,128)(2,1)S(1)}, bf16[1024,256]{1,0:T(8,128)(2,1)S(1)}, u32[]{:S(2)}, u32[]{:S(2)}) collective-permute-start(bf16[1024,256]{1,0:T(8,128)(2,1)S(1)} %get-tuple-element.24.refs_2_.refs_1_), channel_id=1, source_target_pairs={{0,4},{4,8},{8,12},{1,5},{5,9},{9,13},{2,6},{6,10},{10,14},{3,7},{... | collective-permute-start | bytes 1572872 | tf_op jit(solution)/shard_map/ppermute | solution.py:269
  7.0 1.0 %head.1.refs_0_.refs_2_ = bf16[1024,128]{1,0:T(8,128)(2,1)S(1)} custom-call(bf16[512,2,640]{2,1,0:T(2,128)(2,1)} %raw.3), custom_call_target="tpu_custom_call" | custom-call | flops 655360 | bytes 655360 | tf_op jit(solution)/shard_map/head/pallas_call | solution.py:362
  8.0 1.6 %collective-permute-start.7 = (bf16[1024,128]{1,0:T(8,128)(2,1)S(1)}, bf16[1024,128]{1,0:T(8,128)(2,1)S(1)}, u32[]{:S(2)}, u32[]{:S(2)}) collective-permute-start(bf16[1024,128]{1,0:T(8,128)(2,1)S(1)} %head.1.refs_0_.refs_2_), channel_id=1, source_target_pairs={{0,4},{4,8},{8,12},{12,0},{1,5},{5,9},{9,13},{13,1},{2,6},{6,10},{... | collective-permute-start | bytes 786440 | tf_op jit(solution)/shard_map/ppermute | solution.py:269
  9.6 1.6 %collective-permute-start.8 = (bf16[1024,128]{1,0:T(8,128)(2,1)S(1)}, bf16[1024,128]{1,0:T(8,128)(2,1)S(1)}, u32[]{:S(2)}, u32[]{:S(2)}) collective-permute-start(bf16[1024,128]{1,0:T(8,128)(2,1)S(1)} %get-tuple-element.23.refs_1_.refs_3_), channel_id=1, source_target_pairs={{0,4},{4,8},{8,12},{12,0},{1,5},{5,9},{9,13},{13,1},{2,6},{6,10},{... | collective-permute-start | bytes 786440 | tf_op jit(solution)/shard_map/ppermute | solution.py:269
  11.2 0.1 collective-permute-start.1
  11.3 0.0 copy-start.3
  11.3 1.8 %spec.1 = (f32[256,640]{1,0:T(8,128)S(1)}, f32[256,1]{1,0:T(8,128)S(1)}, f32[2,128]{1,0:T(2,128)S(1)}) custom-call(s32[2]{0:T(128)} %bands.1, f32[2]{0:T(128)} %memory.1, bf16[256,1024]{1,0:T(8,128)(2,1)} %constant.25.clone.table.refs_4_.refs_6_, bf16[1024,128]{1,0:T(8,128)(2,1)S(1)} %head.1.refs_0_.refs_2_, ...), custom_call_target="tpu_custom_call" | custom-call | flops 335544320 | bytes 2621440 | tf_op jit(solution)/shard_map/spec/pallas_call | solution.py:384
  13.1 16.4 %collective-permute-done.1.refs_1_ = f32[2,640]{1,0:T(2,128)S(1)} collective-permute-done((f32[2,640]{1,0:T(2,128)S(1)}, f32[2,640]{1,0:T(2,128)S(1)}, u32[]{:S(2)}, u32[]{:S(2)}) %collective-permute-start.1) | collective-permute-done | bytes 5152 | tf_op jit(solution)/shard_map/ppermute | solution.py:269
  29.5 0.1 shard_map.64
  29.6 3.5 %collective-permute-start.2 = (f32[2,640]{1,0:T(2,128)S(1)}, f32[2,640]{1,0:T(2,128)S(1)}, u32[]{:S(2)}, u32[]{:S(2)}) collective-permute-start(f32[2,640]{1,0:T(2,128)S(1)} %get-tuple-element.29), channel_id=1, source_target_pairs={{0,8},{4,12},{8,0},{12,4},{1,9},{5,13},{9,1},{13,5},{2,10},{6,14},... | collective-permute-start | bytes 15368 | tf_op jit(solution)/shard_map/ppermute | solution.py:269
  33.1 1.6 %collective-permute-done.2.refs_1_ = f32[2,640]{1,0:T(2,128)S(1)} collective-permute-done((f32[2,640]{1,0:T(2,128)S(1)}, f32[2,640]{1,0:T(2,128)S(1)}, u32[]{:S(2)}, u32[]{:S(2)}) %collective-permute-start.2) | collective-permute-done | bytes 5152 | tf_op jit(solution)/shard_map/ppermute | solution.py:269
  34.7 0.1 shard_map.65
  34.7 1.6 %collective-permute-start.3 = (f32[1,640]{1,0:T(1,128)S(1)}, f32[1,640]{1,0:T(1,128)S(1)}, u32[]{:S(2)}, u32[]{:S(2)}) collective-permute-start(f32[1,640]{1,0:T(1,128)S(1)} %get-tuple-element.32), channel_id=1, source_target_pairs={{0,2},{2,0},{1,3},{3,1},{4,6},{6,4},{5,7},{7,5},{8,10},{10,8},{9,1... | collective-permute-start | bytes 7688 | tf_op jit(solution)/shard_map/ppermute | solution.py:298
  36.3 2.1 %collective-permute-done.3.before.after = f32[1,640]{1,0:T(1,128)S(1)} collective-permute-done((f32[1,640]{1,0:T(1,128)S(1)}, f32[1,640]{1,0:T(1,128)S(1)}, u32[]{:S(2)}, u32[]{:S(2)}) %collective-permute-start.3) | collective-permute-done | bytes 2592 | tf_op jit(solution)/shard_map/ppermute | solution.py:298
  38.4 0.0 collective-permute-done.7.refs_0_
  38.4 0.0 collective-permute-done.8.refs_1_
  38.4 0.0 copy-start
  38.5 1.0 %copy-done = bf16[256,1024]{1,0:T(8,128)(2,1)S(1)} copy-done((bf16[256,1024]{1,0:T(8,128)(2,1)S(1)}, bf16[256,1024]{1,0:T(8,128)(2,1)}, u32[]{:S(2)}) %copy-start) | copy-done | bytes 524312
  39.5 0.0 copy-start.2
  39.5 1.0 %copy-done.2 = bf16[1024,256]{1,0:T(8,128)(2,1)S(1)} copy-done((bf16[1024,256]{1,0:T(8,128)(2,1)S(1)}, bf16[1024,256]{1,0:T(8,128)(2,1)}, u32[]{:S(2)}) %copy-start.2) | copy-done | bytes 524312
  40.5 1.7 %shard_map.68 = (bf16[1024,256]{1,0:T(8,128)(2,1)S(1)}, bf16[1024,256]{1,0:T(8,128)(2,1)}) custom-call(bf16[1024,128]{1,0:T(8,128)(2,1)S(1)} %collective-permute-done.7.refs_0_, bf16[1024,128]{1,0:T(8,128)(2,1)S(1)} %collective-permute-done.8.refs_1_, bf16[1024,128]{1,0:T(8,128)(2,1)S(1)} %head.1.refs_0_.refs_2_, ...), custom_call_target="tpu_custom_call" | custom-call | flops 402653184 | bytes 2097152 | tf_op jit(solution)/shard_map/pallas_call | solution.py:426
  42.3 0.0 collective-permute-start.9
  42.3 0.0 collective-permute-done.5.refs_0_
  42.3 1.6 %shard_map.67 = (bf16[1024,256]{1,0:T(8,128)(2,1)S(1)}, bf16[1024,256]{1,0:T(8,128)(2,1)}) custom-call(bf16[1024,256]{1,0:T(8,128)(2,1)S(1)} %collective-permute-done.5.refs_0_, bf16[1024,256]{1,0:T(8,128)(2,1)S(1)} %get-tuple-element.24.refs_2_.refs_1_, f32[256,640]{1,0:T(8,128)S(1)} %get-tuple-element.25.refs_2_.refs_4_, ...), custom_call_target="tpu_custom_call" | custom-call | flops 402653184 | bytes 2097152 | tf_op jit(solution)/shard_map/pallas_call | solution.py:426
  43.8 0.5 collective-permute-start.6
  44.4 3.8 %collective-permute-start = (bf16[1024,128]{1,0:T(8,128)(2,1)S(1)}, bf16[1024,128]{1,0:T(8,128)(2,1)S(1)}, u32[]{:S(2)}, u32[]{:S(2)}) collective-permute-start(bf16[1024,128]{1,0:T(8,128)(2,1)S(1)} %get-tuple-element.22.refs_3_.refs_1_.own), channel_id=1, source_target_pairs={{0,4},{4,8},{8,12},{1,5},{5,9},{9,13},{2,6},{6,10},{10,14},{3,7},{... | collective-permute-start | bytes 786440 | tf_op jit(solution)/shard_map/ppermute | solution.py:269
  48.2 5.7 %collective-permute-done.refs_0_.piece = bf16[1024,128]{1,0:T(8,128)(2,1)S(1)} collective-permute-done((bf16[1024,128]{1,0:T(8,128)(2,1)S(1)}, bf16[1024,128]{1,0:T(8,128)(2,1)S(1)}, u32[]{:S(2)}, u32[]{:S(2)}) %collective-permute-start) | collective-permute-done | bytes 262176 | tf_op jit(solution)/shard_map/ppermute | solution.py:269
  53.9 0.0 copy-done.1
  53.9 1.4 %shard_map.66 = (bf16[256,128]{1,0:T(8,128)(2,1)S(1)}, bf16[1024,128]{1,0:T(8,128)(2,1)}) custom-call(bf16[1024,128]{1,0:T(8,128)(2,1)S(1)} %collective-permute-done.refs_0_.piece, bf16[1024,128]{1,0:T(8,128)(2,1)S(1)} %get-tuple-element.22.refs_3_.refs_1_.own, f32[256,640]{1,0:T(8,128)S(1)} %get-tuple-element.25.refs_2_.refs_4_, ...), custom_call_target="tpu_custom_call" | custom-call | flops 201326592 | bytes 1048576 | tf_op jit(solution)/shard_map/pallas_call | solution.py:426
  55.3 0.0 collective-permute-start.4
  55.9 0.5 taps.1.refs_2_.refs_1_
  56.5 0.0 copy-done.3
  56.5 0.3 hold.1.refs_0_
  56.8 0.0 collective-permute-done.9.refs_1_
  56.8 1.5 %shard_map.69.refs_2_ = f32[1024,1280]{1,0:T(8,128)S(1)} custom-call(bf16[1024,256]{1,0:T(8,128)(2,1)S(1)} %get-tuple-element.37.refs_0_, bf16[1024,256]{1,0:T(8,128)(2,1)S(1)} %collective-permute-done.9.refs_1_, bf16[256,2560]{1,0:T(8,128)(2,1)S(1)} %taps.1.refs_2_.refs_1_), custom_call_target="tpu_custom_call" | custom-call | flops 1342177280 | bytes 10485760 | tf_op jit(solution)/shard_map/pallas_call | solution.py:464
  58.3 1.0 %shard_map.70.refs_2_ = f32[1024,1280]{1,0:T(8,128)S(1)} custom-call(bf16[1024,256]{1,0:T(8,128)(2,1)S(1)} %get-tuple-element.36.refs_0_, bf16[256,2560]{1,0:T(8,128)(2,1)S(1)} %taps.1.refs_2_.refs_1_, f32[1024,1280]{1,0:T(8,128)S(1)} %shard_map.69.refs_2_), custom_call_target="tpu_custom_call", output_to_operand_aliasing={{}: (2, {})} | custom-call | flops 671088640 | bytes 10485760 | tf_op jit(solution)/shard_map/pallas_call | solution.py:464
  59.3 0.0 collective-permute-done.6.refs_0_
  59.3 1.0 %shard_map.71.refs_3_ = f32[1024,1280]{1,0:T(8,128)S(1)} custom-call(bf16[1024,256]{1,0:T(8,128)(2,1)S(1)} %collective-permute-done.6.refs_0_, bf16[256,2560]{1,0:T(8,128)(2,1)S(1)} %taps.1.refs_2_.refs_1_, f32[1024,1280]{1,0:T(8,128)S(1)} %shard_map.70.refs_2_), custom_call_target="tpu_custom_call", output_to_operand_aliasing={{}: (2, {})} | custom-call | flops 671088640 | bytes 10485760 | tf_op jit(solution)/shard_map/pallas_call | solution.py:464
  60.3 0.0 collective-permute-done.4.refs_1_
  60.3 2.4 %finish.1 = bf16[512,2,1280]{2,1,0:T(2,128)(2,1)} custom-call(bf16[1024,128]{1,0:T(8,128)(2,1)S(1)} %hold.1.refs_0_, bf16[1024,128]{1,0:T(8,128)(2,1)S(1)} %collective-permute-done.4.refs_1_, bf16[256,2560]{1,0:T(8,128)(2,1)S(1)} %taps.1.refs_2_.refs_1_, f32[1024,1280]{1,0:T(8,128)S(1)} %shard_map.71.refs_3_), custom_call_target="tpu_custom_call" | custom-call | flops 671088640 | bytes 10485760 | tf_op jit(solution)/shard_map/finish/pallas_call | solution.py:455
  (1 shorter events, 0.0 us)
Async XLA Ops:
  0.0 53.9 %copy-start.1 = (bf16[256,1024]{1,0:T(8,128)(2,1)S(1)}, bf16[256,1024]{1,0:T(8,128)(2,1)}, u32[]{:S(2)}) copy-start(bf16[256,1024]{1,0:T(8,128)(2,1)} %constant.25.clone.table.refs_4_.refs_6_) | copy-start | bytes 1572868
  2.0 40.3 %collective-permute-start.5 = (bf16[1024,256]{1,0:T(8,128)(2,1)S(1)}, bf16[1024,256]{1,0:T(8,128)(2,1)S(1)}, u32[]{:S(2)}, u32[]{:S(2)}) collective-permute-start(bf16[1024,256]{1,0:T(8,128)(2,1)S(1)} %get-tuple-element.24.refs_2_.refs_1_), channel_id=1, source_target_pairs={{0,4},{4,8},{8,12},{1,5},{5,9},{9,13},{2,6},{6,10},{10,14},{3,7},{... | collective-permute-start | bytes 1572872 | tf_op jit(solution)/shard_map/ppermute | solution.py:269
  8.0 30.4 %collective-permute-start.7 = (bf16[1024,128]{1,0:T(8,128)(2,1)S(1)}, bf16[1024,128]{1,0:T(8,128)(2,1)S(1)}, u32[]{:S(2)}, u32[]{:S(2)}) collective-permute-start(bf16[1024,128]{1,0:T(8,128)(2,1)S(1)} %head.1.refs_0_.refs_2_), channel_id=1, source_target_pairs={{0,4},{4,8},{8,12},{12,0},{1,5},{5,9},{9,13},{13,1},{2,6},{6,10},{... | collective-permute-start | bytes 786440 | tf_op jit(solution)/shard_map/ppermute | solution.py:269
  9.6 28.8 %collective-permute-start.8 = (bf16[1024,128]{1,0:T(8,128)(2,1)S(1)}, bf16[1024,128]{1,0:T(8,128)(2,1)S(1)}, u32[]{:S(2)}, u32[]{:S(2)}) collective-permute-start(bf16[1024,128]{1,0:T(8,128)(2,1)S(1)} %get-tuple-element.23.refs_1_.refs_3_), channel_id=1, source_target_pairs={{0,4},{4,8},{8,12},{12,0},{1,5},{5,9},{9,13},{13,1},{2,6},{6,10},{... | collective-permute-start | bytes 786440 | tf_op jit(solution)/shard_map/ppermute | solution.py:269
  11.2 18.3 %collective-permute-start.1 = (f32[2,640]{1,0:T(2,128)S(1)}, f32[2,640]{1,0:T(2,128)S(1)}, u32[]{:S(2)}, u32[]{:S(2)}) collective-permute-start(f32[2,640]{1,0:T(2,128)S(1)} %get-tuple-element.28.refs_2_), channel_id=1, source_target_pairs={{0,4},{4,8},{8,12},{12,0},{1,5},{5,9},{9,13},{13,1},{2,6},{6,10},{... | collective-permute-start | bytes 15368 | tf_op jit(solution)/shard_map/ppermute | solution.py:269
  11.3 45.2 %copy-start.3 = (bf16[1024,256]{1,0:T(8,128)(2,1)S(1)}, bf16[1024,256]{1,0:T(8,128)(2,1)}, u32[]{:S(2)}) copy-start(bf16[1024,256]{1,0:T(8,128)(2,1)} %constant.26.clone.refs_5_.turned.refs_7_) | copy-start | bytes 1572868
  29.6 5.1 %collective-permute-start.2 = (f32[2,640]{1,0:T(2,128)S(1)}, f32[2,640]{1,0:T(2,128)S(1)}, u32[]{:S(2)}, u32[]{:S(2)}) collective-permute-start(f32[2,640]{1,0:T(2,128)S(1)} %get-tuple-element.29), channel_id=1, source_target_pairs={{0,8},{4,12},{8,0},{12,4},{1,9},{5,13},{9,1},{13,5},{2,10},{6,14},... | collective-permute-start | bytes 15368 | tf_op jit(solution)/shard_map/ppermute | solution.py:269
  34.7 3.7 %collective-permute-start.3 = (f32[1,640]{1,0:T(1,128)S(1)}, f32[1,640]{1,0:T(1,128)S(1)}, u32[]{:S(2)}, u32[]{:S(2)}) collective-permute-start(f32[1,640]{1,0:T(1,128)S(1)} %get-tuple-element.32), channel_id=1, source_target_pairs={{0,2},{2,0},{1,3},{3,1},{4,6},{6,4},{5,7},{7,5},{8,10},{10,8},{9,1... | collective-permute-start | bytes 7688 | tf_op jit(solution)/shard_map/ppermute | solution.py:298
  38.4 1.0 %copy-start = (bf16[256,1024]{1,0:T(8,128)(2,1)S(1)}, bf16[256,1024]{1,0:T(8,128)(2,1)}, u32[]{:S(2)}) copy-start(bf16[256,1024]{1,0:T(8,128)(2,1)} %constant.25.clone.table.refs_4_.refs_6_) | copy-start | bytes 1572868
  39.5 1.0 %copy-start.2 = (bf16[1024,256]{1,0:T(8,128)(2,1)S(1)}, bf16[1024,256]{1,0:T(8,128)(2,1)}, u32[]{:S(2)}) copy-start(bf16[1024,256]{1,0:T(8,128)(2,1)} %constant.26.clone.refs_5_.turned.refs_7_) | copy-start | bytes 1572868
  42.3 14.5 %collective-permute-start.9 = (bf16[1024,256]{1,0:T(8,128)(2,1)}, bf16[1024,256]{1,0:T(8,128)(2,1)S(1)}, u32[]{:S(2)}, u32[]{:S(2)}) collective-permute-start(bf16[1024,256]{1,0:T(8,128)(2,1)} %get-tuple-element.38), channel_id=1, source_target_pairs={{0,1},{1,0},{2,3},{3,2},{4,5},{5,4},{6,7},{7,6},{8,9},{9,8},{10,11... | collective-permute-start | bytes 1572872 | tf_op jit(solution)/shard_map/ppermute | solution.py:434
  43.8 15.5 %collective-permute-start.6 = (bf16[1024,256]{1,0:T(8,128)(2,1)}, bf16[1024,256]{1,0:T(8,128)(2,1)S(1)}, u32[]{:S(2)}, u32[]{:S(2)}) collective-permute-start(bf16[1024,256]{1,0:T(8,128)(2,1)} %get-tuple-element.35), channel_id=1, source_target_pairs={{0,1},{1,0},{2,3},{3,2},{4,5},{5,4},{6,7},{7,6},{8,9},{9,8},{10,11... | collective-permute-start | bytes 1572872 | tf_op jit(solution)/shard_map/ppermute | solution.py:434
  44.4 9.5 %collective-permute-start = (bf16[1024,128]{1,0:T(8,128)(2,1)S(1)}, bf16[1024,128]{1,0:T(8,128)(2,1)S(1)}, u32[]{:S(2)}, u32[]{:S(2)}) collective-permute-start(bf16[1024,128]{1,0:T(8,128)(2,1)S(1)} %get-tuple-element.22.refs_3_.refs_1_.own), channel_id=1, source_target_pairs={{0,4},{4,8},{8,12},{1,5},{5,9},{9,13},{2,6},{6,10},{10,14},{3,7},{... | collective-permute-start | bytes 786440 | tf_op jit(solution)/shard_map/ppermute | solution.py:269
  55.3 5.1 %collective-permute-start.4 = (bf16[1024,128]{1,0:T(8,128)(2,1)}, bf16[1024,128]{1,0:T(8,128)(2,1)S(1)}, u32[]{:S(2)}, u32[]{:S(2)}) collective-permute-start(bf16[1024,128]{1,0:T(8,128)(2,1)} %get-tuple-element.34), channel_id=1, source_target_pairs={{0,1},{1,0},{2,3},{3,2},{4,5},{5,4},{6,7},{7,6},{8,9},{9,8},{10,11... | collective-permute-start | bytes 786440 | tf_op jit(solution)/shard_map/ppermute | solution.py:434

commit v5 on v4

--- a/solution.py
+++ b/solution.py
@@ -12,7 +12,7 @@
 BAND_FREQS = 64
 WAVES = 2 * BAND_FREQS
 TAP_ROWS = 256
-FINISH = 2
+FINISH = 8
 PIECES = ((0, 128), (128, 256), (256, 512), (512, 640))
 STAGES = ((0, 1), (2,), (3,))
 WRAPS = (0, 1)
@@ -163,11 +163,11 @@
 
     def damp(half, source, target):
         scaled = (total if half == 0 else total * flip).astype(BF16)
-        for r in range(0, count, 256):
-            low = jnp.dot(turned[r : r + 256, :], scaled, preferred_element_type=F32)
-            rest = source[r : r + 256, :].astype(F32) - low
-            rest = rest.reshape(32, 8, cols) - ring[None]
-            target[r : r + 256, :] = rest.reshape(256, cols).astype(BF16)
+        for r in range(0, count, 512):
+            low = jnp.dot(turned[r : r + 512, :], scaled, preferred_element_type=F32)
+            rest = source[r : r + 512, :].astype(F32) - low
+            rest = rest.reshape(64, 8, cols) - ring[None]
+            target[r : r + 512, :] = rest.reshape(512, cols).astype(BF16)
 
     def both(sent, kept, source, held):
         damp(sent, source, send)
@@ -190,16 +190,16 @@
     ring = cycle[:, lo : lo + cols]
 
     def damp(source):
-        for r in range(0, count, 256):
-            low = jnp.dot(turned[r : r + 256, :], scaled[...], preferred_element_type=F32)
-            rest = source(slice(r, r + 256)).astype(F32) - low
-            rest = rest.reshape(32, 8, cols) - ring[None]
-            keep[r : r + 256, :] = rest.reshape(256, cols).astype(BF16)
+        for r in range(0, count, 512):
+            low = jnp.dot(turned[r : r + 512, :], scaled[...], preferred_element_type=F32)
+            rest = source(slice(r, r + 512)).astype(F32) - low
+            rest = rest.reshape(64, 8, cols) - ring[None]
+            keep[r : r + 512, :] = rest.reshape(512, cols).astype(BF16)
 
     @pl.when(lax.axis_index("col") == 0)
     def _():
         here = lax.axis_index("tm") > 0
-        damp(lambda r: jnp.where(here, piece[r, :], jnp.zeros((256, cols), BF16)))
+        damp(lambda r: jnp.where(here, piece[r, :], jnp.zeros((512, cols), BF16)))
 
     @pl.when(lax.axis_index("col") != 0)
     def _():
@@ -210,7 +210,10 @@
     n = len(starts)
     taps = refs[n]
     acc = None if first else refs[n + 1]
-    out = refs[-1]
+    if last:
+        out, buffer, sems = refs[-3:]
+    else:
+        out = refs[-1]
     width = out.shape[-1]
     count = refs[0].shape[0]
     step = count // FINISH if last else 256
@@ -233,8 +236,15 @@
         return total
 
     if last:
-        r = pl.ds(pl.multiple_of(pl.program_id(0) * step, step), step)
-        out[...] = block(r).astype(BF16).reshape(step // rows, rows, width)
+        copies = []
+        for i in range(FINISH):
+            part = pl.ds(i * (step // rows), step // rows)
+            total = block(slice(i * step, (i + 1) * step)).astype(BF16)
+            buffer[part] = total.reshape(step // rows, rows, width)
+            copies.append(pltpu.make_async_copy(buffer.at[part], out.at[part], sems.at[i]))
+            copies[-1].start()
+        for copy in copies:
+            copy.wait()
     else:
         for b in range(0, count, step):
             out[b : b + step, :] = block(slice(b, b + step))
@@ -449,15 +459,18 @@
         inputs = [*data, taps] + ([] if acc is None else [acc])
         kernel = functools.partial(filter_kernel, starts, acc is None, last, rows)
         depth = sum(x.shape[1] for x in data)
-        cost = params(2 * count * depth * width, 8 * count * width)
+        cost = params(2 * count * depth * width, 8 * count * width, (16 if last else 8) << 20)
         specs = [VMEM] * len(inputs)
         if last:
             return pl.pallas_call(
                 kernel,
-                grid=(FINISH,),
                 out_shape=jax.ShapeDtypeStruct((half, rows, width), BF16),
                 in_specs=specs,
-                out_specs=pl.BlockSpec((half // FINISH, rows, width), lambda g: (g, 0, 0)),
+                out_specs=ANY,
+                scratch_shapes=[
+                    pltpu.VMEM((half, rows, width), BF16),
+                    pltpu.SemaphoreType.DMA((FINISH,)),
+                ],
                 name="finish",
                 **cost,
             )(*inputs)

time: 63.2 us -> 62.7 us (level)
  no operation moved by 1% of the time
where the time goes in v5:
time: 62.7 us; the launch traced here: 62.2 us
  waiting for transfers between devices  25.8 us (41%)
  starting transfers between devices  17.6 us (28%)
  Pallas kernels  15.9 us (25%)
  local copies, waits for them, and re-layouts  2.09 us (3%)
  between operations  0.81 us (1%)
    ppermute x6, waiting for transfers between devices, along_tm(): return lax.ppermute(x, 'tm', route)  23.7 us
    ppermute x6, starting transfers between devices, along_tm(): return lax.ppermute(x, 'tm', route)  15.6 us
    pallas_call x3, Pallas kernels, damp(): pl.pallas_call(functools.partial(damp_kernel, lo, rows, len(stage), late)...  4.67 us
    pallas_call x3, Pallas kernels, accumulate(): pl.pallas_call(kernel, out_shape=jax.ShapeDtypeStruct((count, width), F32...  3.52 us
    ppermute x1, waiting for transfers between devices, row_neighbours(): before = lax.ppermute(last, 'cuts', up)  2.1 us
    unnamed x8, local copies, waits for them, and re-layouts  2.09 us
    pallas_call x1, Pallas kernels, local(): pl.pallas_call(split_kernel, out_shape=(*shapes[1:], jax.ShapeDtypeStruct...  1.99 us
    pallas_call x1, Pallas kernels, accumulate(): pl.pallas_call(kernel, out_shape=jax.ShapeDtypeStruct((half, rows, width)...  1.87 us
  transfers between devices with their start and end apart: 10, of which 4 were waited for; matrix products, arithmetic and copies ran while one was open for 0% of the time, Pallas kernels for 19%

profile of v5, /device:TPU:0, one launch (start us, length us, event | category | flops | bytes accessed | tf_op | source)
XLA Modules:
  0.0 62.2 jit_solution(11564680635971464916)
XLA Ops:
  0.0 0.0 copy-start.1
  0.0 2.0 %split.1 = (bf16[1024,128]{1,0:T(8,128)(2,1)S(1)}, bf16[1024,256]{1,0:T(8,128)(2,1)S(1)}, bf16[1024,128]{1,0:T(8,128)(2,1)S(1)}, f32[2,640]{1,0:T(2,128)S(1)}) custom-call(bf16[512,2,640]{2,1,0:T(2,128)(2,1)} %raw.3), custom_call_target="tpu_custom_call" | custom-call | flops 10485760 | bytes 2621440 | tf_op jit(solution)/shard_map/split/pallas_call | solution.py:384
  2.0 5.0 %collective-permute-start.5 = (bf16[1024,256]{1,0:T(8,128)(2,1)S(1)}, bf16[1024,256]{1,0:T(8,128)(2,1)S(1)}, u32[]{:S(2)}, u32[]{:S(2)}) collective-permute-start(bf16[1024,256]{1,0:T(8,128)(2,1)S(1)} %get-tuple-element.24.refs_2_.refs_1_), channel_id=1, source_target_pairs={{0,4},{4,8},{8,12},{1,5},{5,9},{9,13},{2,6},{6,10},{10,14},{3,7},{... | collective-permute-start | bytes 1572872 | tf_op jit(solution)/shard_map/ppermute | solution.py:279
  7.0 1.0 %head.1.refs_0_.refs_2_ = bf16[1024,128]{1,0:T(8,128)(2,1)S(1)} custom-call(bf16[512,2,640]{2,1,0:T(2,128)(2,1)} %raw.3), custom_call_target="tpu_custom_call" | custom-call | flops 655360 | bytes 655360 | tf_op jit(solution)/shard_map/head/pallas_call | solution.py:372
  8.0 1.6 %collective-permute-start.7 = (bf16[1024,128]{1,0:T(8,128)(2,1)S(1)}, bf16[1024,128]{1,0:T(8,128)(2,1)S(1)}, u32[]{:S(2)}, u32[]{:S(2)}) collective-permute-start(bf16[1024,128]{1,0:T(8,128)(2,1)S(1)} %head.1.refs_0_.refs_2_), channel_id=1, source_target_pairs={{0,4},{4,8},{8,12},{12,0},{1,5},{5,9},{9,13},{13,1},{2,6},{6,10},{... | collective-permute-start | bytes 786440 | tf_op jit(solution)/shard_map/ppermute | solution.py:279
  9.6 1.6 %collective-permute-start.8 = (bf16[1024,128]{1,0:T(8,128)(2,1)S(1)}, bf16[1024,128]{1,0:T(8,128)(2,1)S(1)}, u32[]{:S(2)}, u32[]{:S(2)}) collective-permute-start(bf16[1024,128]{1,0:T(8,128)(2,1)S(1)} %get-tuple-element.23.refs_1_.refs_3_), channel_id=1, source_target_pairs={{0,4},{4,8},{8,12},{12,0},{1,5},{5,9},{9,13},{13,1},{2,6},{6,10},{... | collective-permute-start | bytes 786440 | tf_op jit(solution)/shard_map/ppermute | solution.py:279
  11.2 0.1 collective-permute-start.1
  11.3 0.0 copy-start.3
  11.3 1.8 %spec.1 = (f32[256,640]{1,0:T(8,128)S(1)}, f32[256,1]{1,0:T(8,128)S(1)}, f32[2,128]{1,0:T(2,128)S(1)}) custom-call(s32[2]{0:T(128)} %bands.1, f32[2]{0:T(128)} %memory.1, bf16[256,1024]{1,0:T(8,128)(2,1)} %constant.25.clone.table.refs_4_.refs_6_, bf16[1024,128]{1,0:T(8,128)(2,1)S(1)} %head.1.refs_0_.refs_2_, ...), custom_call_target="tpu_custom_call" | custom-call | flops 335544320 | bytes 2621440 | tf_op jit(solution)/shard_map/spec/pallas_call | solution.py:394
  13.1 16.4 %collective-permute-done.1.refs_1_ = f32[2,640]{1,0:T(2,128)S(1)} collective-permute-done((f32[2,640]{1,0:T(2,128)S(1)}, f32[2,640]{1,0:T(2,128)S(1)}, u32[]{:S(2)}, u32[]{:S(2)}) %collective-permute-start.1) | collective-permute-done | bytes 5152 | tf_op jit(solution)/shard_map/ppermute | solution.py:279
  29.5 0.1 shard_map.64
  29.6 3.5 %collective-permute-start.2 = (f32[2,640]{1,0:T(2,128)S(1)}, f32[2,640]{1,0:T(2,128)S(1)}, u32[]{:S(2)}, u32[]{:S(2)}) collective-permute-start(f32[2,640]{1,0:T(2,128)S(1)} %get-tuple-element.29), channel_id=1, source_target_pairs={{0,8},{4,12},{8,0},{12,4},{1,9},{5,13},{9,1},{13,5},{2,10},{6,14},... | collective-permute-start | bytes 15368 | tf_op jit(solution)/shard_map/ppermute | solution.py:279
  33.1 1.6 %collective-permute-done.2.refs_1_ = f32[2,640]{1,0:T(2,128)S(1)} collective-permute-done((f32[2,640]{1,0:T(2,128)S(1)}, f32[2,640]{1,0:T(2,128)S(1)}, u32[]{:S(2)}, u32[]{:S(2)}) %collective-permute-start.2) | collective-permute-done | bytes 5152 | tf_op jit(solution)/shard_map/ppermute | solution.py:279
  34.7 0.1 shard_map.65
  34.7 1.6 %collective-permute-start.3 = (f32[1,640]{1,0:T(1,128)S(1)}, f32[1,640]{1,0:T(1,128)S(1)}, u32[]{:S(2)}, u32[]{:S(2)}) collective-permute-start(f32[1,640]{1,0:T(1,128)S(1)} %get-tuple-element.32), channel_id=1, source_target_pairs={{0,2},{2,0},{1,3},{3,1},{4,6},{6,4},{5,7},{7,5},{8,10},{10,8},{9,1... | collective-permute-start | bytes 7688 | tf_op jit(solution)/shard_map/ppermute | solution.py:308
  36.3 2.1 %collective-permute-done.3.before.after = f32[1,640]{1,0:T(1,128)S(1)} collective-permute-done((f32[1,640]{1,0:T(1,128)S(1)}, f32[1,640]{1,0:T(1,128)S(1)}, u32[]{:S(2)}, u32[]{:S(2)}) %collective-permute-start.3) | collective-permute-done | bytes 2592 | tf_op jit(solution)/shard_map/ppermute | solution.py:308
  38.4 0.0 collective-permute-done.7.refs_0_
  38.4 0.0 collective-permute-done.8.refs_1_
  38.4 0.0 copy-start
  38.5 1.0 %copy-done = bf16[256,1024]{1,0:T(8,128)(2,1)S(1)} copy-done((bf16[256,1024]{1,0:T(8,128)(2,1)S(1)}, bf16[256,1024]{1,0:T(8,128)(2,1)}, u32[]{:S(2)}) %copy-start) | copy-done | bytes 524312
  39.5 0.0 copy-start.2
  39.5 1.0 %copy-done.2 = bf16[1024,256]{1,0:T(8,128)(2,1)S(1)} copy-done((bf16[1024,256]{1,0:T(8,128)(2,1)S(1)}, bf16[1024,256]{1,0:T(8,128)(2,1)}, u32[]{:S(2)}) %copy-start.2) | copy-done | bytes 524312
  40.5 1.7 %shard_map.68 = (bf16[1024,256]{1,0:T(8,128)(2,1)S(1)}, bf16[1024,256]{1,0:T(8,128)(2,1)}) custom-call(bf16[1024,128]{1,0:T(8,128)(2,1)S(1)} %collective-permute-done.7.refs_0_, bf16[1024,128]{1,0:T(8,128)(2,1)S(1)} %collective-permute-done.8.refs_1_, bf16[1024,128]{1,0:T(8,128)(2,1)S(1)} %head.1.refs_0_.refs_2_, ...), custom_call_target="tpu_custom_call" | custom-call | flops 402653184 | bytes 2097152 | tf_op jit(solution)/shard_map/pallas_call | solution.py:436
  42.3 0.0 collective-permute-start.9
  42.3 0.0 collective-permute-done.5.refs_0_
  42.3 1.6 %shard_map.67 = (bf16[1024,256]{1,0:T(8,128)(2,1)S(1)}, bf16[1024,256]{1,0:T(8,128)(2,1)}) custom-call(bf16[1024,256]{1,0:T(8,128)(2,1)S(1)} %collective-permute-done.5.refs_0_, bf16[1024,256]{1,0:T(8,128)(2,1)S(1)} %get-tuple-element.24.refs_2_.refs_1_, f32[256,640]{1,0:T(8,128)S(1)} %get-tuple-element.25.refs_2_.refs_4_, ...), custom_call_target="tpu_custom_call" | custom-call | flops 402653184 | bytes 2097152 | tf_op jit(solution)/shard_map/pallas_call | solution.py:436
  43.8 0.5 collective-permute-start.6
  44.4 3.8 %collective-permute-start = (bf16[1024,128]{1,0:T(8,128)(2,1)S(1)}, bf16[1024,128]{1,0:T(8,128)(2,1)S(1)}, u32[]{:S(2)}, u32[]{:S(2)}) collective-permute-start(bf16[1024,128]{1,0:T(8,128)(2,1)S(1)} %get-tuple-element.22.refs_3_.refs_1_.own), channel_id=1, source_target_pairs={{0,4},{4,8},{8,12},{1,5},{5,9},{9,13},{2,6},{6,10},{10,14},{3,7},{... | collective-permute-start | bytes 786440 | tf_op jit(solution)/shard_map/ppermute | solution.py:279
  48.2 5.7 %collective-permute-done.refs_0_.piece = bf16[1024,128]{1,0:T(8,128)(2,1)S(1)} collective-permute-done((bf16[1024,128]{1,0:T(8,128)(2,1)S(1)}, bf16[1024,128]{1,0:T(8,128)(2,1)S(1)}, u32[]{:S(2)}, u32[]{:S(2)}) %collective-permute-start) | collective-permute-done | bytes 262176 | tf_op jit(solution)/shard_map/ppermute | solution.py:279
  53.9 0.0 copy-done.1
  53.9 1.4 %shard_map.66 = (bf16[256,128]{1,0:T(8,128)(2,1)S(1)}, bf16[1024,128]{1,0:T(8,128)(2,1)}) custom-call(bf16[1024,128]{1,0:T(8,128)(2,1)S(1)} %collective-permute-done.refs_0_.piece, bf16[1024,128]{1,0:T(8,128)(2,1)S(1)} %get-tuple-element.22.refs_3_.refs_1_.own, f32[256,640]{1,0:T(8,128)S(1)} %get-tuple-element.25.refs_2_.refs_4_, ...), custom_call_target="tpu_custom_call" | custom-call | flops 201326592 | bytes 1048576 | tf_op jit(solution)/shard_map/pallas_call | solution.py:436
  55.2 0.0 collective-permute-start.4
  55.9 0.5 taps.1.refs_2_.refs_1_
  56.4 0.0 copy-done.3
  56.5 0.3 hold.1.refs_0_
  56.8 0.0 collective-permute-done.9.refs_1_
  56.8 1.5 %shard_map.69.refs_2_ = f32[1024,1280]{1,0:T(8,128)S(1)} custom-call(bf16[1024,256]{1,0:T(8,128)(2,1)S(1)} %get-tuple-element.37.refs_0_, bf16[1024,256]{1,0:T(8,128)(2,1)S(1)} %collective-permute-done.9.refs_1_, bf16[256,2560]{1,0:T(8,128)(2,1)S(1)} %taps.1.refs_2_.refs_1_), custom_call_target="tpu_custom_call" | custom-call | flops 1342177280 | bytes 10485760 | tf_op jit(solution)/shard_map/pallas_call | solution.py:477
  58.3 1.0 %shard_map.70.refs_2_ = f32[1024,1280]{1,0:T(8,128)S(1)} custom-call(bf16[1024,256]{1,0:T(8,128)(2,1)S(1)} %get-tuple-element.36.refs_0_, bf16[256,2560]{1,0:T(8,128)(2,1)S(1)} %taps.1.refs_2_.refs_1_, f32[1024,1280]{1,0:T(8,128)S(1)} %shard_map.69.refs_2_), custom_call_target="tpu_custom_call", output_to_operand_aliasing={{}: (2, {})} | custom-call | flops 671088640 | bytes 10485760 | tf_op jit(solution)/shard_map/pallas_call | solution.py:477
  59.3 0.0 collective-permute-done.6.refs_0_
  59.3 1.0 %shard_map.71.refs_3_ = f32[1024,1280]{1,0:T(8,128)S(1)} custom-call(bf16[1024,256]{1,0:T(8,128)(2,1)S(1)} %collective-permute-done.6.refs_0_, bf16[256,2560]{1,0:T(8,128)(2,1)S(1)} %taps.1.refs_2_.refs_1_, f32[1024,1280]{1,0:T(8,128)S(1)} %shard_map.70.refs_2_), custom_call_target="tpu_custom_call", output_to_operand_aliasing={{}: (2, {})} | custom-call | flops 671088640 | bytes 10485760 | tf_op jit(solution)/shard_map/pallas_call | solution.py:477
  60.3 0.0 collective-permute-done.4.refs_1_
  60.3 1.9 %finish.1 = bf16[512,2,1280]{2,1,0:T(2,128)(2,1)} custom-call(bf16[1024,128]{1,0:T(8,128)(2,1)S(1)} %hold.1.refs_0_, bf16[1024,128]{1,0:T(8,128)(2,1)S(1)} %collective-permute-done.4.refs_1_, bf16[256,2560]{1,0:T(8,128)(2,1)S(1)} %taps.1.refs_2_.refs_1_, f32[1024,1280]{1,0:T(8,128)S(1)} %shard_map.71.refs_3_), custom_call_target="tpu_custom_call" | custom-call | flops 671088640 | bytes 10485760 | tf_op jit(solution)/shard_map/finish/pallas_call | solution.py:465
  (1 shorter events, 0.0 us)
Async XLA Ops:
  0.0 53.9 %copy-start.1 = (bf16[256,1024]{1,0:T(8,128)(2,1)S(1)}, bf16[256,1024]{1,0:T(8,128)(2,1)}, u32[]{:S(2)}) copy-start(bf16[256,1024]{1,0:T(8,128)(2,1)} %constant.25.clone.table.refs_4_.refs_6_) | copy-start | bytes 1572868
  2.0 40.3 %collective-permute-start.5 = (bf16[1024,256]{1,0:T(8,128)(2,1)S(1)}, bf16[1024,256]{1,0:T(8,128)(2,1)S(1)}, u32[]{:S(2)}, u32[]{:S(2)}) collective-permute-start(bf16[1024,256]{1,0:T(8,128)(2,1)S(1)} %get-tuple-element.24.refs_2_.refs_1_), channel_id=1, source_target_pairs={{0,4},{4,8},{8,12},{1,5},{5,9},{9,13},{2,6},{6,10},{10,14},{3,7},{... | collective-permute-start | bytes 1572872 | tf_op jit(solution)/shard_map/ppermute | solution.py:279
  8.0 30.4 %collective-permute-start.7 = (bf16[1024,128]{1,0:T(8,128)(2,1)S(1)}, bf16[1024,128]{1,0:T(8,128)(2,1)S(1)}, u32[]{:S(2)}, u32[]{:S(2)}) collective-permute-start(bf16[1024,128]{1,0:T(8,128)(2,1)S(1)} %head.1.refs_0_.refs_2_), channel_id=1, source_target_pairs={{0,4},{4,8},{8,12},{12,0},{1,5},{5,9},{9,13},{13,1},{2,6},{6,10},{... | collective-permute-start | bytes 786440 | tf_op jit(solution)/shard_map/ppermute | solution.py:279
  9.6 28.8 %collective-permute-start.8 = (bf16[1024,128]{1,0:T(8,128)(2,1)S(1)}, bf16[1024,128]{1,0:T(8,128)(2,1)S(1)}, u32[]{:S(2)}, u32[]{:S(2)}) collective-permute-start(bf16[1024,128]{1,0:T(8,128)(2,1)S(1)} %get-tuple-element.23.refs_1_.refs_3_), channel_id=1, source_target_pairs={{0,4},{4,8},{8,12},{12,0},{1,5},{5,9},{9,13},{13,1},{2,6},{6,10},{... | collective-permute-start | bytes 786440 | tf_op jit(solution)/shard_map/ppermute | solution.py:279
  11.2 18.3 %collective-permute-start.1 = (f32[2,640]{1,0:T(2,128)S(1)}, f32[2,640]{1,0:T(2,128)S(1)}, u32[]{:S(2)}, u32[]{:S(2)}) collective-permute-start(f32[2,640]{1,0:T(2,128)S(1)} %get-tuple-element.28.refs_2_), channel_id=1, source_target_pairs={{0,4},{4,8},{8,12},{12,0},{1,5},{5,9},{9,13},{13,1},{2,6},{6,10},{... | collective-permute-start | bytes 15368 | tf_op jit(solution)/shard_map/ppermute | solution.py:279
  11.3 45.2 %copy-start.3 = (bf16[1024,256]{1,0:T(8,128)(2,1)S(1)}, bf16[1024,256]{1,0:T(8,128)(2,1)}, u32[]{:S(2)}) copy-start(bf16[1024,256]{1,0:T(8,128)(2,1)} %constant.26.clone.refs_5_.turned.refs_7_) | copy-start | bytes 1572868
  29.6 5.1 %collective-permute-start.2 = (f32[2,640]{1,0:T(2,128)S(1)}, f32[2,640]{1,0:T(2,128)S(1)}, u32[]{:S(2)}, u32[]{:S(2)}) collective-permute-start(f32[2,640]{1,0:T(2,128)S(1)} %get-tuple-element.29), channel_id=1, source_target_pairs={{0,8},{4,12},{8,0},{12,4},{1,9},{5,13},{9,1},{13,5},{2,10},{6,14},... | collective-permute-start | bytes 15368 | tf_op jit(solution)/shard_map/ppermute | solution.py:279
  34.7 3.7 %collective-permute-start.3 = (f32[1,640]{1,0:T(1,128)S(1)}, f32[1,640]{1,0:T(1,128)S(1)}, u32[]{:S(2)}, u32[]{:S(2)}) collective-permute-start(f32[1,640]{1,0:T(1,128)S(1)} %get-tuple-element.32), channel_id=1, source_target_pairs={{0,2},{2,0},{1,3},{3,1},{4,6},{6,4},{5,7},{7,5},{8,10},{10,8},{9,1... | collective-permute-start | bytes 7688 | tf_op jit(solution)/shard_map/ppermute | solution.py:308
  38.4 1.0 %copy-start = (bf16[256,1024]{1,0:T(8,128)(2,1)S(1)}, bf16[256,1024]{1,0:T(8,128)(2,1)}, u32[]{:S(2)}) copy-start(bf16[256,1024]{1,0:T(8,128)(2,1)} %constant.25.clone.table.refs_4_.refs_6_) | copy-start | bytes 1572868
  39.5 1.0 %copy-start.2 = (bf16[1024,256]{1,0:T(8,128)(2,1)S(1)}, bf16[1024,256]{1,0:T(8,128)(2,1)}, u32[]{:S(2)}) copy-start(bf16[1024,256]{1,0:T(8,128)(2,1)} %constant.26.clone.refs_5_.turned.refs_7_) | copy-start | bytes 1572868
  42.3 14.5 %collective-permute-start.9 = (bf16[1024,256]{1,0:T(8,128)(2,1)}, bf16[1024,256]{1,0:T(8,128)(2,1)S(1)}, u32[]{:S(2)}, u32[]{:S(2)}) collective-permute-start(bf16[1024,256]{1,0:T(8,128)(2,1)} %get-tuple-element.38), channel_id=1, source_target_pairs={{0,1},{1,0},{2,3},{3,2},{4,5},{5,4},{6,7},{7,6},{8,9},{9,8},{10,11... | collective-permute-start | bytes 1572872 | tf_op jit(solution)/shard_map/ppermute | solution.py:444
  43.8 15.5 %collective-permute-start.6 = (bf16[1024,256]{1,0:T(8,128)(2,1)}, bf16[1024,256]{1,0:T(8,128)(2,1)S(1)}, u32[]{:S(2)}, u32[]{:S(2)}) collective-permute-start(bf16[1024,256]{1,0:T(8,128)(2,1)} %get-tuple-element.35), channel_id=1, source_target_pairs={{0,1},{1,0},{2,3},{3,2},{4,5},{5,4},{6,7},{7,6},{8,9},{9,8},{10,11... | collective-permute-start | bytes 1572872 | tf_op jit(solution)/shard_map/ppermute | solution.py:444
  44.4 9.5 %collective-permute-start = (bf16[1024,128]{1,0:T(8,128)(2,1)S(1)}, bf16[1024,128]{1,0:T(8,128)(2,1)S(1)}, u32[]{:S(2)}, u32[]{:S(2)}) collective-permute-start(bf16[1024,128]{1,0:T(8,128)(2,1)S(1)} %get-tuple-element.22.refs_3_.refs_1_.own), channel_id=1, source_target_pairs={{0,4},{4,8},{8,12},{1,5},{5,9},{9,13},{2,6},{6,10},{10,14},{3,7},{... | collective-permute-start | bytes 786440 | tf_op jit(solution)/shard_map/ppermute | solution.py:279
  55.2 5.1 %collective-permute-start.4 = (bf16[1024,128]{1,0:T(8,128)(2,1)}, bf16[1024,128]{1,0:T(8,128)(2,1)S(1)}, u32[]{:S(2)}, u32[]{:S(2)}) collective-permute-start(bf16[1024,128]{1,0:T(8,128)(2,1)} %get-tuple-element.34), channel_id=1, source_target_pairs={{0,1},{1,0},{2,3},{3,2},{4,5},{5,4},{6,7},{7,6},{8,9},{9,8},{10,11... | collective-permute-start | bytes 786440 | tf_op jit(solution)/shard_map/ppermute | solution.py:444

commit v6 on v5

--- a/solution.py
+++ b/solution.py
@@ -12,7 +12,7 @@
 BAND_FREQS = 64
 WAVES = 2 * BAND_FREQS
 TAP_ROWS = 256
-FINISH = 8
+FINISH = 4
 PIECES = ((0, 128), (128, 256), (256, 512), (512, 640))
 STAGES = ((0, 1), (2,), (3,))
 WRAPS = (0, 1)
@@ -163,11 +163,11 @@
 
     def damp(half, source, target):
         scaled = (total if half == 0 else total * flip).astype(BF16)
-        for r in range(0, count, 512):
-            low = jnp.dot(turned[r : r + 512, :], scaled, preferred_element_type=F32)
-            rest = source[r : r + 512, :].astype(F32) - low
-            rest = rest.reshape(64, 8, cols) - ring[None]
-            target[r : r + 512, :] = rest.reshape(512, cols).astype(BF16)
+        for r in range(0, count, 256):
+            low = jnp.dot(turned[r : r + 256, :], scaled, preferred_element_type=F32)
+            rest = source[r : r + 256, :].astype(F32) - low
+            rest = rest.reshape(32, 8, cols) - ring[None]
+            target[r : r + 256, :] = rest.reshape(256, cols).astype(BF16)
 
     def both(sent, kept, source, held):
         damp(sent, source, send)
@@ -190,16 +190,16 @@
     ring = cycle[:, lo : lo + cols]
 
     def damp(source):
-        for r in range(0, count, 512):
-            low = jnp.dot(turned[r : r + 512, :], scaled[...], preferred_element_type=F32)
-            rest = source(slice(r, r + 512)).astype(F32) - low
-            rest = rest.reshape(64, 8, cols) - ring[None]
-            keep[r : r + 512, :] = rest.reshape(512, cols).astype(BF16)
+        for r in range(0, count, 256):
+            low = jnp.dot(turned[r : r + 256, :], scaled[...], preferred_element_type=F32)
+            rest = source(slice(r, r + 256)).astype(F32) - low
+            rest = rest.reshape(32, 8, cols) - ring[None]
+            keep[r : r + 256, :] = rest.reshape(256, cols).astype(BF16)
 
     @pl.when(lax.axis_index("col") == 0)
     def _():
         here = lax.axis_index("tm") > 0
-        damp(lambda r: jnp.where(here, piece[r, :], jnp.zeros((512, cols), BF16)))
+        damp(lambda r: jnp.where(here, piece[r, :], jnp.zeros((256, cols), BF16)))
 
     @pl.when(lax.axis_index("col") != 0)
     def _():
@@ -216,7 +216,7 @@
         out = refs[-1]
     width = out.shape[-1]
     count = refs[0].shape[0]
-    step = count // FINISH if last else 256
+    step = count // FINISH if last else 512
 
     depth = refs[0].shape[1]
     offs = [(-start) % width for start in starts]

time: 62.7 us -> 62.6 us (level)
  no operation moved by 1% of the time
where the time goes in v6:
time: 62.6 us; the launch traced here: 62.1 us
  waiting for transfers between devices  25.8 us (41%)
  starting transfers between devices  17.6 us (28%)
  Pallas kernels  15.8 us (25%)
  local copies, waits for them, and re-layouts  2.09 us (3%)
  between operations  0.81 us (1%)
    ppermute x6, waiting for transfers between devices, along_tm(): return lax.ppermute(x, 'tm', route)  23.7 us
    ppermute x6, starting transfers between devices, along_tm(): return lax.ppermute(x, 'tm', route)  15.6 us
    pallas_call x3, Pallas kernels, damp(): pl.pallas_call(functools.partial(damp_kernel, lo, rows, len(stage), late)...  4.67 us
    pallas_call x3, Pallas kernels, accumulate(): pl.pallas_call(kernel, out_shape=jax.ShapeDtypeStruct((count, width), F32...  3.4 us
    ppermute x1, waiting for transfers between devices, row_neighbours(): before = lax.ppermute(last, 'cuts', up)  2.1 us
    unnamed x8, local copies, waits for them, and re-layouts  2.09 us
    pallas_call x1, Pallas kernels, local(): pl.pallas_call(split_kernel, out_shape=(*shapes[1:], jax.ShapeDtypeStruct...  1.99 us
    pallas_call x1, Pallas kernels, accumulate(): pl.pallas_call(kernel, out_shape=jax.ShapeDtypeStruct((half, rows, width)...  1.93 us
  transfers between devices with their start and end apart: 10, of which 4 were waited for; matrix products, arithmetic and copies ran while one was open for 0% of the time, Pallas kernels for 19%

profile of v6, /device:TPU:0, one launch (start us, length us, event | category | flops | bytes accessed | tf_op | source)
XLA Modules:
  0.0 62.1 jit_solution(13348289770831659309)
XLA Ops:
  0.0 0.0 copy-start.1
  0.0 2.0 %split.1 = (bf16[1024,128]{1,0:T(8,128)(2,1)S(1)}, bf16[1024,256]{1,0:T(8,128)(2,1)S(1)}, bf16[1024,128]{1,0:T(8,128)(2,1)S(1)}, f32[2,640]{1,0:T(2,128)S(1)}) custom-call(bf16[512,2,640]{2,1,0:T(2,128)(2,1)} %raw.3), custom_call_target="tpu_custom_call" | custom-call | flops 10485760 | bytes 2621440 | tf_op jit(solution)/shard_map/split/pallas_call | solution.py:384
  2.0 5.0 %collective-permute-start.5 = (bf16[1024,256]{1,0:T(8,128)(2,1)S(1)}, bf16[1024,256]{1,0:T(8,128)(2,1)S(1)}, u32[]{:S(2)}, u32[]{:S(2)}) collective-permute-start(bf16[1024,256]{1,0:T(8,128)(2,1)S(1)} %get-tuple-element.24.refs_2_.refs_1_), channel_id=1, source_target_pairs={{0,4},{4,8},{8,12},{1,5},{5,9},{9,13},{2,6},{6,10},{10,14},{3,7},{... | collective-permute-start | bytes 1572872 | tf_op jit(solution)/shard_map/ppermute | solution.py:279
  7.0 1.0 %head.1.refs_0_.refs_2_ = bf16[1024,128]{1,0:T(8,128)(2,1)S(1)} custom-call(bf16[512,2,640]{2,1,0:T(2,128)(2,1)} %raw.3), custom_call_target="tpu_custom_call" | custom-call | flops 655360 | bytes 655360 | tf_op jit(solution)/shard_map/head/pallas_call | solution.py:372
  8.0 1.6 %collective-permute-start.7 = (bf16[1024,128]{1,0:T(8,128)(2,1)S(1)}, bf16[1024,128]{1,0:T(8,128)(2,1)S(1)}, u32[]{:S(2)}, u32[]{:S(2)}) collective-permute-start(bf16[1024,128]{1,0:T(8,128)(2,1)S(1)} %head.1.refs_0_.refs_2_), channel_id=1, source_target_pairs={{0,4},{4,8},{8,12},{12,0},{1,5},{5,9},{9,13},{13,1},{2,6},{6,10},{... | collective-permute-start | bytes 786440 | tf_op jit(solution)/shard_map/ppermute | solution.py:279
  9.6 1.6 %collective-permute-start.8 = (bf16[1024,128]{1,0:T(8,128)(2,1)S(1)}, bf16[1024,128]{1,0:T(8,128)(2,1)S(1)}, u32[]{:S(2)}, u32[]{:S(2)}) collective-permute-start(bf16[1024,128]{1,0:T(8,128)(2,1)S(1)} %get-tuple-element.23.refs_1_.refs_3_), channel_id=1, source_target_pairs={{0,4},{4,8},{8,12},{12,0},{1,5},{5,9},{9,13},{13,1},{2,6},{6,10},{... | collective-permute-start | bytes 786440 | tf_op jit(solution)/shard_map/ppermute | solution.py:279
  11.2 0.1 collective-permute-start.1
  11.3 0.0 copy-start.3
  11.3 1.8 %spec.1 = (f32[256,640]{1,0:T(8,128)S(1)}, f32[256,1]{1,0:T(8,128)S(1)}, f32[2,128]{1,0:T(2,128)S(1)}) custom-call(s32[2]{0:T(128)} %bands.1, f32[2]{0:T(128)} %memory.1, bf16[256,1024]{1,0:T(8,128)(2,1)} %constant.25.clone.table.refs_4_.refs_6_, bf16[1024,128]{1,0:T(8,128)(2,1)S(1)} %head.1.refs_0_.refs_2_, ...), custom_call_target="tpu_custom_call" | custom-call | flops 335544320 | bytes 2621440 | tf_op jit(solution)/shard_map/spec/pallas_call | solution.py:394
  13.1 16.4 %collective-permute-done.1.refs_1_ = f32[2,640]{1,0:T(2,128)S(1)} collective-permute-done((f32[2,640]{1,0:T(2,128)S(1)}, f32[2,640]{1,0:T(2,128)S(1)}, u32[]{:S(2)}, u32[]{:S(2)}) %collective-permute-start.1) | collective-permute-done | bytes 5152 | tf_op jit(solution)/shard_map/ppermute | solution.py:279
  29.5 0.1 shard_map.64
  29.6 3.5 %collective-permute-start.2 = (f32[2,640]{1,0:T(2,128)S(1)}, f32[2,640]{1,0:T(2,128)S(1)}, u32[]{:S(2)}, u32[]{:S(2)}) collective-permute-start(f32[2,640]{1,0:T(2,128)S(1)} %get-tuple-element.29), channel_id=1, source_target_pairs={{0,8},{4,12},{8,0},{12,4},{1,9},{5,13},{9,1},{13,5},{2,10},{6,14},... | collective-permute-start | bytes 15368 | tf_op jit(solution)/shard_map/ppermute | solution.py:279
  33.1 1.6 %collective-permute-done.2.refs_1_ = f32[2,640]{1,0:T(2,128)S(1)} collective-permute-done((f32[2,640]{1,0:T(2,128)S(1)}, f32[2,640]{1,0:T(2,128)S(1)}, u32[]{:S(2)}, u32[]{:S(2)}) %collective-permute-start.2) | collective-permute-done | bytes 5152 | tf_op jit(solution)/shard_map/ppermute | solution.py:279
  34.7 0.1 shard_map.65
  34.7 1.6 %collective-permute-start.3 = (f32[1,640]{1,0:T(1,128)S(1)}, f32[1,640]{1,0:T(1,128)S(1)}, u32[]{:S(2)}, u32[]{:S(2)}) collective-permute-start(f32[1,640]{1,0:T(1,128)S(1)} %get-tuple-element.32), channel_id=1, source_target_pairs={{0,2},{2,0},{1,3},{3,1},{4,6},{6,4},{5,7},{7,5},{8,10},{10,8},{9,1... | collective-permute-start | bytes 7688 | tf_op jit(solution)/shard_map/ppermute | solution.py:308
  36.3 2.1 %collective-permute-done.3.before.after = f32[1,640]{1,0:T(1,128)S(1)} collective-permute-done((f32[1,640]{1,0:T(1,128)S(1)}, f32[1,640]{1,0:T(1,128)S(1)}, u32[]{:S(2)}, u32[]{:S(2)}) %collective-permute-start.3) | collective-permute-done | bytes 2592 | tf_op jit(solution)/shard_map/ppermute | solution.py:308
  38.4 0.0 collective-permute-done.7.refs_0_
  38.4 0.0 collective-permute-done.8.refs_1_
  38.4 0.0 copy-start
  38.5 1.0 %copy-done = bf16[256,1024]{1,0:T(8,128)(2,1)S(1)} copy-done((bf16[256,1024]{1,0:T(8,128)(2,1)S(1)}, bf16[256,1024]{1,0:T(8,128)(2,1)}, u32[]{:S(2)}) %copy-start) | copy-done | bytes 524312
  39.5 0.0 copy-start.2
  39.5 1.0 %copy-done.2 = bf16[1024,256]{1,0:T(8,128)(2,1)S(1)} copy-done((bf16[1024,256]{1,0:T(8,128)(2,1)S(1)}, bf16[1024,256]{1,0:T(8,128)(2,1)}, u32[]{:S(2)}) %copy-start.2) | copy-done | bytes 524312
  40.5 1.7 %shard_map.68 = (bf16[1024,256]{1,0:T(8,128)(2,1)S(1)}, bf16[1024,256]{1,0:T(8,128)(2,1)}) custom-call(bf16[1024,128]{1,0:T(8,128)(2,1)S(1)} %collective-permute-done.7.refs_0_, bf16[1024,128]{1,0:T(8,128)(2,1)S(1)} %collective-permute-done.8.refs_1_, bf16[1024,128]{1,0:T(8,128)(2,1)S(1)} %head.1.refs_0_.refs_2_, ...), custom_call_target="tpu_custom_call" | custom-call | flops 402653184 | bytes 2097152 | tf_op jit(solution)/shard_map/pallas_call | solution.py:436
  42.3 0.0 collective-permute-start.9
  42.3 0.0 collective-permute-done.5.refs_0_
  42.3 1.6 %shard_map.67 = (bf16[1024,256]{1,0:T(8,128)(2,1)S(1)}, bf16[1024,256]{1,0:T(8,128)(2,1)}) custom-call(bf16[1024,256]{1,0:T(8,128)(2,1)S(1)} %collective-permute-done.5.refs_0_, bf16[1024,256]{1,0:T(8,128)(2,1)S(1)} %get-tuple-element.24.refs_2_.refs_1_, f32[256,640]{1,0:T(8,128)S(1)} %get-tuple-element.25.refs_2_.refs_4_, ...), custom_call_target="tpu_custom_call" | custom-call | flops 402653184 | bytes 2097152 | tf_op jit(solution)/shard_map/pallas_call | solution.py:436
  43.8 0.5 collective-permute-start.6
  44.4 3.8 %collective-permute-start = (bf16[1024,128]{1,0:T(8,128)(2,1)S(1)}, bf16[1024,128]{1,0:T(8,128)(2,1)S(1)}, u32[]{:S(2)}, u32[]{:S(2)}) collective-permute-start(bf16[1024,128]{1,0:T(8,128)(2,1)S(1)} %get-tuple-element.22.refs_3_.refs_1_.own), channel_id=1, source_target_pairs={{0,4},{4,8},{8,12},{1,5},{5,9},{9,13},{2,6},{6,10},{10,14},{3,7},{... | collective-permute-start | bytes 786440 | tf_op jit(solution)/shard_map/ppermute | solution.py:279
  48.2 5.7 %collective-permute-done.refs_0_.piece = bf16[1024,128]{1,0:T(8,128)(2,1)S(1)} collective-permute-done((bf16[1024,128]{1,0:T(8,128)(2,1)S(1)}, bf16[1024,128]{1,0:T(8,128)(2,1)S(1)}, u32[]{:S(2)}, u32[]{:S(2)}) %collective-permute-start) | collective-permute-done | bytes 262176 | tf_op jit(solution)/shard_map/ppermute | solution.py:279
  53.9 0.0 copy-done.1
  53.9 1.4 %shard_map.66 = (bf16[256,128]{1,0:T(8,128)(2,1)S(1)}, bf16[1024,128]{1,0:T(8,128)(2,1)}) custom-call(bf16[1024,128]{1,0:T(8,128)(2,1)S(1)} %collective-permute-done.refs_0_.piece, bf16[1024,128]{1,0:T(8,128)(2,1)S(1)} %get-tuple-element.22.refs_3_.refs_1_.own, f32[256,640]{1,0:T(8,128)S(1)} %get-tuple-element.25.refs_2_.refs_4_, ...), custom_call_target="tpu_custom_call" | custom-call | flops 201326592 | bytes 1048576 | tf_op jit(solution)/shard_map/pallas_call | solution.py:436
  55.3 0.0 collective-permute-start.4
  55.9 0.5 taps.1.refs_2_.refs_1_
  56.5 0.0 copy-done.3
  56.5 0.3 hold.1.refs_0_
  56.8 0.0 collective-permute-done.9.refs_1_
  56.8 1.5 %shard_map.69.refs_2_ = f32[1024,1280]{1,0:T(8,128)S(1)} custom-call(bf16[1024,256]{1,0:T(8,128)(2,1)S(1)} %get-tuple-element.37.refs_0_, bf16[1024,256]{1,0:T(8,128)(2,1)S(1)} %collective-permute-done.9.refs_1_, bf16[256,2560]{1,0:T(8,128)(2,1)S(1)} %taps.1.refs_2_.refs_1_), custom_call_target="tpu_custom_call" | custom-call | flops 1342177280 | bytes 10485760 | tf_op jit(solution)/shard_map/pallas_call | solution.py:477
  58.3 0.9 %shard_map.70.refs_2_ = f32[1024,1280]{1,0:T(8,128)S(1)} custom-call(bf16[1024,256]{1,0:T(8,128)(2,1)S(1)} %get-tuple-element.36.refs_0_, bf16[256,2560]{1,0:T(8,128)(2,1)S(1)} %taps.1.refs_2_.refs_1_, f32[1024,1280]{1,0:T(8,128)S(1)} %shard_map.69.refs_2_), custom_call_target="tpu_custom_call", output_to_operand_aliasing={{}: (2, {})} | custom-call | flops 671088640 | bytes 10485760 | tf_op jit(solution)/shard_map/pallas_call | solution.py:477
  59.2 0.0 collective-permute-done.6.refs_0_
  59.3 0.9 %shard_map.71.refs_3_ = f32[1024,1280]{1,0:T(8,128)S(1)} custom-call(bf16[1024,256]{1,0:T(8,128)(2,1)S(1)} %collective-permute-done.6.refs_0_, bf16[256,2560]{1,0:T(8,128)(2,1)S(1)} %taps.1.refs_2_.refs_1_, f32[1024,1280]{1,0:T(8,128)S(1)} %shard_map.70.refs_2_), custom_call_target="tpu_custom_call", output_to_operand_aliasing={{}: (2, {})} | custom-call | flops 671088640 | bytes 10485760 | tf_op jit(solution)/shard_map/pallas_call | solution.py:477
  60.2 0.0 collective-permute-done.4.refs_1_
  60.2 1.9 %finish.1 = bf16[512,2,1280]{2,1,0:T(2,128)(2,1)} custom-call(bf16[1024,128]{1,0:T(8,128)(2,1)S(1)} %hold.1.refs_0_, bf16[1024,128]{1,0:T(8,128)(2,1)S(1)} %collective-permute-done.4.refs_1_, bf16[256,2560]{1,0:T(8,128)(2,1)S(1)} %taps.1.refs_2_.refs_1_, f32[1024,1280]{1,0:T(8,128)S(1)} %shard_map.71.refs_3_), custom_call_target="tpu_custom_call" | custom-call | flops 671088640 | bytes 10485760 | tf_op jit(solution)/shard_map/finish/pallas_call | solution.py:465
  (1 shorter events, 0.0 us)
Async XLA Ops:
  0.0 53.9 %copy-start.1 = (bf16[256,1024]{1,0:T(8,128)(2,1)S(1)}, bf16[256,1024]{1,0:T(8,128)(2,1)}, u32[]{:S(2)}) copy-start(bf16[256,1024]{1,0:T(8,128)(2,1)} %constant.25.clone.table.refs_4_.refs_6_) | copy-start | bytes 1572868
  2.0 40.3 %collective-permute-start.5 = (bf16[1024,256]{1,0:T(8,128)(2,1)S(1)}, bf16[1024,256]{1,0:T(8,128)(2,1)S(1)}, u32[]{:S(2)}, u32[]{:S(2)}) collective-permute-start(bf16[1024,256]{1,0:T(8,128)(2,1)S(1)} %get-tuple-element.24.refs_2_.refs_1_), channel_id=1, source_target_pairs={{0,4},{4,8},{8,12},{1,5},{5,9},{9,13},{2,6},{6,10},{10,14},{3,7},{... | collective-permute-start | bytes 1572872 | tf_op jit(solution)/shard_map/ppermute | solution.py:279
  8.0 30.4 %collective-permute-start.7 = (bf16[1024,128]{1,0:T(8,128)(2,1)S(1)}, bf16[1024,128]{1,0:T(8,128)(2,1)S(1)}, u32[]{:S(2)}, u32[]{:S(2)}) collective-permute-start(bf16[1024,128]{1,0:T(8,128)(2,1)S(1)} %head.1.refs_0_.refs_2_), channel_id=1, source_target_pairs={{0,4},{4,8},{8,12},{12,0},{1,5},{5,9},{9,13},{13,1},{2,6},{6,10},{... | collective-permute-start | bytes 786440 | tf_op jit(solution)/shard_map/ppermute | solution.py:279
  9.6 28.8 %collective-permute-start.8 = (bf16[1024,128]{1,0:T(8,128)(2,1)S(1)}, bf16[1024,128]{1,0:T(8,128)(2,1)S(1)}, u32[]{:S(2)}, u32[]{:S(2)}) collective-permute-start(bf16[1024,128]{1,0:T(8,128)(2,1)S(1)} %get-tuple-element.23.refs_1_.refs_3_), channel_id=1, source_target_pairs={{0,4},{4,8},{8,12},{12,0},{1,5},{5,9},{9,13},{13,1},{2,6},{6,10},{... | collective-permute-start | bytes 786440 | tf_op jit(solution)/shard_map/ppermute | solution.py:279
  11.2 18.3 %collective-permute-start.1 = (f32[2,640]{1,0:T(2,128)S(1)}, f32[2,640]{1,0:T(2,128)S(1)}, u32[]{:S(2)}, u32[]{:S(2)}) collective-permute-start(f32[2,640]{1,0:T(2,128)S(1)} %get-tuple-element.28.refs_2_), channel_id=1, source_target_pairs={{0,4},{4,8},{8,12},{12,0},{1,5},{5,9},{9,13},{13,1},{2,6},{6,10},{... | collective-permute-start | bytes 15368 | tf_op jit(solution)/shard_map/ppermute | solution.py:279
  11.3 45.2 %copy-start.3 = (bf16[1024,256]{1,0:T(8,128)(2,1)S(1)}, bf16[1024,256]{1,0:T(8,128)(2,1)}, u32[]{:S(2)}) copy-start(bf16[1024,256]{1,0:T(8,128)(2,1)} %constant.26.clone.refs_5_.turned.refs_7_) | copy-start | bytes 1572868
  29.6 5.1 %collective-permute-start.2 = (f32[2,640]{1,0:T(2,128)S(1)}, f32[2,640]{1,0:T(2,128)S(1)}, u32[]{:S(2)}, u32[]{:S(2)}) collective-permute-start(f32[2,640]{1,0:T(2,128)S(1)} %get-tuple-element.29), channel_id=1, source_target_pairs={{0,8},{4,12},{8,0},{12,4},{1,9},{5,13},{9,1},{13,5},{2,10},{6,14},... | collective-permute-start | bytes 15368 | tf_op jit(solution)/shard_map/ppermute | solution.py:279
  34.7 3.7 %collective-permute-start.3 = (f32[1,640]{1,0:T(1,128)S(1)}, f32[1,640]{1,0:T(1,128)S(1)}, u32[]{:S(2)}, u32[]{:S(2)}) collective-permute-start(f32[1,640]{1,0:T(1,128)S(1)} %get-tuple-element.32), channel_id=1, source_target_pairs={{0,2},{2,0},{1,3},{3,1},{4,6},{6,4},{5,7},{7,5},{8,10},{10,8},{9,1... | collective-permute-start | bytes 7688 | tf_op jit(solution)/shard_map/ppermute | solution.py:308
  38.4 1.0 %copy-start = (bf16[256,1024]{1,0:T(8,128)(2,1)S(1)}, bf16[256,1024]{1,0:T(8,128)(2,1)}, u32[]{:S(2)}) copy-start(bf16[256,1024]{1,0:T(8,128)(2,1)} %constant.25.clone.table.refs_4_.refs_6_) | copy-start | bytes 1572868
  39.5 1.0 %copy-start.2 = (bf16[1024,256]{1,0:T(8,128)(2,1)S(1)}, bf16[1024,256]{1,0:T(8,128)(2,1)}, u32[]{:S(2)}) copy-start(bf16[1024,256]{1,0:T(8,128)(2,1)} %constant.26.clone.refs_5_.turned.refs_7_) | copy-start | bytes 1572868
  42.3 14.5 %collective-permute-start.9 = (bf16[1024,256]{1,0:T(8,128)(2,1)}, bf16[1024,256]{1,0:T(8,128)(2,1)S(1)}, u32[]{:S(2)}, u32[]{:S(2)}) collective-permute-start(bf16[1024,256]{1,0:T(8,128)(2,1)} %get-tuple-element.38), channel_id=1, source_target_pairs={{0,1},{1,0},{2,3},{3,2},{4,5},{5,4},{6,7},{7,6},{8,9},{9,8},{10,11... | collective-permute-start | bytes 1572872 | tf_op jit(solution)/shard_map/ppermute | solution.py:444
  43.8 15.4 %collective-permute-start.6 = (bf16[1024,256]{1,0:T(8,128)(2,1)}, bf16[1024,256]{1,0:T(8,128)(2,1)S(1)}, u32[]{:S(2)}, u32[]{:S(2)}) collective-permute-start(bf16[1024,256]{1,0:T(8,128)(2,1)} %get-tuple-element.35), channel_id=1, source_target_pairs={{0,1},{1,0},{2,3},{3,2},{4,5},{5,4},{6,7},{7,6},{8,9},{9,8},{10,11... | collective-permute-start | bytes 1572872 | tf_op jit(solution)/shard_map/ppermute | solution.py:444
  44.4 9.5 %collective-permute-start = (bf16[1024,128]{1,0:T(8,128)(2,1)S(1)}, bf16[1024,128]{1,0:T(8,128)(2,1)S(1)}, u32[]{:S(2)}, u32[]{:S(2)}) collective-permute-start(bf16[1024,128]{1,0:T(8,128)(2,1)S(1)} %get-tuple-element.22.refs_3_.refs_1_.own), channel_id=1, source_target_pairs={{0,4},{4,8},{8,12},{1,5},{5,9},{9,13},{2,6},{6,10},{10,14},{3,7},{... | collective-permute-start | bytes 786440 | tf_op jit(solution)/shard_map/ppermute | solution.py:279
  55.3 4.9 %collective-permute-start.4 = (bf16[1024,128]{1,0:T(8,128)(2,1)}, bf16[1024,128]{1,0:T(8,128)(2,1)S(1)}, u32[]{:S(2)}, u32[]{:S(2)}) collective-permute-start(bf16[1024,128]{1,0:T(8,128)(2,1)} %get-tuple-element.34), channel_id=1, source_target_pairs={{0,1},{1,0},{2,3},{3,2},{4,5},{5,4},{6,7},{7,6},{8,9},{9,8},{10,11... | collective-permute-start | bytes 786440 | tf_op jit(solution)/shard_map/ppermute | solution.py:444
